TPU v7x, 32 devices: a whole 2x2x4 slice. The times are simulated.
32 devices in a mesh: lev: 8 (over z, x), tile: 4 (over y, core).
Axes of the slice: x: 2, y: 2, z: 4, core: 2. Of those that a mesh axis runs over, the one named last changes fastest.
Arguments:
- increment: float32 [144, 96, 1440], P('lev', 'tile'), may hold values from -6 to 6
- kappa: float32 [144], P('lev'), may hold values from 0.02 to 0.24
- balance: float32 [144, 144], replicated, may hold values from -0.5 to 0.5
- correlation: float32 [144, 144], replicated, may hold values from -0.5 to 0.5
- ground_level: int32 [96, 1440], P('tile'), may hold values from 72 to 144
Outputs:
- covaried: float32 [144, 96, 1440], P('lev', 'tile')
Inputs may be any that keep to these rules, and one draw needn't show every extreme that they name: Levels from ground_level of a column down to the last one lie below ground.
All inputs are finite; a program needn't handle non-finite values.
Results may differ from a plain program's by a relative error of at most 0.00019.
Values sent between devices are 32-bit elements; how exact they have to be, the bound alone decides.
No kernel may reach another device: no remote copies, remote signals or barrier semaphores. Data moves between devices by JAX's collectives and lax.ppermute only.
A program may use at most 64 MiB of HBM per device.

v0:
```python
import functools

import jax
import jax.numpy as jnp
from jax import lax
from jax.experimental import pallas as pl
from jax.experimental.pallas import tpu as pltpu
from jax.sharding import PartitionSpec as P


PASSES = 10
LANES = 128
SUBS = 8
TOGETHER = 8
TOGETHER_CHUNKS = ()

VMEM = pl.BlockSpec(memory_space=pltpu.VMEM)
ANY = pl.BlockSpec(memory_space=pl.ANY)


def level_chunks(levels):
    chunks = [(first, SUBS) for first in range(0, levels - levels % SUBS, SUBS)]
    if levels % SUBS:
        chunks.append((levels - levels % SUBS, levels % SUBS))
    return chunks


def up_to(value, multiple):
    return -(-value // multiple) * multiple


class Plan:
    def __init__(self, shape, group):
        self.levels, self.rows, self.lons = shape
        self.group = group
        self.halo = PASSES
        self.full = self.lons // LANES
        self.rest = self.lons % LANES
        self.tiles = self.full + 1
        assert self.halo <= self.rest and self.rest + 2 * self.halo <= LANES
        assert self.halo <= self.rows and group & (group - 1) == 0
        self.rows_each = -(-self.rows // group)
        self.rows_held = self.rows_each * group
        self.per_merged = LANES // self.rest
        self.merged = -(-self.rows_each // self.per_merged)
        self.units = self.rows_each * self.full + self.merged
        self.chunks = level_chunks(self.levels)


def lane_ids():
    return lax.broadcasted_iota(jnp.int32, (SUBS, LANES), 1)


def arrange_kernel(plan, chunks, x_ref, all_ref, inner_ref, outer_ref, x_vmem, sem):
    begin = chunks[0][0]
    levels = chunks[-1][0] + chunks[-1][1] - begin
    copy = pltpu.make_async_copy(x_ref.at[begin : begin + levels], x_vmem, sem)
    copy.start()
    copy.wait()
    lane = lane_ids()
    even = lax.axis_index("tile") % 2 == 0
    inner_row = jnp.where(even, plan.rows - plan.halo, 0)
    outer_row = jnp.where(even, 0, plan.rows - plan.halo)
    for c, (first, count) in enumerate(chunks):
        for row in range(plan.rows):

            def take(tile):
                width = LANES if tile < plan.full else plan.rest
                lanes = slice(tile * LANES, tile * LANES + width)
                value = x_vmem[first - begin : first - begin + count, row, lanes]
                if count < SUBS or width < LANES:
                    value = jnp.pad(value, ((0, SUBS - count), (0, LANES - width)))
                return value

            values = [take(tile) for tile in range(plan.tiles)]
            last = values[-1]
            values[-1] = jnp.where(
                lane < plan.rest,
                last,
                jnp.where(
                    lane < plan.rest + plan.halo,
                    pltpu.roll(values[0], plan.rest, 1),
                    pltpu.roll(last, LANES - plan.rest, 1),
                ),
            )
            for tile, value in enumerate(values):
                all_ref[c, row, tile] = value
        for row in range(plan.halo):
            for tile in range(plan.tiles):
                inner_ref[c, row, tile] = all_ref[c, inner_row + row, tile]
                outer_ref[c, row, tile] = all_ref[c, outer_row + row, tile]


def diffuse_kernel(plan, count, at, together, x_ref, inner_ref, outer_ref, kappa_ref, *refs):
    out_refs, (a_ref, b_ref) = refs[:-2], refs[-2:]
    me = lax.axis_index("lev")
    tile_index = lax.axis_index("tile")
    rows_total = plan.rows * lax.axis_size("tile")
    first_row = tile_index * plan.rows - plan.halo
    height = plan.rows + 2 * plan.halo
    lane = lane_ids()
    at_start, at_end = lane == 0, lane == LANES - 1
    kappa = kappa_ref[...]
    below = plan.halo + plan.rows
    inner_row = jnp.where(tile_index % 2 == 0, below, 0)
    for row in range(plan.halo):
        a_ref[inner_row + row] = inner_ref[at, row]
        a_ref[below - inner_row + row] = outer_ref[at, row]
    a_ref[plan.halo : below] = x_ref[at]

    def sweep(source, target, done):
        def one_row(row):
            here = [source[row, tile] for tile in range(plan.tiles)]
            right = [pltpu.roll(value, 1, 1) for value in here]
            left = [pltpu.roll(value, LANES - 1, 1) for value in here]
            inside = (first_row + row >= 0) & (first_row + row < rows_total)
            weight = jnp.where(inside, kappa, 0.0)
            centre = 1.0 - 4.0 * weight
            for tile in range(plan.tiles):
                west = jnp.where(at_start, right[tile - 1], right[tile])
                east = jnp.where(at_end, left[(tile + 1) % plan.tiles], left[tile])
                beside = (source[row - 1, tile] + source[row + 1, tile]) + (west + east)
                target[row, tile] = centre * here[tile] + weight * beside

        def some_rows(step, _):
            for i in range(TOGETHER):
                one_row(done + 1 + step * TOGETHER + i)
            return 0

        count = height - 2 - 2 * done
        lax.fori_loop(0, (count + TOGETHER - 1) // TOGETHER, some_rows, 0)

    def two_passes(step, _):
        sweep(a_ref, b_ref, 2 * step)
        sweep(b_ref, a_ref, 2 * step + 1)
        return 0

    lax.fori_loop(0, PASSES // 2, two_passes, 0)

    for d in range(plan.group):
        out_ref = out_refs[0].at[d] if together else out_refs[d]
        base = plan.halo + (d if together else me ^ d) * plan.rows_each

        def put(unit, value):
            if count == SUBS:
                out_ref[unit] = value
            else:
                out_ref[unit * count : (unit + 1) * count] = value[:count]

        for i in range(plan.rows_each):
            for tile in range(plan.full):
                put(i * plan.full + tile, a_ref[base + i, tile])
        for m in range(plan.merged):
            value = None
            for k in range(plan.per_merged):
                i = m * plan.per_merged + k
                if i < plan.rows_each:
                    piece = a_ref[base + i, plan.full]
                    if k == 0:
                        value = piece
                    else:
                        value = jnp.where(
                            lane < k * plan.rest, value, pltpu.roll(piece, k * plan.rest, 1)
                        )
            put(plan.rows_each * plan.full + m, value)


def operator_kernel(plan, together, correlation_ref, balance_ref, high_ref, low_ref):
    group, levels = plan.group, plan.levels
    stride = up_to(levels, SUBS)
    me = lax.axis_index("lev")

    def exact(left, right, dims=((1,), (0,))):
        return lax.dot_general(
            left,
            right,
            (dims, ((), ())),
            precision=lax.Precision.HIGHEST,
            preferred_element_type=jnp.float32,
        )

    def picked(shape, pieces):
        place = lax.broadcasted_iota(jnp.int32, shape, 0)
        level = jnp.full(shape, -1, jnp.int32)
        for first, count, start in pieces:
            here = (place >= first) & (place < first + count)
            level = jnp.where(here, start + place - first, level)
        return (level == lax.broadcasted_iota(jnp.int32, shape, 1)).astype(jnp.float32)

    rows = [(d * stride, levels, (me ^ d) * levels) for d in range(group)]
    columns, place = [], 0
    for (first, count), alike in zip(plan.chunks, together):
        for d in range(group):
            columns.append((place, count, (d if alike else me ^ d) * levels + first))
            place += count
    left = exact(picked((group * stride, group * levels), rows), correlation_ref[...])
    right = exact(
        balance_ref[...], picked((group * levels, group * levels), columns), ((1,), (1,))
    )
    operator = exact(left, right)
    high = operator.astype(jnp.bfloat16)
    high_ref[...] = high
    low_ref[...] = (operator - high.astype(jnp.float32)).astype(jnp.bfloat16)


def mix_kernel(plan, counts, first, stop, high_ref, low_ref, *refs):
    chunks, group, levels = plan.chunks, plan.group, plan.levels
    held, place = [], 0
    for given in counts:
        refs_here = refs[place : place + given]
        held.append([refs_here[0].at[d] for d in range(group)] if given == 1 else refs_here)
        place += given
    out_refs = refs[place : place + group]
    high, low = high_ref[...], low_ref[...]
    stride = up_to(levels, SUBS)
    for unit in range(first, stop):
        pieces = []
        for (_, count), blocks in zip(chunks, held):
            for block in blocks:
                if count == SUBS:
                    pieces.append(block[unit])
                else:
                    pieces.append(block[unit * count : (unit + 1) * count])
        column = jnp.concatenate(pieces, axis=0)
        column_high = column.astype(jnp.bfloat16)
        column_low = (column - column_high.astype(jnp.float32)).astype(jnp.bfloat16)

        def dot(matrix, values):
            return jnp.dot(matrix, values, preferred_element_type=jnp.float32)

        result = dot(high, column_high) + (dot(high, column_low) + dot(low, column_high))
        for d in range(group):
            out_refs[d][(unit - first) * levels : (unit - first + 1) * levels] = result[
                d * stride : d * stride + levels
            ]


def unpack(plan, begin, stop, received, held_ref):
    levels, rows_held = plan.levels, plan.rows_held
    me = lax.axis_index("lev")

    def store(tile, row, value):
        for first in range(0, levels, SUBS):
            count = min(SUBS, levels - first)
            held_ref[tile, pl.ds(row + first * rows_held, count, stride=rows_held), :] = value[
                first : first + count
            ]

    for d in range(plan.group):
        base = (me ^ d) * plan.rows_each
        for unit in range(begin, stop):
            value = received[d][(unit - begin) * levels : (unit - begin + 1) * levels]
            if unit < plan.rows_each * plan.full:
                store(unit % plan.full, base + unit // plan.full, value)
            else:
                m = unit - plan.rows_each * plan.full
                for k in range(plan.per_merged):
                    i = m * plan.per_merged + k
                    if i < plan.rows_each:
                        piece = pltpu.roll(value, LANES - k * plan.rest, 1) if k else value
                        store(plan.full, base + i, piece)


def unpack_kernel(plan, begin, stop, *refs):
    unpack(plan, begin, stop, refs[:-1], refs[-1])


def finish_kernel(plan, begin, stop, ground_ref, held_ref, *refs):
    out_ref = refs[plan.group]
    levels, rows_held = plan.levels, plan.rows_held
    unpack(plan, begin, stop, refs[: plan.group], held_ref)
    me = lax.axis_index("lev")
    for tile in range(plan.tiles):
        width = LANES if tile < plan.full else plan.rest
        lanes = slice(tile * LANES, tile * LANES + width)
        ground = ground_ref[:, lanes]
        for level in range(levels):
            value = held_ref[tile, level * rows_held : level * rows_held + plan.rows, :width]
            out_ref[level, :, lanes] = jnp.where(me * levels + level < ground, value, 0.0)


def program(increment, kappa, balance, correlation, ground_level):
    group = lax.axis_size("lev")
    tiles_around = lax.axis_size("tile")
    plan = Plan(increment.shape, group)
    levels, halo = plan.levels, plan.halo
    f32 = jnp.float32

    def shape(*dims):
        return jax.ShapeDtypeStruct(dims, f32)

    def call(kernel, outs, *args, scratch=(), flops, first_spec=VMEM, aliases=None):
        return pl.pallas_call(
            kernel,
            out_shape=outs,
            in_specs=[first_spec] + [VMEM] * (len(args) - 1),
            out_specs=jax.tree.map(lambda _: VMEM, outs),
            scratch_shapes=list(scratch),
            input_output_aliases=aliases or {},
            compiler_params=pltpu.CompilerParams(vmem_limit_bytes=14 << 20),
            cost_estimate=pl.CostEstimate(flops=flops, bytes_accessed=1 << 20, transcendentals=0),
        )(*args)

    def swap(start):
        return [(i + k, i + 1 - k) for i in range(start, tiles_around - 1, 2) for k in range(2)]

    parts = [plan.chunks[:1], plan.chunks[1:]]
    fields = []
    for chunks in parts:
        held_levels = sum(count for _, count in chunks)
        field = shape(len(chunks), plan.rows, plan.tiles, SUBS, LANES)
        edge = shape(len(chunks), halo, plan.tiles, SUBS, LANES)
        field, inner, outer = call(
            functools.partial(arrange_kernel, plan, chunks),
            (field, edge, edge),
            increment,
            scratch=[
                pltpu.VMEM((held_levels, *increment.shape[1:]), f32),
                pltpu.SemaphoreType.DMA,
            ],
            flops=10**7,
            first_spec=pl.BlockSpec(memory_space=pltpu.HBM),
        )
        outer = lax.ppermute(outer, "tile", swap(1))
        inner = lax.ppermute(inner, "tile", swap(0))
        fields += [(c, field, inner, outer) for c in range(len(chunks))]

    def exchange(blocks):
        if not isinstance(blocks, tuple):
            return [lax.all_to_all(blocks, "lev", 0, 0, tiled=True)]
        got = {0: blocks[0]}
        for d in reversed(range(1, group)):
            got[d] = lax.ppermute(blocks[d], "lev", [(i, i ^ d) for i in range(group)])
        return [got[d] for d in range(group)]

    together = [c in TOGETHER_CHUNKS for c in range(len(plan.chunks))]
    held, counts = [], []
    for c, (first, count) in enumerate(plan.chunks):
        factor = jnp.pad(kappa[first : first + count], (0, SUBS - count))
        factor = jnp.broadcast_to(factor[:, None], (SUBS, LANES))
        if count == SUBS:
            block = (plan.units, SUBS, LANES)
        else:
            block = (up_to(plan.units * count, SUBS), LANES)
        height = plan.rows_held + 2 * halo + TOGETHER
        blocks = call(
            functools.partial(diffuse_kernel, plan, count, fields[c][0], together[c]),
            shape(group, *block) if together[c] else (shape(*block),) * group,
            *fields[c][1:],
            factor,
            scratch=[pltpu.VMEM((height, plan.tiles, SUBS, LANES), f32)] * 2,
            flops=10**9,
        )
        got = exchange(blocks)
        counts.append(len(got))
        held += got

    stride = up_to(levels, SUBS)
    operator = jax.ShapeDtypeStruct((group * stride, group * levels), jnp.bfloat16)
    high, low = call(
        functools.partial(operator_kernel, plan, together),
        (operator, operator),
        correlation,
        balance,
        flops=10**8,
    )

    half = plan.units // 2
    splits = [(0, half), (half, plan.units)]
    back = []
    for begin, stop in splits:
        block = shape(up_to((stop - begin) * levels, SUBS), LANES)
        blocks = call(
            functools.partial(mix_kernel, plan, counts, begin, stop),
            (block,) * group,
            high,
            low,
            *held,
            flops=10**9,
        )
        back.append(exchange(blocks))

    partly = call(
        functools.partial(unpack_kernel, plan, *splits[0]),
        shape(plan.tiles, levels * plan.rows_held, LANES),
        *back[0],
        flops=10**7,
    )
    return call(
        functools.partial(finish_kernel, plan, *splits[1]),
        shape(*increment.shape),
        ground_level,
        partly,
        *back[1],
        flops=10**7,
    )


def solution(mesh):
    return jax.shard_map(
        program,
        mesh=mesh,
        in_specs=(P("lev", "tile", None), P("lev"), P(), P(), P("tile", None)),
        out_specs=P("lev", "tile", None),
        check_vma=False,
    )
```

profile of v0, /device:TPU:12, one launch (start us, length us, event | category | flops | bytes accessed | tf_op | source)
XLA Modules:
  0.0 171.9 jit_solution(16536251365426218178)
XLA Ops:
  3.0 1.9 %collective-permute-start.10 = (f32[2,10,12,8,128]{4,3,2,1,0:T(8,128)S(1)}, f32[2,10,12,8,128]{4,3,2,1,0:T(8,128)S(1)}, u32[]{:S(2)}, u32[]{:S(2)}) collective-permute-start(f32[2,10,12,8,128]{4,3,2,1,0:T(8,128)S(1)} %get-tuple-element.68), channel_id=1, source_target_pairs={{1,2},{2,1},{5,6},{6,5},{9,10},{10,9},{13,14},{14,13},{17,18},{18,... | collective-permute-start | bytes 2949128 | tf_op jit(solution)/shard_map/ppermute | solution.py:324
  6.5 3.6 %collective-permute-start.1 = (f32[1,10,12,8,128]{4,3,2,1,0:T(8,128)S(1)}, f32[1,10,12,8,128]{4,3,2,1,0:T(8,128)S(1)}, u32[]{:S(2)}, u32[]{:S(2)}) collective-permute-start(f32[1,10,12,8,128]{4,3,2,1,0:T(8,128)S(1)} %get-tuple-element.57), channel_id=1, source_target_pairs={{1,2},{2,1},{5,6},{6,5},{9,10},{10,9},{13,14},{14,13},{17,18},{18,... | collective-permute-start | bytes 1474568 | tf_op jit(solution)/shard_map/ppermute | solution.py:324
  10.2 13.5 %collective-permute-done.1.outer_ref = f32[1,10,12,8,128]{4,3,2,1,0:T(8,128)S(1)} collective-permute-done((f32[1,10,12,8,128]{4,3,2,1,0:T(8,128)S(1)}, f32[1,10,12,8,128]{4,3,2,1,0:T(8,128)S(1)}, u32[]{:S(2)}, u32[]{:S(2)}) %collective-permute-start.1) | collective-permute-done | bytes 491552 | tf_op jit(solution)/shard_map/ppermute | solution.py:324
  23.8 12.8 %shard_map.57 = (f32[34,8,128]{2,1,0:T(8,128)S(1)}, f32[34,8,128]{2,1,0:T(8,128)S(1)}, f32[34,8,128]{2,1,0:T(8,128)S(1)}, f32[34,8,128]{2,1,0:T(8,128)S(1)}, f32...) custom-call(f32[1,24,12,8,128]{4,3,2,1,0:T(8,128)S(1)} %get-tuple-ele, ...), custom_call_target="tpu_custom_call" | custom-call | flops 1000000000 | bytes 1048576 | tf_op jit(solution)/shard_map/pallas_call | solution.py:293
  40.1 2.0 %collective-permute-done.2.refs_1_ = f32[34,8,128]{2,1,0:T(8,128)S(1)} collective-permute-done((f32[34,8,128]{2,1,0:T(8,128)S(1)}, f32[34,8,128]{2,1,0:T(8,128)S(1)}, u32[]{:S(2)}, u32[]{:S(2)}) %collective-permute-start.2) | collective-permute-done | bytes 139296 | tf_op jit(solution)/shard_map/ppermute | solution.py:333
  42.1 2.2 %collective-permute-start.5 = (f32[34,8,128]{2,1,0:T(8,128)S(1)}, f32[34,8,128]{2,1,0:T(8,128)S(1)}, u32[]{:S(2)}, u32[]{:S(2)}) collective-permute-start(f32[34,8,128]{2,1,0:T(8,128)S(1)} %get-tuple-element.62), channel_id=1, source_target_pairs={{0,16},{4,20},{8,24},{12,28},{16,0},{20,4},{24,8},{28,12},{1,17},{... | collective-permute-start | bytes 417800 | tf_op jit(solution)/shard_map/ppermute | solution.py:333
  45.7 1.9 %collective-permute-start.7 = (f32[34,8,128]{2,1,0:T(8,128)S(1)}, f32[34,8,128]{2,1,0:T(8,128)S(1)}, u32[]{:S(2)}, u32[]{:S(2)}) collective-permute-start(f32[34,8,128]{2,1,0:T(8,128)S(1)} %get-tuple-element.64), channel_id=1, source_target_pairs={{0,24},{4,28},{8,16},{12,20},{16,8},{20,12},{24,0},{28,4},{1,25},{... | collective-permute-start | bytes 417800 | tf_op jit(solution)/shard_map/ppermute | solution.py:333
  48.8 12.8 %shard_map.59 = (f32[34,8,128]{2,1,0:T(8,128)S(1)}, f32[34,8,128]{2,1,0:T(8,128)S(1)}, f32[34,8,128]{2,1,0:T(8,128)S(1)}, f32[34,8,128]{2,1,0:T(8,128)S(1)}, f32...) custom-call(f32[2,24,12,8,128]{4,3,2,1,0:T(8,128)S(1)} %get-tuple-ele, ...), custom_call_target="tpu_custom_call" | custom-call | flops 1000000000 | bytes 1048576 | tf_op jit(solution)/shard_map/pallas_call | solution.py:293
  62.2 2.4 %collective-permute-start.12 = (f32[34,8,128]{2,1,0:T(8,128)S(1)}, f32[34,8,128]{2,1,0:T(8,128)S(1)}, u32[]{:S(2)}, u32[]{:S(2)}) collective-permute-start(f32[34,8,128]{2,1,0:T(8,128)S(1)} %get-tuple-element.71), channel_id=1, source_target_pairs={{0,8},{4,12},{8,0},{12,4},{16,24},{20,28},{24,16},{28,20},{1,9},{5... | collective-permute-start | bytes 417800 | tf_op jit(solution)/shard_map/ppermute | solution.py:333
  64.7 12.8 %shard_map.60 = (f32[72,128]{1,0:T(8,128)S(1)}, f32[72,128]{1,0:T(8,128)S(1)}, f32[72,128]{1,0:T(8,128)S(1)}, f32[72,128]{1,0:T(8,128)S(1)}, f32[72,128]{1,0:T(8...) custom-call(f32[2,24,12,8,128]{4,3,2,1,0:T(8,128)S(1)} %get-tuple-element.66.x_ref, ...), custom_call_target="tpu_custom_call" | custom-call | flops 1000000000 | bytes 1048576 | tf_op jit(solution)/shard_map/pallas_call | solution.py:293
  78.9 2.1 %collective-permute-start.20 = (f32[72,128]{1,0:T(8,128)S(1)}, f32[72,128]{1,0:T(8,128)S(1)}, u32[]{:S(2)}, u32[]{:S(2)}) collective-permute-start(f32[72,128]{1,0:T(8,128)S(1)} %get-tuple-element.80), channel_id=1, source_target_pairs={{0,12},{4,8},{8,4},{12,0},{16,28},{20,24},{24,20},{28,16},{1,13},{... | collective-permute-start | bytes 110600 | tf_op jit(solution)/shard_map/ppermute | solution.py:333
  81.5 2.2 %collective-permute-start.21 = (f32[72,128]{1,0:T(8,128)S(1)}, f32[72,128]{1,0:T(8,128)S(1)}, u32[]{:S(2)}, u32[]{:S(2)}) collective-permute-start(f32[72,128]{1,0:T(8,128)S(1)} %get-tuple-element.81), channel_id=1, source_target_pairs={{0,16},{4,20},{8,24},{12,28},{16,0},{20,4},{24,8},{28,12},{1,17},{... | collective-permute-start | bytes 110600 | tf_op jit(solution)/shard_map/ppermute | solution.py:333
  83.7 1.9 %collective-permute-start.22 = (f32[72,128]{1,0:T(8,128)S(1)}, f32[72,128]{1,0:T(8,128)S(1)}, u32[]{:S(2)}, u32[]{:S(2)}) collective-permute-start(f32[72,128]{1,0:T(8,128)S(1)} %get-tuple-element.82), channel_id=1, source_target_pairs={{0,20},{4,16},{8,28},{12,24},{16,4},{20,0},{24,12},{28,8},{1,21},{... | collective-permute-start | bytes 110600 | tf_op jit(solution)/shard_map/ppermute | solution.py:333
  86.8 1.9 %collective-permute-start.24 = (f32[72,128]{1,0:T(8,128)S(1)}, f32[72,128]{1,0:T(8,128)S(1)}, u32[]{:S(2)}, u32[]{:S(2)}) collective-permute-start(f32[72,128]{1,0:T(8,128)S(1)} %get-tuple-element.84), channel_id=1, source_target_pairs={{0,28},{4,24},{8,20},{12,16},{16,12},{20,8},{24,4},{28,0},{1,29},{... | collective-permute-start | bytes 110600 | tf_op jit(solution)/shard_map/ppermute | solution.py:333
  89.4 2.2 %collective-permute-start.13 = (f32[34,8,128]{2,1,0:T(8,128)S(1)}, f32[34,8,128]{2,1,0:T(8,128)S(1)}, u32[]{:S(2)}, u32[]{:S(2)}) collective-permute-start(f32[34,8,128]{2,1,0:T(8,128)S(1)} %get-tuple-element.72), channel_id=1, source_target_pairs={{0,12},{4,8},{8,4},{12,0},{16,28},{20,24},{24,20},{28,16},{1,13},{... | collective-permute-start | bytes 417800 | tf_op jit(solution)/shard_map/ppermute | solution.py:333
  91.6 3.0 %collective-permute-start.14 = (f32[34,8,128]{2,1,0:T(8,128)S(1)}, f32[34,8,128]{2,1,0:T(8,128)S(1)}, u32[]{:S(2)}, u32[]{:S(2)}) collective-permute-start(f32[34,8,128]{2,1,0:T(8,128)S(1)} %get-tuple-element.73), channel_id=1, source_target_pairs={{0,16},{4,20},{8,24},{12,28},{16,0},{20,4},{24,8},{28,12},{1,17},{... | collective-permute-start | bytes 417800 | tf_op jit(solution)/shard_map/ppermute | solution.py:333
  94.6 3.1 %collective-permute-start.15 = (f32[34,8,128]{2,1,0:T(8,128)S(1)}, f32[34,8,128]{2,1,0:T(8,128)S(1)}, u32[]{:S(2)}, u32[]{:S(2)}) collective-permute-start(f32[34,8,128]{2,1,0:T(8,128)S(1)} %get-tuple-element.74), channel_id=1, source_target_pairs={{0,20},{4,16},{8,28},{12,24},{16,4},{20,0},{24,12},{28,8},{1,21},{... | collective-permute-start | bytes 417800 | tf_op jit(solution)/shard_map/ppermute | solution.py:333
  100.3 11.3 %collective-permute-done.14.refs_12_ = f32[34,8,128]{2,1,0:T(8,128)S(1)} collective-permute-done((f32[34,8,128]{2,1,0:T(8,128)S(1)}, f32[34,8,128]{2,1,0:T(8,128)S(1)}, u32[]{:S(2)}, u32[]{:S(2)}) %collective-permute-start.14) | collective-permute-done | bytes 139296 | tf_op jit(solution)/shard_map/ppermute | solution.py:333
  111.6 4.7 %collective-permute-done.15.refs_13_ = f32[34,8,128]{2,1,0:T(8,128)S(1)} collective-permute-done((f32[34,8,128]{2,1,0:T(8,128)S(1)}, f32[34,8,128]{2,1,0:T(8,128)S(1)}, u32[]{:S(2)}, u32[]{:S(2)}) %collective-permute-start.15) | collective-permute-done | bytes 139296 | tf_op jit(solution)/shard_map/ppermute | solution.py:333
  116.3 4.7 %collective-permute-done.16.refs_14_ = f32[34,8,128]{2,1,0:T(8,128)S(1)} collective-permute-done((f32[34,8,128]{2,1,0:T(8,128)S(1)}, f32[34,8,128]{2,1,0:T(8,128)S(1)}, u32[]{:S(2)}, u32[]{:S(2)}) %collective-permute-start.16) | collective-permute-done | bytes 139296 | tf_op jit(solution)/shard_map/ppermute | solution.py:333
  121.0 8.1 %collective-permute-done.17.refs_15_ = f32[34,8,128]{2,1,0:T(8,128)S(1)} collective-permute-done((f32[34,8,128]{2,1,0:T(8,128)S(1)}, f32[34,8,128]{2,1,0:T(8,128)S(1)}, u32[]{:S(2)}, u32[]{:S(2)}) %collective-permute-start.17) | collective-permute-done | bytes 139296 | tf_op jit(solution)/shard_map/ppermute | solution.py:333
  134.2 2.0 %collective-permute-start.26 = (f32[312,128]{1,0:T(8,128)S(1)}, f32[312,128]{1,0:T(8,128)S(1)}, u32[]{:S(2)}, u32[]{:S(2)}) collective-permute-start(f32[312,128]{1,0:T(8,128)S(1)} %get-tuple-element.87), channel_id=1, source_target_pairs={{0,8},{4,12},{8,0},{12,4},{16,24},{20,28},{24,16},{28,20},{1,9},{5... | collective-permute-start | bytes 479240 | tf_op jit(solution)/shard_map/ppermute | solution.py:333
  137.5 1.9 %collective-permute-start.28 = (f32[312,128]{1,0:T(8,128)S(1)}, f32[312,128]{1,0:T(8,128)S(1)}, u32[]{:S(2)}, u32[]{:S(2)}) collective-permute-start(f32[312,128]{1,0:T(8,128)S(1)} %get-tuple-element.89), channel_id=1, source_target_pairs={{0,16},{4,20},{8,24},{12,28},{16,0},{20,4},{24,8},{28,12},{1,17},{... | collective-permute-start | bytes 479240 | tf_op jit(solution)/shard_map/ppermute | solution.py:333
  140.5 1.8 %collective-permute-start.30 = (f32[312,128]{1,0:T(8,128)S(1)}, f32[312,128]{1,0:T(8,128)S(1)}, u32[]{:S(2)}, u32[]{:S(2)}) collective-permute-start(f32[312,128]{1,0:T(8,128)S(1)} %get-tuple-element.91), channel_id=1, source_target_pairs={{0,24},{4,28},{8,16},{12,20},{16,8},{20,12},{24,0},{28,4},{1,25},{... | collective-permute-start | bytes 479240 | tf_op jit(solution)/shard_map/ppermute | solution.py:333
  143.4 3.4 %collective-permute-start.34 = (f32[312,128]{1,0:T(8,128)S(1)}, f32[312,128]{1,0:T(8,128)S(1)}, u32[]{:S(2)}, u32[]{:S(2)}) collective-permute-start(f32[312,128]{1,0:T(8,128)S(1)} %get-tuple-element.96), channel_id=1, source_target_pairs={{0,12},{4,8},{8,4},{12,0},{16,28},{20,24},{24,20},{28,16},{1,13},{... | collective-permute-start | bytes 479240 | tf_op jit(solution)/shard_map/ppermute | solution.py:333
  146.8 2.2 %collective-permute-done.28.refs_4_ = f32[312,128]{1,0:T(8,128)S(1)} collective-permute-done((f32[312,128]{1,0:T(8,128)S(1)}, f32[312,128]{1,0:T(8,128)S(1)}, u32[]{:S(2)}, u32[]{:S(2)}) %collective-permute-start.28) | collective-permute-done | bytes 159776 | tf_op jit(solution)/shard_map/ppermute | solution.py:333
  149.0 3.4 %collective-permute-start.35 = (f32[312,128]{1,0:T(8,128)S(1)}, f32[312,128]{1,0:T(8,128)S(1)}, u32[]{:S(2)}, u32[]{:S(2)}) collective-permute-start(f32[312,128]{1,0:T(8,128)S(1)} %get-tuple-element.97), channel_id=1, source_target_pairs={{0,16},{4,20},{8,24},{12,28},{16,0},{20,4},{24,8},{28,12},{1,17},{... | collective-permute-start | bytes 479240 | tf_op jit(solution)/shard_map/ppermute | solution.py:333
  152.5 4.2 %collective-permute-start.36 = (f32[312,128]{1,0:T(8,128)S(1)}, f32[312,128]{1,0:T(8,128)S(1)}, u32[]{:S(2)}, u32[]{:S(2)}) collective-permute-start(f32[312,128]{1,0:T(8,128)S(1)} %get-tuple-element.98), channel_id=1, source_target_pairs={{0,20},{4,16},{8,28},{12,24},{16,4},{20,0},{24,12},{28,8},{1,21},{... | collective-permute-start | bytes 479240 | tf_op jit(solution)/shard_map/ppermute | solution.py:333
  159.6 3.1 %collective-permute-done.35.refs_4_ = f32[312,128]{1,0:T(8,128)S(1)} collective-permute-done((f32[312,128]{1,0:T(8,128)S(1)}, f32[312,128]{1,0:T(8,128)S(1)}, u32[]{:S(2)}, u32[]{:S(2)}) %collective-permute-start.35) | collective-permute-done | bytes 159776 | tf_op jit(solution)/shard_map/ppermute | solution.py:333
  164.4 2.5 %collective-permute-done.37.refs_6_ = f32[312,128]{1,0:T(8,128)S(1)} collective-permute-done((f32[312,128]{1,0:T(8,128)S(1)}, f32[312,128]{1,0:T(8,128)S(1)}, u32[]{:S(2)}, u32[]{:S(2)}) %collective-permute-start.37) | collective-permute-done | bytes 159776 | tf_op jit(solution)/shard_map/ppermute | solution.py:333
  167.0 2.6 %collective-permute-done.38.refs_7_ = f32[312,128]{1,0:T(8,128)S(1)} collective-permute-done((f32[312,128]{1,0:T(8,128)S(1)}, f32[312,128]{1,0:T(8,128)S(1)}, u32[]{:S(2)}, u32[]{:S(2)}) %collective-permute-start.38) | collective-permute-done | bytes 159776 | tf_op jit(solution)/shard_map/ppermute | solution.py:333
  169.6 2.3 %shard_map.64 = f32[18,24,1440]{2,1,0:T(8,128)} custom-call(s32[24,1440]{1,0:T(8,128)S(1)} %copy-done.1, f32[12,432,128]{2,1,0:T(8,128)S(1)} %shard_map.62.held_ref, f32[312,128]{1,0:T(8,128)S(1)} %get-tuple-element.93.refs_0_, f32[312,128]{1,0:T(8,128)S(1)} %collective-permute-done.32.refs_1_, f32[312,128]{1,0:T(8,128)S(1)} %collective-permute-done.33.refs_2_, ...), custom_call_target="tpu_custom_call" | custom-call | flops 10000000 | bytes 1048576 | tf_op jit(solution)/shard_map/pallas_call | solution.py:293
  (72 shorter events, 31.1 us)
Async XLA Ops:
  3.0 42.7 %collective-permute-start.10 = (f32[2,10,12,8,128]{4,3,2,1,0:T(8,128)S(1)}, f32[2,10,12,8,128]{4,3,2,1,0:T(8,128)S(1)}, u32[]{:S(2)}, u32[]{:S(2)}) collective-permute-start(f32[2,10,12,8,128]{4,3,2,1,0:T(8,128)S(1)} %get-tuple-element.68), channel_id=1, source_target_pairs={{1,2},{2,1},{5,6},{6,5},{9,10},{10,9},{13,14},{14,13},{17,18},{18,... | collective-permute-start | bytes 2949128 | tf_op jit(solution)/shard_map/ppermute | solution.py:324
  5.0 42.7 %collective-permute-start.9 = (f32[2,10,12,8,128]{4,3,2,1,0:T(8,128)S(1)}, f32[2,10,12,8,128]{4,3,2,1,0:T(8,128)S(1)}, u32[]{:S(2)}, u32[]{:S(2)}) collective-permute-start(f32[2,10,12,8,128]{4,3,2,1,0:T(8,128)S(1)} %get-tuple-element.67), channel_id=1, source_target_pairs={{0,1},{1,0},{2,3},{3,2},{4,5},{5,4},{6,7},{7,6},{8,9},{9,8},{10,11... | collective-permute-start | bytes 2949128 | tf_op jit(solution)/shard_map/ppermute | solution.py:325
  6.5 17.3 %collective-permute-start.1 = (f32[1,10,12,8,128]{4,3,2,1,0:T(8,128)S(1)}, f32[1,10,12,8,128]{4,3,2,1,0:T(8,128)S(1)}, u32[]{:S(2)}, u32[]{:S(2)}) collective-permute-start(f32[1,10,12,8,128]{4,3,2,1,0:T(8,128)S(1)} %get-tuple-element.57), channel_id=1, source_target_pairs={{1,2},{2,1},{5,6},{6,5},{9,10},{10,9},{13,14},{14,13},{17,18},{18,... | collective-permute-start | bytes 1474568 | tf_op jit(solution)/shard_map/ppermute | solution.py:324
  38.1 6.2 %collective-permute-start.3 = (f32[34,8,128]{2,1,0:T(8,128)S(1)}, f32[34,8,128]{2,1,0:T(8,128)S(1)}, u32[]{:S(2)}, u32[]{:S(2)}) collective-permute-start(f32[34,8,128]{2,1,0:T(8,128)S(1)} %get-tuple-element.60), channel_id=1, source_target_pairs={{0,8},{4,12},{8,0},{12,4},{16,24},{20,28},{24,16},{28,20},{1,9},{5... | collective-permute-start | bytes 417800 | tf_op jit(solution)/shard_map/ppermute | solution.py:333
  38.6 23.0 %collective-permute-start.4 = (f32[34,8,128]{2,1,0:T(8,128)S(1)}, f32[34,8,128]{2,1,0:T(8,128)S(1)}, u32[]{:S(2)}, u32[]{:S(2)}) collective-permute-start(f32[34,8,128]{2,1,0:T(8,128)S(1)} %get-tuple-element.61), channel_id=1, source_target_pairs={{0,12},{4,8},{8,4},{12,0},{16,28},{20,24},{24,20},{28,16},{1,13},{... | collective-permute-start | bytes 417800 | tf_op jit(solution)/shard_map/ppermute | solution.py:333
  42.1 20.1 %collective-permute-start.5 = (f32[34,8,128]{2,1,0:T(8,128)S(1)}, f32[34,8,128]{2,1,0:T(8,128)S(1)}, u32[]{:S(2)}, u32[]{:S(2)}) collective-permute-start(f32[34,8,128]{2,1,0:T(8,128)S(1)} %get-tuple-element.62), channel_id=1, source_target_pairs={{0,16},{4,20},{8,24},{12,28},{16,0},{20,4},{24,8},{28,12},{1,17},{... | collective-permute-start | bytes 417800 | tf_op jit(solution)/shard_map/ppermute | solution.py:333
  44.4 33.1 %collective-permute-start.6 = (f32[34,8,128]{2,1,0:T(8,128)S(1)}, f32[34,8,128]{2,1,0:T(8,128)S(1)}, u32[]{:S(2)}, u32[]{:S(2)}) collective-permute-start(f32[34,8,128]{2,1,0:T(8,128)S(1)} %get-tuple-element.63), channel_id=1, source_target_pairs={{0,20},{4,16},{8,28},{12,24},{16,4},{20,0},{24,12},{28,8},{1,21},{... | collective-permute-start | bytes 417800 | tf_op jit(solution)/shard_map/ppermute | solution.py:333
  45.7 33.2 %collective-permute-start.7 = (f32[34,8,128]{2,1,0:T(8,128)S(1)}, f32[34,8,128]{2,1,0:T(8,128)S(1)}, u32[]{:S(2)}, u32[]{:S(2)}) collective-permute-start(f32[34,8,128]{2,1,0:T(8,128)S(1)} %get-tuple-element.64), channel_id=1, source_target_pairs={{0,24},{4,28},{8,16},{12,20},{16,8},{20,12},{24,0},{28,4},{1,25},{... | collective-permute-start | bytes 417800 | tf_op jit(solution)/shard_map/ppermute | solution.py:333
  47.7 31.2 %collective-permute-start.8 = (f32[34,8,128]{2,1,0:T(8,128)S(1)}, f32[34,8,128]{2,1,0:T(8,128)S(1)}, u32[]{:S(2)}, u32[]{:S(2)}) collective-permute-start(f32[34,8,128]{2,1,0:T(8,128)S(1)} %get-tuple-element.65), channel_id=1, source_target_pairs={{0,28},{4,24},{8,20},{12,16},{16,12},{20,8},{24,4},{28,0},{1,29},{... | collective-permute-start | bytes 417800 | tf_op jit(solution)/shard_map/ppermute | solution.py:333
  61.6 36.1 %collective-permute-start.11 = (f32[34,8,128]{2,1,0:T(8,128)S(1)}, f32[34,8,128]{2,1,0:T(8,128)S(1)}, u32[]{:S(2)}, u32[]{:S(2)}) collective-permute-start(f32[34,8,128]{2,1,0:T(8,128)S(1)} %get-tuple-element.70), channel_id=1, source_target_pairs={{0,4},{4,0},{8,12},{12,8},{16,20},{20,16},{24,28},{28,24},{1,5},{5... | collective-permute-start | bytes 417800 | tf_op jit(solution)/shard_map/ppermute | solution.py:333
  62.2 35.5 %collective-permute-start.12 = (f32[34,8,128]{2,1,0:T(8,128)S(1)}, f32[34,8,128]{2,1,0:T(8,128)S(1)}, u32[]{:S(2)}, u32[]{:S(2)}) collective-permute-start(f32[34,8,128]{2,1,0:T(8,128)S(1)} %get-tuple-element.71), channel_id=1, source_target_pairs={{0,8},{4,12},{8,0},{12,4},{16,24},{20,28},{24,16},{28,20},{1,9},{5... | collective-permute-start | bytes 417800 | tf_op jit(solution)/shard_map/ppermute | solution.py:333
  78.9 6.6 %collective-permute-start.20 = (f32[72,128]{1,0:T(8,128)S(1)}, f32[72,128]{1,0:T(8,128)S(1)}, u32[]{:S(2)}, u32[]{:S(2)}) collective-permute-start(f32[72,128]{1,0:T(8,128)S(1)} %get-tuple-element.80), channel_id=1, source_target_pairs={{0,12},{4,8},{8,4},{12,0},{16,28},{20,24},{24,20},{28,16},{1,13},{... | collective-permute-start | bytes 110600 | tf_op jit(solution)/shard_map/ppermute | solution.py:333
  86.8 7.8 %collective-permute-start.24 = (f32[72,128]{1,0:T(8,128)S(1)}, f32[72,128]{1,0:T(8,128)S(1)}, u32[]{:S(2)}, u32[]{:S(2)}) collective-permute-start(f32[72,128]{1,0:T(8,128)S(1)} %get-tuple-element.84), channel_id=1, source_target_pairs={{0,28},{4,24},{8,20},{12,16},{16,12},{20,8},{24,4},{28,0},{1,29},{... | collective-permute-start | bytes 110600 | tf_op jit(solution)/shard_map/ppermute | solution.py:333
  89.4 10.8 %collective-permute-start.13 = (f32[34,8,128]{2,1,0:T(8,128)S(1)}, f32[34,8,128]{2,1,0:T(8,128)S(1)}, u32[]{:S(2)}, u32[]{:S(2)}) collective-permute-start(f32[34,8,128]{2,1,0:T(8,128)S(1)} %get-tuple-element.72), channel_id=1, source_target_pairs={{0,12},{4,8},{8,4},{12,0},{16,28},{20,24},{24,20},{28,16},{1,13},{... | collective-permute-start | bytes 417800 | tf_op jit(solution)/shard_map/ppermute | solution.py:333
  91.6 20.0 %collective-permute-start.14 = (f32[34,8,128]{2,1,0:T(8,128)S(1)}, f32[34,8,128]{2,1,0:T(8,128)S(1)}, u32[]{:S(2)}, u32[]{:S(2)}) collective-permute-start(f32[34,8,128]{2,1,0:T(8,128)S(1)} %get-tuple-element.73), channel_id=1, source_target_pairs={{0,16},{4,20},{8,24},{12,28},{16,0},{20,4},{24,8},{28,12},{1,17},{... | collective-permute-start | bytes 417800 | tf_op jit(solution)/shard_map/ppermute | solution.py:333
  94.6 21.7 %collective-permute-start.15 = (f32[34,8,128]{2,1,0:T(8,128)S(1)}, f32[34,8,128]{2,1,0:T(8,128)S(1)}, u32[]{:S(2)}, u32[]{:S(2)}) collective-permute-start(f32[34,8,128]{2,1,0:T(8,128)S(1)} %get-tuple-element.74), channel_id=1, source_target_pairs={{0,20},{4,16},{8,28},{12,24},{16,4},{20,0},{24,12},{28,8},{1,21},{... | collective-permute-start | bytes 417800 | tf_op jit(solution)/shard_map/ppermute | solution.py:333
  97.7 23.3 %collective-permute-start.16 = (f32[34,8,128]{2,1,0:T(8,128)S(1)}, f32[34,8,128]{2,1,0:T(8,128)S(1)}, u32[]{:S(2)}, u32[]{:S(2)}) collective-permute-start(f32[34,8,128]{2,1,0:T(8,128)S(1)} %get-tuple-element.75), channel_id=1, source_target_pairs={{0,24},{4,28},{8,16},{12,20},{16,8},{20,12},{24,0},{28,4},{1,25},{... | collective-permute-start | bytes 417800 | tf_op jit(solution)/shard_map/ppermute | solution.py:333
  97.7 31.4 %collective-permute-start.17 = (f32[34,8,128]{2,1,0:T(8,128)S(1)}, f32[34,8,128]{2,1,0:T(8,128)S(1)}, u32[]{:S(2)}, u32[]{:S(2)}) collective-permute-start(f32[34,8,128]{2,1,0:T(8,128)S(1)} %get-tuple-element.76), channel_id=1, source_target_pairs={{0,28},{4,24},{8,20},{12,16},{16,12},{20,8},{24,4},{28,0},{1,29},{... | collective-permute-start | bytes 417800 | tf_op jit(solution)/shard_map/ppermute | solution.py:333
  130.5 7.0 %collective-permute-start.32 = (f32[312,128]{1,0:T(8,128)S(1)}, f32[312,128]{1,0:T(8,128)S(1)}, u32[]{:S(2)}, u32[]{:S(2)}) collective-permute-start(f32[312,128]{1,0:T(8,128)S(1)} %get-tuple-element.94), channel_id=1, source_target_pairs={{0,4},{4,0},{8,12},{12,8},{16,20},{20,16},{24,28},{28,24},{1,5},{5... | collective-permute-start | bytes 479240 | tf_op jit(solution)/shard_map/ppermute | solution.py:333
  131.1 8.3 %collective-permute-start.33 = (f32[312,128]{1,0:T(8,128)S(1)}, f32[312,128]{1,0:T(8,128)S(1)}, u32[]{:S(2)}, u32[]{:S(2)}) collective-permute-start(f32[312,128]{1,0:T(8,128)S(1)} %get-tuple-element.95), channel_id=1, source_target_pairs={{0,8},{4,12},{8,0},{12,4},{16,24},{20,28},{24,16},{28,20},{1,9},{5... | collective-permute-start | bytes 479240 | tf_op jit(solution)/shard_map/ppermute | solution.py:333
  132.6 7.9 %collective-permute-start.25 = (f32[312,128]{1,0:T(8,128)S(1)}, f32[312,128]{1,0:T(8,128)S(1)}, u32[]{:S(2)}, u32[]{:S(2)}) collective-permute-start(f32[312,128]{1,0:T(8,128)S(1)} %get-tuple-element.86), channel_id=1, source_target_pairs={{0,4},{4,0},{8,12},{12,8},{16,20},{20,16},{24,28},{28,24},{1,5},{5... | collective-permute-start | bytes 479240 | tf_op jit(solution)/shard_map/ppermute | solution.py:333
  134.2 8.0 %collective-permute-start.26 = (f32[312,128]{1,0:T(8,128)S(1)}, f32[312,128]{1,0:T(8,128)S(1)}, u32[]{:S(2)}, u32[]{:S(2)}) collective-permute-start(f32[312,128]{1,0:T(8,128)S(1)} %get-tuple-element.87), channel_id=1, source_target_pairs={{0,8},{4,12},{8,0},{12,4},{16,24},{20,28},{24,16},{28,20},{1,9},{5... | collective-permute-start | bytes 479240 | tf_op jit(solution)/shard_map/ppermute | solution.py:333
  136.2 7.1 %collective-permute-start.27 = (f32[312,128]{1,0:T(8,128)S(1)}, f32[312,128]{1,0:T(8,128)S(1)}, u32[]{:S(2)}, u32[]{:S(2)}) collective-permute-start(f32[312,128]{1,0:T(8,128)S(1)} %get-tuple-element.88), channel_id=1, source_target_pairs={{0,12},{4,8},{8,4},{12,0},{16,28},{20,24},{24,20},{28,16},{1,13},{... | collective-permute-start | bytes 479240 | tf_op jit(solution)/shard_map/ppermute | solution.py:333
  137.5 11.5 %collective-permute-start.28 = (f32[312,128]{1,0:T(8,128)S(1)}, f32[312,128]{1,0:T(8,128)S(1)}, u32[]{:S(2)}, u32[]{:S(2)}) collective-permute-start(f32[312,128]{1,0:T(8,128)S(1)} %get-tuple-element.89), channel_id=1, source_target_pairs={{0,16},{4,20},{8,24},{12,28},{16,0},{20,4},{24,8},{28,12},{1,17},{... | collective-permute-start | bytes 479240 | tf_op jit(solution)/shard_map/ppermute | solution.py:333
  139.4 13.1 %collective-permute-start.29 = (f32[312,128]{1,0:T(8,128)S(1)}, f32[312,128]{1,0:T(8,128)S(1)}, u32[]{:S(2)}, u32[]{:S(2)}) collective-permute-start(f32[312,128]{1,0:T(8,128)S(1)} %get-tuple-element.90), channel_id=1, source_target_pairs={{0,20},{4,16},{8,28},{12,24},{16,4},{20,0},{24,12},{28,8},{1,21},{... | collective-permute-start | bytes 479240 | tf_op jit(solution)/shard_map/ppermute | solution.py:333
  140.5 16.3 %collective-permute-start.30 = (f32[312,128]{1,0:T(8,128)S(1)}, f32[312,128]{1,0:T(8,128)S(1)}, u32[]{:S(2)}, u32[]{:S(2)}) collective-permute-start(f32[312,128]{1,0:T(8,128)S(1)} %get-tuple-element.91), channel_id=1, source_target_pairs={{0,24},{4,28},{8,16},{12,20},{16,8},{20,12},{24,0},{28,4},{1,25},{... | collective-permute-start | bytes 479240 | tf_op jit(solution)/shard_map/ppermute | solution.py:333
  142.2 15.4 %collective-permute-start.31 = (f32[312,128]{1,0:T(8,128)S(1)}, f32[312,128]{1,0:T(8,128)S(1)}, u32[]{:S(2)}, u32[]{:S(2)}) collective-permute-start(f32[312,128]{1,0:T(8,128)S(1)} %get-tuple-element.92), channel_id=1, source_target_pairs={{0,28},{4,24},{8,20},{12,16},{16,12},{20,8},{24,4},{28,0},{1,29},{... | collective-permute-start | bytes 479240 | tf_op jit(solution)/shard_map/ppermute | solution.py:333
  143.4 16.2 %collective-permute-start.34 = (f32[312,128]{1,0:T(8,128)S(1)}, f32[312,128]{1,0:T(8,128)S(1)}, u32[]{:S(2)}, u32[]{:S(2)}) collective-permute-start(f32[312,128]{1,0:T(8,128)S(1)} %get-tuple-element.96), channel_id=1, source_target_pairs={{0,12},{4,8},{8,4},{12,0},{16,28},{20,24},{24,20},{28,16},{1,13},{... | collective-permute-start | bytes 479240 | tf_op jit(solution)/shard_map/ppermute | solution.py:333
  149.0 13.7 %collective-permute-start.35 = (f32[312,128]{1,0:T(8,128)S(1)}, f32[312,128]{1,0:T(8,128)S(1)}, u32[]{:S(2)}, u32[]{:S(2)}) collective-permute-start(f32[312,128]{1,0:T(8,128)S(1)} %get-tuple-element.97), channel_id=1, source_target_pairs={{0,16},{4,20},{8,24},{12,28},{16,0},{20,4},{24,8},{28,12},{1,17},{... | collective-permute-start | bytes 479240 | tf_op jit(solution)/shard_map/ppermute | solution.py:333
  152.5 11.9 %collective-permute-start.36 = (f32[312,128]{1,0:T(8,128)S(1)}, f32[312,128]{1,0:T(8,128)S(1)}, u32[]{:S(2)}, u32[]{:S(2)}) collective-permute-start(f32[312,128]{1,0:T(8,128)S(1)} %get-tuple-element.98), channel_id=1, source_target_pairs={{0,20},{4,16},{8,28},{12,24},{16,4},{20,0},{24,12},{28,8},{1,21},{... | collective-permute-start | bytes 479240 | tf_op jit(solution)/shard_map/ppermute | solution.py:333
  156.7 10.2 %collective-permute-start.37 = (f32[312,128]{1,0:T(8,128)S(1)}, f32[312,128]{1,0:T(8,128)S(1)}, u32[]{:S(2)}, u32[]{:S(2)}) collective-permute-start(f32[312,128]{1,0:T(8,128)S(1)} %get-tuple-element.99), channel_id=1, source_target_pairs={{0,24},{4,28},{8,16},{12,20},{16,8},{20,12},{24,0},{28,4},{1,25},{... | collective-permute-start | bytes 479240 | tf_op jit(solution)/shard_map/ppermute | solution.py:333
  157.6 12.0 %collective-permute-start.38 = (f32[312,128]{1,0:T(8,128)S(1)}, f32[312,128]{1,0:T(8,128)S(1)}, u32[]{:S(2)}, u32[]{:S(2)}) collective-permute-start(f32[312,128]{1,0:T(8,128)S(1)} %get-tuple-element.100), channel_id=1, source_target_pairs={{0,28},{4,24},{8,20},{12,16},{16,12},{20,8},{24,4},{28,0},{1,29},{... | collective-permute-start | bytes 479240 | tf_op jit(solution)/shard_map/ppermute | solution.py:333
  (12 other events, 158.6 us)
where the time goes:
time: 172 us
  starting transfers between devices  62.9 us (37%)
  waiting for transfers between devices  59.8 us (35%)
  Pallas kernels  46.9 us (27%)
  local copies, waits for them, and re-layouts  2.13 us (1%)
    ppermute x35, starting transfers between devices, exchange(): got[d] = lax.ppermute(blocks[d], 'lev', [(i, i ^ d) for i in range(group)])  56.7 us
    pallas_call x10, Pallas kernels, call(): pl.pallas_call(kernel, out_shape=outs, in_specs=[first_spec] + [VMEM] * (...  46.9 us
    ppermute x35, waiting for transfers between devices, exchange(): got[d] = lax.ppermute(blocks[d], 'lev', [(i, i ^ d) for i in range(group)])  46.3 us
    ppermute x2, waiting for transfers between devices, program(): outer = lax.ppermute(outer, 'tile', swap(1))  13.5 us
    ppermute x2, starting transfers between devices, program(): outer = lax.ppermute(outer, 'tile', swap(1))  5.55 us
  transfers between devices with their start and end apart: 39, of which 15 were waited for; matrix products, arithmetic and copies ran while one was open for 0% of the time, Pallas kernels for 24%

commit v1 on v0

--- a/solution.py
+++ b/solution.py
@@ -11,7 +11,8 @@
 PASSES = 10
 LANES = 128
 SUBS = 8
-TOGETHER = 8
+UNROLLS = (4, 2)
+DEAL = 4
 TOGETHER_CHUNKS = ()
 
 VMEM = pl.BlockSpec(memory_space=pltpu.VMEM)
@@ -38,6 +39,7 @@
         self.rest = self.lons % LANES
         self.tiles = self.full + 1
         assert self.halo <= self.rest and self.rest + 2 * self.halo <= LANES
+        assert PASSES % 2 == 0 and self.tiles % DEAL == 0 and self.rows % 2 == 0
         assert self.halo <= self.rows and group & (group - 1) == 0
         self.rows_each = -(-self.rows // group)
         self.rows_held = self.rows_each * group
@@ -51,12 +53,41 @@
     return lax.broadcasted_iota(jnp.int32, (SUBS, LANES), 1)
 
 
-def arrange_kernel(plan, chunks, x_ref, all_ref, inner_ref, outer_ref, x_vmem, sem):
-    begin = chunks[0][0]
-    levels = chunks[-1][0] + chunks[-1][1] - begin
-    copy = pltpu.make_async_copy(x_ref.at[begin : begin + levels], x_vmem, sem)
-    copy.start()
-    copy.wait()
+def swapped(tiles):
+    lane = lane_ids()
+    even, low = (lane & 32) == 0, lane < 64
+    a, b, c, d = tiles
+    first, second = (
+        (jnp.where(even, x, pltpu.roll(y, 32, 1)), jnp.where(even, pltpu.roll(x, 96, 1), y))
+        for x, y in ((a, b), (c, d))
+    )
+    (a, b), (c, d) = first, second
+    return [
+        jnp.where(low, a, pltpu.roll(c, 64, 1)),
+        jnp.where(low, b, pltpu.roll(d, 64, 1)),
+        jnp.where(low, pltpu.roll(a, 64, 1), c),
+        jnp.where(low, pltpu.roll(b, 64, 1), d),
+    ]
+
+
+def lanes_taken(value, index):
+    return jnp.take_along_axis(value, index, axis=1, mode="promise_in_bounds")
+
+
+def dealt(tiles):
+    lane = lane_ids()
+    index = 4 * (lane & 31) + (lane >> 5)
+    return swapped([lanes_taken(tile, index) for tile in tiles])
+
+
+def gathered(tiles):
+    lane = lane_ids()
+    index = 32 * (lane & 3) + (lane >> 2)
+    return [lanes_taken(tile, index) for tile in swapped(tiles)]
+
+
+def arrange_kernel(plan, chunks, alone, x_ref, all_ref, inner_ref, outer_ref):
+    begin = chunks[0][0] if alone else 0
     lane = lane_ids()
     even = lax.axis_index("tile") % 2 == 0
     inner_row = jnp.where(even, plan.rows - plan.halo, 0)
@@ -67,7 +98,7 @@
             def take(tile):
                 width = LANES if tile < plan.full else plan.rest
                 lanes = slice(tile * LANES, tile * LANES + width)
-                value = x_vmem[first - begin : first - begin + count, row, lanes]
+                value = x_ref[first - begin : first - begin + count, row, lanes]
                 if count < SUBS or width < LANES:
                     value = jnp.pad(value, ((0, SUBS - count), (0, LANES - width)))
                 return value
@@ -85,6 +116,19 @@
             )
             for tile, value in enumerate(values):
                 all_ref[c, row, tile] = value
+
+        unroll = next(u for u in UNROLLS if plan.rows % u == 0)
+
+        def deal(step, _):
+            for i in range(unroll):
+                row = step * unroll + i
+                for tile in range(0, plan.tiles, DEAL):
+                    values = [all_ref[c, row, tile + b] for b in range(DEAL)]
+                    for b, value in enumerate(dealt(values)):
+                        all_ref[c, row, tile + b] = value
+            return 0
+
+        lax.fori_loop(0, plan.rows // unroll, deal, 0)
         for row in range(plan.halo):
             for tile in range(plan.tiles):
                 inner_ref[c, row, tile] = all_ref[c, inner_row + row, tile]
@@ -95,12 +139,15 @@
     out_refs, (a_ref, b_ref) = refs[:-2], refs[-2:]
     me = lax.axis_index("lev")
     tile_index = lax.axis_index("tile")
-    rows_total = plan.rows * lax.axis_size("tile")
-    first_row = tile_index * plan.rows - plan.halo
     height = plan.rows + 2 * plan.halo
     lane = lane_ids()
     at_start, at_end = lane == 0, lane == LANES - 1
     kappa = kappa_ref[...]
+    ratio = (1.0 - 4.0 * kappa) / kappa
+    kept = {
+        plan.halo - 1: jnp.where(tile_index == 0, 0.0, 1.0),
+        plan.halo + plan.rows: jnp.where(tile_index == lax.axis_size("tile") - 1, 0.0, 1.0),
+    }
     below = plan.halo + plan.rows
     inner_row = jnp.where(tile_index % 2 == 0, below, 0)
     for row in range(plan.halo):
@@ -108,38 +155,65 @@
         a_ref[below - inner_row + row] = outer_ref[at, row]
     a_ref[plan.halo : below] = x_ref[at]
 
-    def sweep(source, target, done):
-        def one_row(row):
+    groups = range(0, plan.tiles, DEAL)
+
+    def sweep(source, target, first, stop):
+        def turned(row):
+            left = [pltpu.roll(source[row, t], LANES - 1, 1) for t in groups]
+            right = [pltpu.roll(source[row, t + DEAL - 1], 1, 1) for t in groups]
+            return left, right
+
+        ahead = turned(first)
+        for row in range(first, stop):
+            left, right = ahead
+            if row + 1 < stop:
+                ahead = turned(row + 1)
             here = [source[row, tile] for tile in range(plan.tiles)]
-            right = [pltpu.roll(value, 1, 1) for value in here]
-            left = [pltpu.roll(value, LANES - 1, 1) for value in here]
-            inside = (first_row + row >= 0) & (first_row + row < rows_total)
-            weight = jnp.where(inside, kappa, 0.0)
-            centre = 1.0 - 4.0 * weight
             for tile in range(plan.tiles):
-                west = jnp.where(at_start, right[tile - 1], right[tile])
-                east = jnp.where(at_end, left[(tile + 1) % plan.tiles], left[tile])
+                g = tile // DEAL
+                if tile % DEAL == 0:
+                    west = jnp.where(at_start, right[g - 1], right[g])
+                else:
+                    west = here[tile - 1]
+                if tile % DEAL == DEAL - 1:
+                    east = jnp.where(at_end, left[(g + 1) % len(groups)], left[g])
+                else:
+                    east = here[tile + 1]
                 beside = (source[row - 1, tile] + source[row + 1, tile]) + (west + east)
-                target[row, tile] = centre * here[tile] + weight * beside
-
-        def some_rows(step, _):
-            for i in range(TOGETHER):
-                one_row(done + 1 + step * TOGETHER + i)
+                value = ratio * here[tile] + beside
+                target[row, tile] = value * kept[row] if row in kept else value
+
+    def two_passes(done):
+        def body(step, _):
+            sweep(a_ref, b_ref, done + 1, height - 1 - done)
+            sweep(b_ref, a_ref, done + 2, height - 2 - done)
             return 0
 
-        count = height - 2 - 2 * done
-        lax.fori_loop(0, (count + TOGETHER - 1) // TOGETHER, some_rows, 0)
-
-    def two_passes(step, _):
-        sweep(a_ref, b_ref, 2 * step)
-        sweep(b_ref, a_ref, 2 * step + 1)
+        return body
+
+    early = PASSES // 4
+    lax.fori_loop(0, early, two_passes(0), 0)
+    lax.fori_loop(early, PASSES // 2, two_passes(2 * early), 0)
+    power = kappa
+    for _ in range(PASSES - 1):
+        power = power * kappa
+
+    unroll = next(u for u in UNROLLS if plan.rows % u == 0)
+
+    def undo(step, _):
+        for i in range(unroll):
+            row = step * unroll + i
+            for tile in groups:
+                values = [a_ref[plan.halo + row, tile + b] * power for b in range(DEAL)]
+                for b, value in enumerate(gathered(values)):
+                    b_ref[row, tile + b] = value
         return 0
 
-    lax.fori_loop(0, PASSES // 2, two_passes, 0)
+    lax.fori_loop(0, plan.rows // unroll, undo, 0)
 
     for d in range(plan.group):
         out_ref = out_refs[0].at[d] if together else out_refs[d]
-        base = plan.halo + (d if together else me ^ d) * plan.rows_each
+        base = (d if together else me ^ d) * plan.rows_each
 
         def put(unit, value):
             if count == SUBS:
@@ -149,13 +223,13 @@
 
         for i in range(plan.rows_each):
             for tile in range(plan.full):
-                put(i * plan.full + tile, a_ref[base + i, tile])
+                put(i * plan.full + tile, b_ref[base + i, tile])
         for m in range(plan.merged):
             value = None
             for k in range(plan.per_merged):
                 i = m * plan.per_merged + k
                 if i < plan.rows_each:
-                    piece = a_ref[base + i, plan.full]
+                    piece = b_ref[base + i, plan.full]
                     if k == 0:
                         value = piece
                     else:
@@ -289,37 +363,30 @@
     def shape(*dims):
         return jax.ShapeDtypeStruct(dims, f32)
 
-    def call(kernel, outs, *args, scratch=(), flops, first_spec=VMEM, aliases=None):
+    def call(kernel, outs, *args, scratch=(), flops, vmem=14 << 20):
         return pl.pallas_call(
             kernel,
             out_shape=outs,
-            in_specs=[first_spec] + [VMEM] * (len(args) - 1),
+            in_specs=[VMEM] * len(args),
             out_specs=jax.tree.map(lambda _: VMEM, outs),
             scratch_shapes=list(scratch),
-            input_output_aliases=aliases or {},
-            compiler_params=pltpu.CompilerParams(vmem_limit_bytes=14 << 20),
+            compiler_params=pltpu.CompilerParams(vmem_limit_bytes=vmem),
             cost_estimate=pl.CostEstimate(flops=flops, bytes_accessed=1 << 20, transcendentals=0),
         )(*args)
 
     def swap(start):
         return [(i + k, i + 1 - k) for i in range(start, tiles_around - 1, 2) for k in range(2)]
 
-    parts = [plan.chunks[:1], plan.chunks[1:]]
+    parts = [[chunk] for chunk in plan.chunks]
     fields = []
-    for chunks in parts:
-        held_levels = sum(count for _, count in chunks)
+    for p, chunks in enumerate(parts):
         field = shape(len(chunks), plan.rows, plan.tiles, SUBS, LANES)
         edge = shape(len(chunks), halo, plan.tiles, SUBS, LANES)
         field, inner, outer = call(
-            functools.partial(arrange_kernel, plan, chunks),
+            functools.partial(arrange_kernel, plan, chunks, p == 0),
             (field, edge, edge),
-            increment,
-            scratch=[
-                pltpu.VMEM((held_levels, *increment.shape[1:]), f32),
-                pltpu.SemaphoreType.DMA,
-            ],
+            increment[: chunks[0][1]] if p == 0 else increment,
             flops=10**7,
-            first_spec=pl.BlockSpec(memory_space=pltpu.HBM),
         )
         outer = lax.ppermute(outer, "tile", swap(1))
         inner = lax.ppermute(inner, "tile", swap(0))
@@ -336,13 +403,15 @@
     together = [c in TOGETHER_CHUNKS for c in range(len(plan.chunks))]
     held, counts = [], []
     for c, (first, count) in enumerate(plan.chunks):
-        factor = jnp.pad(kappa[first : first + count], (0, SUBS - count))
+        factor = jnp.pad(
+            kappa[first : first + count], (0, SUBS - count), constant_values=0.125
+        )
         factor = jnp.broadcast_to(factor[:, None], (SUBS, LANES))
         if count == SUBS:
             block = (plan.units, SUBS, LANES)
         else:
             block = (up_to(plan.units * count, SUBS), LANES)
-        height = plan.rows_held + 2 * halo + TOGETHER
+        height = plan.rows_held + 2 * halo
         blocks = call(
             functools.partial(diffuse_kernel, plan, count, fields[c][0], together[c]),
             shape(group, *block) if together[c] else (shape(*block),) * group,

time: 172 us -> 172 us (level)
  the two profiles are of different devices: /device:TPU:12 before, /device:TPU:0 now
where the time goes in v1:
time: 172 us; the launch traced here: 169 us
  starting transfers between devices  77.8 us (45%)
  waiting for transfers between devices  58.9 us (34%)
  Pallas kernels  30.4 us (18%)
  local copies, waits for them, and re-layouts  2.2 us (1%)
    ppermute x35, starting transfers between devices, exchange(): got[d] = lax.ppermute(blocks[d], 'lev', [(i, i ^ d) for i in range(group)])  69.9 us
    ppermute x35, waiting for transfers between devices, exchange(): got[d] = lax.ppermute(blocks[d], 'lev', [(i, i ^ d) for i in range(group)])  58.9 us
    pallas_call x11, Pallas kernels, call(): pl.pallas_call(kernel, out_shape=outs, in_specs=[VMEM] * len(args), out_s...  30.4 us
    ppermute x3, starting transfers between devices, program(): inner = lax.ppermute(inner, 'tile', swap(0))  5.68 us
  transfers between devices with their start and end apart: 41, of which 9 were waited for; matrix products, arithmetic and copies ran while one was open for 0% of the time, Pallas kernels for 15%

profile of v1, /device:TPU:0, one launch (start us, length us, event | category | flops | bytes accessed | tf_op | source)
XLA Modules:
  0.0 169.4 jit_solution(14754552769513959987)
XLA Ops:
  0.0 1.7 %copy-done = f32[18,24,1440]{2,1,0:T(8,128)S(1)} copy-done((f32[18,24,1440]{2,1,0:T(8,128)S(1)}, f32[18,24,1440]{2,1,0:T(8,128)}, u32[]{:S(2)}) %copy-start) | copy-done | bytes 2488344
  1.8 1.8 %shard_map.60 = (f32[1,24,12,8,128]{4,3,2,1,0:T(8,128)S(1)}, f32[1,10,12,8,128]{4,3,2,1,0:T(8,128)S(1)}, f32[1,10,12,8,128]{4,3,2,1,0:T(8,128)S(1)}) custom-call(f32[18,24,1440]{2,1,0:T(8,128)S(1)} %copy-done), custom_call_target="tpu_custom_call" | custom-call | flops 10000000 | bytes 1048576 | tf_op jit(solution)/shard_map/pallas_call | solution.py:367
  4.9 2.1 %shard_map.56 = (f32[1,24,12,8,128]{4,3,2,1,0:T(8,128)S(1)}, f32[1,10,12,8,128]{4,3,2,1,0:T(8,128)S(1)}, f32[1,10,12,8,128]{4,3,2,1,0:T(8,128)S(1)}) custom-call(f32[8,24,1440]{2,1,0:T(8,128)S(1)} %slice.12.x_ref), custom_call_target="tpu_custom_call" | custom-call | flops 10000000 | bytes 1048576 | tf_op jit(solution)/shard_map/pallas_call | solution.py:367
  7.0 3.9 %collective-permute-start = (f32[1,10,12,8,128]{4,3,2,1,0:T(8,128)S(1)}, f32[1,10,12,8,128]{4,3,2,1,0:T(8,128)S(1)}, u32[]{:S(2)}, u32[]{:S(2)}) collective-permute-start(f32[1,10,12,8,128]{4,3,2,1,0:T(8,128)S(1)} %get-tuple-element.59), channel_id=1, source_target_pairs={{0,1},{1,0},{2,3},{3,2},{4,5},{5,4},{6,7},{7,6},{8,9},{9,8},{10,11... | collective-permute-start | bytes 1474568 | tf_op jit(solution)/shard_map/ppermute | solution.py:392
  11.8 2.1 %shard_map.58 = (f32[1,24,12,8,128]{4,3,2,1,0:T(8,128)S(1)}, f32[1,10,12,8,128]{4,3,2,1,0:T(8,128)S(1)}, f32[1,10,12,8,128]{4,3,2,1,0:T(8,128)S(1)}) custom-call(f32[18,24,1440]{2,1,0:T(8,128)S(1)} %copy-done.1), custom_call_target="tpu_custom_call" | custom-call | flops 10000000 | bytes 1048576 | tf_op jit(solution)/shard_map/pallas_call | solution.py:367
  16.0 5.9 %shard_map.61 = (f32[72,128]{1,0:T(8,128)S(1)}, f32[72,128]{1,0:T(8,128)S(1)}, f32[72,128]{1,0:T(8,128)S(1)}, f32[72,128]{1,0:T(8,128)S(1)}, f32[72,128]{1,0:T(8...) custom-call(f32[1,24,12,8,128]{4,3,2,1,0:T(8,128)S(1)} %get-tuple-element.80.x_ref, ...), custom_call_target="tpu_custom_call" | custom-call | flops 1000000000 | bytes 1048576 | tf_op jit(solution)/shard_map/pallas_call | solution.py:367
  22.0 2.1 %collective-permute-start.20 = (f32[72,128]{1,0:T(8,128)S(1)}, f32[72,128]{1,0:T(8,128)S(1)}, u32[]{:S(2)}, u32[]{:S(2)}) collective-permute-start(f32[72,128]{1,0:T(8,128)S(1)} %get-tuple-element.84), channel_id=1, source_target_pairs={{0,4},{4,0},{8,12},{12,8},{16,20},{20,16},{24,28},{28,24},{1,5},{5... | collective-permute-start | bytes 110600 | tf_op jit(solution)/shard_map/ppermute | solution.py:400
  25.7 3.0 %collective-permute-start.23 = (f32[72,128]{1,0:T(8,128)S(1)}, f32[72,128]{1,0:T(8,128)S(1)}, u32[]{:S(2)}, u32[]{:S(2)}) collective-permute-start(f32[72,128]{1,0:T(8,128)S(1)} %get-tuple-element.87), channel_id=1, source_target_pairs={{0,16},{4,20},{8,24},{12,28},{16,0},{20,4},{24,8},{28,12},{1,17},{... | collective-permute-start | bytes 110600 | tf_op jit(solution)/shard_map/ppermute | solution.py:400
  30.0 5.9 %shard_map.57 = (f32[34,8,128]{2,1,0:T(8,128)S(1)}, f32[34,8,128]{2,1,0:T(8,128)S(1)}, f32[34,8,128]{2,1,0:T(8,128)S(1)}, f32[34,8,128]{2,1,0:T(8,128)S(1)}, f32...) custom-call(f32[1,24,12,8,128]{4,3,2,1,0:T(8,128)S(1)} %get-tuple-ele, ...), custom_call_target="tpu_custom_call" | custom-call | flops 1000000000 | bytes 1048576 | tf_op jit(solution)/shard_map/pallas_call | solution.py:367
  36.3 1.8 %collective-permute-start.3 = (f32[34,8,128]{2,1,0:T(8,128)S(1)}, f32[34,8,128]{2,1,0:T(8,128)S(1)}, u32[]{:S(2)}, u32[]{:S(2)}) collective-permute-start(f32[34,8,128]{2,1,0:T(8,128)S(1)} %get-tuple-element.63), channel_id=1, source_target_pairs={{0,8},{4,12},{8,0},{12,4},{16,24},{20,28},{24,16},{28,20},{1,9},{5... | collective-permute-start | bytes 417800 | tf_op jit(solution)/shard_map/ppermute | solution.py:400
  39.5 2.6 %collective-permute-start.5 = (f32[34,8,128]{2,1,0:T(8,128)S(1)}, f32[34,8,128]{2,1,0:T(8,128)S(1)}, u32[]{:S(2)}, u32[]{:S(2)}) collective-permute-start(f32[34,8,128]{2,1,0:T(8,128)S(1)} %get-tuple-element.65), channel_id=1, source_target_pairs={{0,16},{4,20},{8,24},{12,28},{16,0},{20,4},{24,8},{28,12},{1,17},{... | collective-permute-start | bytes 417800 | tf_op jit(solution)/shard_map/ppermute | solution.py:400
  43.5 8.2 %collective-permute-done.25.refs_22_ = f32[72,128]{1,0:T(8,128)S(1)} collective-permute-done((f32[72,128]{1,0:T(8,128)S(1)}, f32[72,128]{1,0:T(8,128)S(1)}, u32[]{:S(2)}, u32[]{:S(2)}) %collective-permute-start.25) | collective-permute-done | bytes 36896 | tf_op jit(solution)/shard_map/ppermute | solution.py:400
  51.7 2.5 %collective-permute-start.26 = (f32[72,128]{1,0:T(8,128)S(1)}, f32[72,128]{1,0:T(8,128)S(1)}, u32[]{:S(2)}, u32[]{:S(2)}) collective-permute-start(f32[72,128]{1,0:T(8,128)S(1)} %get-tuple-element.90), channel_id=1, source_target_pairs={{0,28},{4,24},{8,20},{12,16},{16,12},{20,8},{24,4},{28,0},{1,29},{... | collective-permute-start | bytes 110600 | tf_op jit(solution)/shard_map/ppermute | solution.py:400
  54.2 6.1 %shard_map.59 = (f32[34,8,128]{2,1,0:T(8,128)S(1)}, f32[34,8,128]{2,1,0:T(8,128)S(1)}, f32[34,8,128]{2,1,0:T(8,128)S(1)}, f32[34,8,128]{2,1,0:T(8,128)S(1)}, f32...) custom-call(f32[1,24,12,8,128]{4,3,2,1,0:T(8,128)S(1)} %get-tuple-ele, ...), custom_call_target="tpu_custom_call" | custom-call | flops 1000000000 | bytes 1048576 | tf_op jit(solution)/shard_map/pallas_call | solution.py:367
  60.6 3.3 %collective-permute-start.7 = (f32[34,8,128]{2,1,0:T(8,128)S(1)}, f32[34,8,128]{2,1,0:T(8,128)S(1)}, u32[]{:S(2)}, u32[]{:S(2)}) collective-permute-start(f32[34,8,128]{2,1,0:T(8,128)S(1)} %get-tuple-element.67), channel_id=1, source_target_pairs={{0,24},{4,28},{8,16},{12,20},{16,8},{20,12},{24,0},{28,4},{1,25},{... | collective-permute-start | bytes 417800 | tf_op jit(solution)/shard_map/ppermute | solution.py:400
  66.7 8.5 %collective-permute-done.6.refs_5_ = f32[34,8,128]{2,1,0:T(8,128)S(1)} collective-permute-done((f32[34,8,128]{2,1,0:T(8,128)S(1)}, f32[34,8,128]{2,1,0:T(8,128)S(1)}, u32[]{:S(2)}, u32[]{:S(2)}) %collective-permute-start.6) | collective-permute-done | bytes 139296 | tf_op jit(solution)/shard_map/ppermute | solution.py:400
  75.2 3.5 %collective-permute-start.14 = (f32[34,8,128]{2,1,0:T(8,128)S(1)}, f32[34,8,128]{2,1,0:T(8,128)S(1)}, u32[]{:S(2)}, u32[]{:S(2)}) collective-permute-start(f32[34,8,128]{2,1,0:T(8,128)S(1)} %get-tuple-element.76), channel_id=1, source_target_pairs={{0,16},{4,20},{8,24},{12,28},{16,0},{20,4},{24,8},{28,12},{1,17},{... | collective-permute-start | bytes 417800 | tf_op jit(solution)/shard_map/ppermute | solution.py:400
  78.7 8.1 %collective-permute-start.15 = (f32[34,8,128]{2,1,0:T(8,128)S(1)}, f32[34,8,128]{2,1,0:T(8,128)S(1)}, u32[]{:S(2)}, u32[]{:S(2)}) collective-permute-start(f32[34,8,128]{2,1,0:T(8,128)S(1)} %get-tuple-element.77), channel_id=1, source_target_pairs={{0,20},{4,16},{8,28},{12,24},{16,4},{20,0},{24,12},{28,8},{1,21},{... | collective-permute-start | bytes 417800 | tf_op jit(solution)/shard_map/ppermute | solution.py:400
  86.8 2.4 %collective-permute-start.16 = (f32[34,8,128]{2,1,0:T(8,128)S(1)}, f32[34,8,128]{2,1,0:T(8,128)S(1)}, u32[]{:S(2)}, u32[]{:S(2)}) collective-permute-start(f32[34,8,128]{2,1,0:T(8,128)S(1)} %get-tuple-element.78), channel_id=1, source_target_pairs={{0,24},{4,28},{8,16},{12,20},{16,8},{20,12},{24,0},{28,4},{1,25},{... | collective-permute-start | bytes 417800 | tf_op jit(solution)/shard_map/ppermute | solution.py:400
  90.4 9.8 %collective-permute-done.15.refs_13_ = f32[34,8,128]{2,1,0:T(8,128)S(1)} collective-permute-done((f32[34,8,128]{2,1,0:T(8,128)S(1)}, f32[34,8,128]{2,1,0:T(8,128)S(1)}, u32[]{:S(2)}, u32[]{:S(2)}) %collective-permute-start.15) | collective-permute-done | bytes 139296 | tf_op jit(solution)/shard_map/ppermute | solution.py:400
  103.3 6.4 %collective-permute-start.35 = (f32[312,128]{1,0:T(8,128)S(1)}, f32[312,128]{1,0:T(8,128)S(1)}, u32[]{:S(2)}, u32[]{:S(2)}) collective-permute-start(f32[312,128]{1,0:T(8,128)S(1)} %get-tuple-element.101), channel_id=1, source_target_pairs={{0,8},{4,12},{8,0},{12,4},{16,24},{20,28},{24,16},{28,20},{1,9},{5... | collective-permute-start | bytes 479240 | tf_op jit(solution)/shard_map/ppermute | solution.py:400
  111.8 3.0 %collective-permute-start.29 = (f32[312,128]{1,0:T(8,128)S(1)}, f32[312,128]{1,0:T(8,128)S(1)}, u32[]{:S(2)}, u32[]{:S(2)}) collective-permute-start(f32[312,128]{1,0:T(8,128)S(1)} %get-tuple-element.94), channel_id=1, source_target_pairs={{0,12},{4,8},{8,4},{12,0},{16,28},{20,24},{24,20},{28,16},{1,13},{... | collective-permute-start | bytes 479240 | tf_op jit(solution)/shard_map/ppermute | solution.py:400
  117.6 2.3 %collective-permute-start.32 = (f32[312,128]{1,0:T(8,128)S(1)}, f32[312,128]{1,0:T(8,128)S(1)}, u32[]{:S(2)}, u32[]{:S(2)}) collective-permute-start(f32[312,128]{1,0:T(8,128)S(1)} %get-tuple-element.97), channel_id=1, source_target_pairs={{0,24},{4,28},{8,16},{12,20},{16,8},{20,12},{24,0},{28,4},{1,25},{... | collective-permute-start | bytes 479240 | tf_op jit(solution)/shard_map/ppermute | solution.py:400
  119.9 3.6 %collective-permute-done.28.refs_2_ = f32[312,128]{1,0:T(8,128)S(1)} collective-permute-done((f32[312,128]{1,0:T(8,128)S(1)}, f32[312,128]{1,0:T(8,128)S(1)}, u32[]{:S(2)}, u32[]{:S(2)}) %collective-permute-start.28) | collective-permute-done | bytes 159776 | tf_op jit(solution)/shard_map/ppermute | solution.py:400
  123.5 2.4 %collective-permute-start.33 = (f32[312,128]{1,0:T(8,128)S(1)}, f32[312,128]{1,0:T(8,128)S(1)}, u32[]{:S(2)}, u32[]{:S(2)}) collective-permute-start(f32[312,128]{1,0:T(8,128)S(1)} %get-tuple-element.98), channel_id=1, source_target_pairs={{0,28},{4,24},{8,20},{12,16},{16,12},{20,8},{24,4},{28,0},{1,29},{... | collective-permute-start | bytes 479240 | tf_op jit(solution)/shard_map/ppermute | solution.py:400
  126.5 9.9 %collective-permute-done.30.refs_4_ = f32[312,128]{1,0:T(8,128)S(1)} collective-permute-done((f32[312,128]{1,0:T(8,128)S(1)}, f32[312,128]{1,0:T(8,128)S(1)}, u32[]{:S(2)}, u32[]{:S(2)}) %collective-permute-start.30) | collective-permute-done | bytes 159776 | tf_op jit(solution)/shard_map/ppermute | solution.py:400
  136.4 4.6 %collective-permute-done.31.refs_5_ = f32[312,128]{1,0:T(8,128)S(1)} collective-permute-done((f32[312,128]{1,0:T(8,128)S(1)}, f32[312,128]{1,0:T(8,128)S(1)}, u32[]{:S(2)}, u32[]{:S(2)}) %collective-permute-start.31) | collective-permute-done | bytes 159776 | tf_op jit(solution)/shard_map/ppermute | solution.py:400
  141.0 9.6 %collective-permute-start.39 = (f32[312,128]{1,0:T(8,128)S(1)}, f32[312,128]{1,0:T(8,128)S(1)}, u32[]{:S(2)}, u32[]{:S(2)}) collective-permute-start(f32[312,128]{1,0:T(8,128)S(1)} %get-tuple-element.105), channel_id=1, source_target_pairs={{0,24},{4,28},{8,16},{12,20},{16,8},{20,12},{24,0},{28,4},{1,25},{... | collective-permute-start | bytes 479240 | tf_op jit(solution)/shard_map/ppermute | solution.py:400
  150.6 2.5 %collective-permute-start.40 = (f32[312,128]{1,0:T(8,128)S(1)}, f32[312,128]{1,0:T(8,128)S(1)}, u32[]{:S(2)}, u32[]{:S(2)}) collective-permute-start(f32[312,128]{1,0:T(8,128)S(1)} %get-tuple-element.106), channel_id=1, source_target_pairs={{0,28},{4,24},{8,20},{12,16},{16,12},{20,8},{24,4},{28,0},{1,29},{... | collective-permute-start | bytes 479240 | tf_op jit(solution)/shard_map/ppermute | solution.py:400
  153.5 10.3 %collective-permute-done.37.refs_4_ = f32[312,128]{1,0:T(8,128)S(1)} collective-permute-done((f32[312,128]{1,0:T(8,128)S(1)}, f32[312,128]{1,0:T(8,128)S(1)}, u32[]{:S(2)}, u32[]{:S(2)}) %collective-permute-start.37) | collective-permute-done | bytes 159776 | tf_op jit(solution)/shard_map/ppermute | solution.py:400
  163.8 3.3 %collective-permute-done.38.refs_5_ = f32[312,128]{1,0:T(8,128)S(1)} collective-permute-done((f32[312,128]{1,0:T(8,128)S(1)}, f32[312,128]{1,0:T(8,128)S(1)}, u32[]{:S(2)}, u32[]{:S(2)}) %collective-permute-start.38) | collective-permute-done | bytes 159776 | tf_op jit(solution)/shard_map/ppermute | solution.py:400
  167.1 2.3 %shard_map.65 = f32[18,24,1440]{2,1,0:T(8,128)} custom-call(s32[24,1440]{1,0:T(8,128)S(1)} %copy-done.2, f32[12,432,128]{2,1,0:T(8,128)S(1)} %shard_map.63.held_ref, f32[312,128]{1,0:T(8,128)S(1)} %get-tuple-element.99.refs_0_, f32[312,128]{1,0:T(8,128)S(1)} %collective-permute-done.34.refs_1_, f32[312,128]{1,0:T(8,128)S(1)} %collective-permute-done.35.refs_2_, ...), custom_call_target="tpu_custom_call" | custom-call | flops 10000000 | bytes 1048576 | tf_op jit(solution)/shard_map/pallas_call | solution.py:367
  (80 shorter events, 23.5 us)
Async XLA Ops:
  7.0 17.1 %collective-permute-start = (f32[1,10,12,8,128]{4,3,2,1,0:T(8,128)S(1)}, f32[1,10,12,8,128]{4,3,2,1,0:T(8,128)S(1)}, u32[]{:S(2)}, u32[]{:S(2)}) collective-permute-start(f32[1,10,12,8,128]{4,3,2,1,0:T(8,128)S(1)} %get-tuple-element.59), channel_id=1, source_target_pairs={{0,1},{1,0},{2,3},{3,2},{4,5},{5,4},{6,7},{7,6},{8,9},{9,8},{10,11... | collective-permute-start | bytes 1474568 | tf_op jit(solution)/shard_map/ppermute | solution.py:392
  11.0 14.7 %collective-permute-start.1 = (f32[1,10,12,8,128]{4,3,2,1,0:T(8,128)S(1)}, f32[1,10,12,8,128]{4,3,2,1,0:T(8,128)S(1)}, u32[]{:S(2)}, u32[]{:S(2)}) collective-permute-start(f32[1,10,12,8,128]{4,3,2,1,0:T(8,128)S(1)} %get-tuple-element.60), channel_id=1, source_target_pairs={{1,2},{2,1},{5,6},{6,5},{9,10},{10,9},{13,14},{14,13},{17,18},{18,... | collective-permute-start | bytes 1474568 | tf_op jit(solution)/shard_map/ppermute | solution.py:391
  15.1 13.6 %collective-permute-start.10 = (f32[1,10,12,8,128]{4,3,2,1,0:T(8,128)S(1)}, f32[1,10,12,8,128]{4,3,2,1,0:T(8,128)S(1)}, u32[]{:S(2)}, u32[]{:S(2)}) collective-permute-start(f32[1,10,12,8,128]{4,3,2,1,0:T(8,128)S(1)} %get-tuple-element.71), channel_id=1, source_target_pairs={{1,2},{2,1},{5,6},{6,5},{9,10},{10,9},{13,14},{14,13},{17,18},{18,... | collective-permute-start | bytes 1474568 | tf_op jit(solution)/shard_map/ppermute | solution.py:391
  22.0 14.0 %collective-permute-start.20 = (f32[72,128]{1,0:T(8,128)S(1)}, f32[72,128]{1,0:T(8,128)S(1)}, u32[]{:S(2)}, u32[]{:S(2)}) collective-permute-start(f32[72,128]{1,0:T(8,128)S(1)} %get-tuple-element.84), channel_id=1, source_target_pairs={{0,4},{4,0},{8,12},{12,8},{16,20},{20,16},{24,28},{28,24},{1,5},{5... | collective-permute-start | bytes 110600 | tf_op jit(solution)/shard_map/ppermute | solution.py:400
  25.7 12.5 %collective-permute-start.22 = (f32[72,128]{1,0:T(8,128)S(1)}, f32[72,128]{1,0:T(8,128)S(1)}, u32[]{:S(2)}, u32[]{:S(2)}) collective-permute-start(f32[72,128]{1,0:T(8,128)S(1)} %get-tuple-element.86), channel_id=1, source_target_pairs={{0,12},{4,8},{8,4},{12,0},{16,28},{20,24},{24,20},{28,16},{1,13},{... | collective-permute-start | bytes 110600 | tf_op jit(solution)/shard_map/ppermute | solution.py:400
  25.7 13.8 %collective-permute-start.23 = (f32[72,128]{1,0:T(8,128)S(1)}, f32[72,128]{1,0:T(8,128)S(1)}, u32[]{:S(2)}, u32[]{:S(2)}) collective-permute-start(f32[72,128]{1,0:T(8,128)S(1)} %get-tuple-element.87), channel_id=1, source_target_pairs={{0,16},{4,20},{8,24},{12,28},{16,0},{20,4},{24,8},{28,12},{1,17},{... | collective-permute-start | bytes 110600 | tf_op jit(solution)/shard_map/ppermute | solution.py:400
  28.7 13.4 %collective-permute-start.24 = (f32[72,128]{1,0:T(8,128)S(1)}, f32[72,128]{1,0:T(8,128)S(1)}, u32[]{:S(2)}, u32[]{:S(2)}) collective-permute-start(f32[72,128]{1,0:T(8,128)S(1)} %get-tuple-element.88), channel_id=1, source_target_pairs={{0,20},{4,16},{8,28},{12,24},{16,4},{20,0},{24,12},{28,8},{1,21},{... | collective-permute-start | bytes 110600 | tf_op jit(solution)/shard_map/ppermute | solution.py:400
  36.0 24.6 %collective-permute-start.2 = (f32[34,8,128]{2,1,0:T(8,128)S(1)}, f32[34,8,128]{2,1,0:T(8,128)S(1)}, u32[]{:S(2)}, u32[]{:S(2)}) collective-permute-start(f32[34,8,128]{2,1,0:T(8,128)S(1)} %get-tuple-element.62), channel_id=1, source_target_pairs={{0,4},{4,0},{8,12},{12,8},{16,20},{20,16},{24,28},{28,24},{1,5},{5... | collective-permute-start | bytes 417800 | tf_op jit(solution)/shard_map/ppermute | solution.py:400
  36.3 27.6 %collective-permute-start.3 = (f32[34,8,128]{2,1,0:T(8,128)S(1)}, f32[34,8,128]{2,1,0:T(8,128)S(1)}, u32[]{:S(2)}, u32[]{:S(2)}) collective-permute-start(f32[34,8,128]{2,1,0:T(8,128)S(1)} %get-tuple-element.63), channel_id=1, source_target_pairs={{0,8},{4,12},{8,0},{12,4},{16,24},{20,28},{24,16},{28,20},{1,9},{5... | collective-permute-start | bytes 417800 | tf_op jit(solution)/shard_map/ppermute | solution.py:400
  38.2 26.7 %collective-permute-start.4 = (f32[34,8,128]{2,1,0:T(8,128)S(1)}, f32[34,8,128]{2,1,0:T(8,128)S(1)}, u32[]{:S(2)}, u32[]{:S(2)}) collective-permute-start(f32[34,8,128]{2,1,0:T(8,128)S(1)} %get-tuple-element.64), channel_id=1, source_target_pairs={{0,12},{4,8},{8,4},{12,0},{16,28},{20,24},{24,20},{28,16},{1,13},{... | collective-permute-start | bytes 417800 | tf_op jit(solution)/shard_map/ppermute | solution.py:400
  39.5 26.4 %collective-permute-start.5 = (f32[34,8,128]{2,1,0:T(8,128)S(1)}, f32[34,8,128]{2,1,0:T(8,128)S(1)}, u32[]{:S(2)}, u32[]{:S(2)}) collective-permute-start(f32[34,8,128]{2,1,0:T(8,128)S(1)} %get-tuple-element.65), channel_id=1, source_target_pairs={{0,16},{4,20},{8,24},{12,28},{16,0},{20,4},{24,8},{28,12},{1,17},{... | collective-permute-start | bytes 417800 | tf_op jit(solution)/shard_map/ppermute | solution.py:400
  60.3 14.9 %collective-permute-start.6 = (f32[34,8,128]{2,1,0:T(8,128)S(1)}, f32[34,8,128]{2,1,0:T(8,128)S(1)}, u32[]{:S(2)}, u32[]{:S(2)}) collective-permute-start(f32[34,8,128]{2,1,0:T(8,128)S(1)} %get-tuple-element.66), channel_id=1, source_target_pairs={{0,20},{4,16},{8,28},{12,24},{16,4},{20,0},{24,12},{28,8},{1,21},{... | collective-permute-start | bytes 417800 | tf_op jit(solution)/shard_map/ppermute | solution.py:400
  60.6 14.6 %collective-permute-start.7 = (f32[34,8,128]{2,1,0:T(8,128)S(1)}, f32[34,8,128]{2,1,0:T(8,128)S(1)}, u32[]{:S(2)}, u32[]{:S(2)}) collective-permute-start(f32[34,8,128]{2,1,0:T(8,128)S(1)} %get-tuple-element.67), channel_id=1, source_target_pairs={{0,24},{4,28},{8,16},{12,20},{16,8},{20,12},{24,0},{28,4},{1,25},{... | collective-permute-start | bytes 417800 | tf_op jit(solution)/shard_map/ppermute | solution.py:400
  64.0 14.7 %collective-permute-start.8 = (f32[34,8,128]{2,1,0:T(8,128)S(1)}, f32[34,8,128]{2,1,0:T(8,128)S(1)}, u32[]{:S(2)}, u32[]{:S(2)}) collective-permute-start(f32[34,8,128]{2,1,0:T(8,128)S(1)} %get-tuple-element.68), channel_id=1, source_target_pairs={{0,28},{4,24},{8,20},{12,16},{16,12},{20,8},{24,4},{28,0},{1,29},{... | collective-permute-start | bytes 417800 | tf_op jit(solution)/shard_map/ppermute | solution.py:400
  64.9 21.9 %collective-permute-start.11 = (f32[34,8,128]{2,1,0:T(8,128)S(1)}, f32[34,8,128]{2,1,0:T(8,128)S(1)}, u32[]{:S(2)}, u32[]{:S(2)}) collective-permute-start(f32[34,8,128]{2,1,0:T(8,128)S(1)} %get-tuple-element.73), channel_id=1, source_target_pairs={{0,4},{4,0},{8,12},{12,8},{16,20},{20,16},{24,28},{28,24},{1,5},{5... | collective-permute-start | bytes 417800 | tf_op jit(solution)/shard_map/ppermute | solution.py:400
  65.9 23.3 %collective-permute-start.12 = (f32[34,8,128]{2,1,0:T(8,128)S(1)}, f32[34,8,128]{2,1,0:T(8,128)S(1)}, u32[]{:S(2)}, u32[]{:S(2)}) collective-permute-start(f32[34,8,128]{2,1,0:T(8,128)S(1)} %get-tuple-element.74), channel_id=1, source_target_pairs={{0,8},{4,12},{8,0},{12,4},{16,24},{20,28},{24,16},{28,20},{1,9},{5... | collective-permute-start | bytes 417800 | tf_op jit(solution)/shard_map/ppermute | solution.py:400
  75.2 15.1 %collective-permute-start.13 = (f32[34,8,128]{2,1,0:T(8,128)S(1)}, f32[34,8,128]{2,1,0:T(8,128)S(1)}, u32[]{:S(2)}, u32[]{:S(2)}) collective-permute-start(f32[34,8,128]{2,1,0:T(8,128)S(1)} %get-tuple-element.75), channel_id=1, source_target_pairs={{0,12},{4,8},{8,4},{12,0},{16,28},{20,24},{24,20},{28,16},{1,13},{... | collective-permute-start | bytes 417800 | tf_op jit(solution)/shard_map/ppermute | solution.py:400
  75.2 15.1 %collective-permute-start.14 = (f32[34,8,128]{2,1,0:T(8,128)S(1)}, f32[34,8,128]{2,1,0:T(8,128)S(1)}, u32[]{:S(2)}, u32[]{:S(2)}) collective-permute-start(f32[34,8,128]{2,1,0:T(8,128)S(1)} %get-tuple-element.76), channel_id=1, source_target_pairs={{0,16},{4,20},{8,24},{12,28},{16,0},{20,4},{24,8},{28,12},{1,17},{... | collective-permute-start | bytes 417800 | tf_op jit(solution)/shard_map/ppermute | solution.py:400
  78.7 21.5 %collective-permute-start.15 = (f32[34,8,128]{2,1,0:T(8,128)S(1)}, f32[34,8,128]{2,1,0:T(8,128)S(1)}, u32[]{:S(2)}, u32[]{:S(2)}) collective-permute-start(f32[34,8,128]{2,1,0:T(8,128)S(1)} %get-tuple-element.77), channel_id=1, source_target_pairs={{0,20},{4,16},{8,28},{12,24},{16,4},{20,0},{24,12},{28,8},{1,21},{... | collective-permute-start | bytes 417800 | tf_op jit(solution)/shard_map/ppermute | solution.py:400
  86.8 13.4 %collective-permute-start.16 = (f32[34,8,128]{2,1,0:T(8,128)S(1)}, f32[34,8,128]{2,1,0:T(8,128)S(1)}, u32[]{:S(2)}, u32[]{:S(2)}) collective-permute-start(f32[34,8,128]{2,1,0:T(8,128)S(1)} %get-tuple-element.78), channel_id=1, source_target_pairs={{0,24},{4,28},{8,16},{12,20},{16,8},{20,12},{24,0},{28,4},{1,25},{... | collective-permute-start | bytes 417800 | tf_op jit(solution)/shard_map/ppermute | solution.py:400
  101.7 13.1 %collective-permute-start.34 = (f32[312,128]{1,0:T(8,128)S(1)}, f32[312,128]{1,0:T(8,128)S(1)}, u32[]{:S(2)}, u32[]{:S(2)}) collective-permute-start(f32[312,128]{1,0:T(8,128)S(1)} %get-tuple-element.100), channel_id=1, source_target_pairs={{0,4},{4,0},{8,12},{12,8},{16,20},{20,16},{24,28},{28,24},{1,5},{5... | collective-permute-start | bytes 479240 | tf_op jit(solution)/shard_map/ppermute | solution.py:400
  103.3 12.7 %collective-permute-start.35 = (f32[312,128]{1,0:T(8,128)S(1)}, f32[312,128]{1,0:T(8,128)S(1)}, u32[]{:S(2)}, u32[]{:S(2)}) collective-permute-start(f32[312,128]{1,0:T(8,128)S(1)} %get-tuple-element.101), channel_id=1, source_target_pairs={{0,8},{4,12},{8,0},{12,4},{16,24},{20,28},{24,16},{28,20},{1,9},{5... | collective-permute-start | bytes 479240 | tf_op jit(solution)/shard_map/ppermute | solution.py:400
  111.8 14.8 %collective-permute-start.29 = (f32[312,128]{1,0:T(8,128)S(1)}, f32[312,128]{1,0:T(8,128)S(1)}, u32[]{:S(2)}, u32[]{:S(2)}) collective-permute-start(f32[312,128]{1,0:T(8,128)S(1)} %get-tuple-element.94), channel_id=1, source_target_pairs={{0,12},{4,8},{8,4},{12,0},{16,28},{20,24},{24,20},{28,16},{1,13},{... | collective-permute-start | bytes 479240 | tf_op jit(solution)/shard_map/ppermute | solution.py:400
  114.8 21.6 %collective-permute-start.30 = (f32[312,128]{1,0:T(8,128)S(1)}, f32[312,128]{1,0:T(8,128)S(1)}, u32[]{:S(2)}, u32[]{:S(2)}) collective-permute-start(f32[312,128]{1,0:T(8,128)S(1)} %get-tuple-element.95), channel_id=1, source_target_pairs={{0,16},{4,20},{8,24},{12,28},{16,0},{20,4},{24,8},{28,12},{1,17},{... | collective-permute-start | bytes 479240 | tf_op jit(solution)/shard_map/ppermute | solution.py:400
  116.0 25.0 %collective-permute-start.31 = (f32[312,128]{1,0:T(8,128)S(1)}, f32[312,128]{1,0:T(8,128)S(1)}, u32[]{:S(2)}, u32[]{:S(2)}) collective-permute-start(f32[312,128]{1,0:T(8,128)S(1)} %get-tuple-element.96), channel_id=1, source_target_pairs={{0,20},{4,16},{8,28},{12,24},{16,4},{20,0},{24,12},{28,8},{1,21},{... | collective-permute-start | bytes 479240 | tf_op jit(solution)/shard_map/ppermute | solution.py:400
  117.6 23.4 %collective-permute-start.32 = (f32[312,128]{1,0:T(8,128)S(1)}, f32[312,128]{1,0:T(8,128)S(1)}, u32[]{:S(2)}, u32[]{:S(2)}) collective-permute-start(f32[312,128]{1,0:T(8,128)S(1)} %get-tuple-element.97), channel_id=1, source_target_pairs={{0,24},{4,28},{8,16},{12,20},{16,8},{20,12},{24,0},{28,4},{1,25},{... | collective-permute-start | bytes 479240 | tf_op jit(solution)/shard_map/ppermute | solution.py:400
  123.5 27.1 %collective-permute-start.33 = (f32[312,128]{1,0:T(8,128)S(1)}, f32[312,128]{1,0:T(8,128)S(1)}, u32[]{:S(2)}, u32[]{:S(2)}) collective-permute-start(f32[312,128]{1,0:T(8,128)S(1)} %get-tuple-element.98), channel_id=1, source_target_pairs={{0,28},{4,24},{8,20},{12,16},{16,12},{20,8},{24,4},{28,0},{1,29},{... | collective-permute-start | bytes 479240 | tf_op jit(solution)/shard_map/ppermute | solution.py:400
  126.5 27.0 %collective-permute-start.36 = (f32[312,128]{1,0:T(8,128)S(1)}, f32[312,128]{1,0:T(8,128)S(1)}, u32[]{:S(2)}, u32[]{:S(2)}) collective-permute-start(f32[312,128]{1,0:T(8,128)S(1)} %get-tuple-element.102), channel_id=1, source_target_pairs={{0,12},{4,8},{8,4},{12,0},{16,28},{20,24},{24,20},{28,16},{1,13},{... | collective-permute-start | bytes 479240 | tf_op jit(solution)/shard_map/ppermute | solution.py:400
  136.4 27.4 %collective-permute-start.37 = (f32[312,128]{1,0:T(8,128)S(1)}, f32[312,128]{1,0:T(8,128)S(1)}, u32[]{:S(2)}, u32[]{:S(2)}) collective-permute-start(f32[312,128]{1,0:T(8,128)S(1)} %get-tuple-element.103), channel_id=1, source_target_pairs={{0,16},{4,20},{8,24},{12,28},{16,0},{20,4},{24,8},{28,12},{1,17},{... | collective-permute-start | bytes 479240 | tf_op jit(solution)/shard_map/ppermute | solution.py:400
  141.0 26.1 %collective-permute-start.38 = (f32[312,128]{1,0:T(8,128)S(1)}, f32[312,128]{1,0:T(8,128)S(1)}, u32[]{:S(2)}, u32[]{:S(2)}) collective-permute-start(f32[312,128]{1,0:T(8,128)S(1)} %get-tuple-element.104), channel_id=1, source_target_pairs={{0,20},{4,16},{8,28},{12,24},{16,4},{20,0},{24,12},{28,8},{1,21},{... | collective-permute-start | bytes 479240 | tf_op jit(solution)/shard_map/ppermute | solution.py:400
  141.0 26.1 %collective-permute-start.39 = (f32[312,128]{1,0:T(8,128)S(1)}, f32[312,128]{1,0:T(8,128)S(1)}, u32[]{:S(2)}, u32[]{:S(2)}) collective-permute-start(f32[312,128]{1,0:T(8,128)S(1)} %get-tuple-element.105), channel_id=1, source_target_pairs={{0,24},{4,28},{8,16},{12,20},{16,8},{20,12},{24,0},{28,4},{1,25},{... | collective-permute-start | bytes 479240 | tf_op jit(solution)/shard_map/ppermute | solution.py:400
  150.6 16.5 %collective-permute-start.40 = (f32[312,128]{1,0:T(8,128)S(1)}, f32[312,128]{1,0:T(8,128)S(1)}, u32[]{:S(2)}, u32[]{:S(2)}) collective-permute-start(f32[312,128]{1,0:T(8,128)S(1)} %get-tuple-element.106), channel_id=1, source_target_pairs={{0,28},{4,24},{8,20},{12,16},{16,12},{20,8},{24,4},{28,0},{1,29},{... | collective-permute-start | bytes 479240 | tf_op jit(solution)/shard_map/ppermute | solution.py:400
  (15 other events, 192.8 us)

commit v2 on v1

--- a/solution.py
+++ b/solution.py
@@ -13,7 +13,6 @@
 SUBS = 8
 UNROLLS = (4, 2)
 DEAL = 4
-TOGETHER_CHUNKS = ()
 
 VMEM = pl.BlockSpec(memory_space=pltpu.VMEM)
 ANY = pl.BlockSpec(memory_space=pl.ANY)
@@ -135,14 +134,15 @@
                 outer_ref[c, row, tile] = all_ref[c, outer_row + row, tile]
 
 
-def diffuse_kernel(plan, count, at, together, x_ref, inner_ref, outer_ref, kappa_ref, *refs):
-    out_refs, (a_ref, b_ref) = refs[:-2], refs[-2:]
-    me = lax.axis_index("lev")
+def diffuse(plan, at, chunk, kappa_ref, x_ref, inner_ref, outer_ref, a_ref, b_ref):
     tile_index = lax.axis_index("tile")
     height = plan.rows + 2 * plan.halo
     lane = lane_ids()
     at_start, at_end = lane == 0, lane == LANES - 1
-    kappa = kappa_ref[...]
+    level = lax.broadcasted_iota(jnp.int32, (SUBS, LANES), 0)
+    kappa = jnp.full((SUBS, LANES), 0.125, jnp.float32)
+    for i in range(chunk[1]):
+        kappa = jnp.where(level == i, kappa_ref[chunk[0] + i], kappa)
     ratio = (1.0 - 4.0 * kappa) / kappa
     kept = {
         plan.halo - 1: jnp.where(tile_index == 0, 0.0, 1.0),
@@ -211,35 +211,49 @@
 
     lax.fori_loop(0, plan.rows // unroll, undo, 0)
 
-    for d in range(plan.group):
-        out_ref = out_refs[0].at[d] if together else out_refs[d]
-        base = (d if together else me ^ d) * plan.rows_each
-
-        def put(unit, value):
-            if count == SUBS:
-                out_ref[unit] = value
-            else:
-                out_ref[unit * count : (unit + 1) * count] = value[:count]
-
-        for i in range(plan.rows_each):
-            for tile in range(plan.full):
-                put(i * plan.full + tile, b_ref[base + i, tile])
-        for m in range(plan.merged):
-            value = None
-            for k in range(plan.per_merged):
-                i = m * plan.per_merged + k
-                if i < plan.rows_each:
-                    piece = b_ref[base + i, plan.full]
-                    if k == 0:
-                        value = piece
-                    else:
-                        value = jnp.where(
-                            lane < k * plan.rest, value, pltpu.roll(piece, k * plan.rest, 1)
-                        )
-            put(plan.rows_each * plan.full + m, value)
-
-
-def operator_kernel(plan, together, correlation_ref, balance_ref, high_ref, low_ref):
+
+def block_rows(parts, units):
+    first = [0]
+    for count in parts:
+        first.append(first[-1] + up_to(units * count, SUBS))
+    return first
+
+
+def diffuse_kernel(plan, chunks, splits, *refs):
+    parts = [count for _, count in chunks]
+    given, out_refs, (a_ref, b_ref) = refs[:4], refs[4:-2], refs[-2:]
+    me = lax.axis_index("lev")
+    lane = lane_ids()
+    for p, count in enumerate(parts):
+        diffuse(plan, p, chunks[p], *given, a_ref, b_ref)
+        for d in range(plan.group):
+            base = (me ^ d) * plan.rows_each
+
+            def put(unit, value):
+                for s, (begin, stop) in enumerate(splits):
+                    if begin <= unit < stop:
+                        row = block_rows(parts, stop - begin)[p] + (unit - begin) * count
+                        out_refs[s * plan.group + d][row : row + count] = value[:count]
+
+            for i in range(plan.rows_each):
+                for tile in range(plan.full):
+                    put(i * plan.full + tile, b_ref[base + i, tile])
+            for m in range(plan.merged):
+                value = None
+                for k in range(plan.per_merged):
+                    i = m * plan.per_merged + k
+                    if i < plan.rows_each:
+                        piece = b_ref[base + i, plan.full]
+                        if k == 0:
+                            value = piece
+                        else:
+                            value = jnp.where(
+                                lane < k * plan.rest, value, pltpu.roll(piece, k * plan.rest, 1)
+                            )
+                put(plan.rows_each * plan.full + m, value)
+
+
+def operator_kernel(plan, correlation_ref, balance_ref, high_ref, low_ref):
     group, levels = plan.group, plan.levels
     stride = up_to(levels, SUBS)
     me = lax.axis_index("lev")
@@ -263,9 +277,9 @@
 
     rows = [(d * stride, levels, (me ^ d) * levels) for d in range(group)]
     columns, place = [], 0
-    for (first, count), alike in zip(plan.chunks, together):
+    for first, count in plan.chunks:
         for d in range(group):
-            columns.append((place, count, (d if alike else me ^ d) * levels + first))
+            columns.append((place, count, (me ^ d) * levels + first))
             place += count
     left = exact(picked((group * stride, group * levels), rows), correlation_ref[...])
     right = exact(
@@ -277,24 +291,18 @@
     low_ref[...] = (operator - high.astype(jnp.float32)).astype(jnp.bfloat16)
 
 
-def mix_kernel(plan, counts, first, stop, high_ref, low_ref, *refs):
-    chunks, group, levels = plan.chunks, plan.group, plan.levels
-    held, place = [], 0
-    for given in counts:
-        refs_here = refs[place : place + given]
-        held.append([refs_here[0].at[d] for d in range(group)] if given == 1 else refs_here)
-        place += given
-    out_refs = refs[place : place + group]
+def mix_kernel(plan, sources, first, stop, high_ref, low_ref, *refs):
+    group, levels = plan.group, plan.levels
+    out_refs = refs[len(sources) * group :]
     high, low = high_ref[...], low_ref[...]
     stride = up_to(levels, SUBS)
     for unit in range(first, stop):
         pieces = []
-        for (_, count), blocks in zip(chunks, held):
-            for block in blocks:
-                if count == SUBS:
-                    pieces.append(block[unit])
-                else:
-                    pieces.append(block[unit * count : (unit + 1) * count])
+        for g, (parts, begin, end) in enumerate(sources):
+            starts = block_rows(parts, end - begin)
+            for p, count in enumerate(parts):
+                row = starts[p] + (unit - begin) * count
+                pieces += [block[row : row + count] for block in refs[g * group : (g + 1) * group]]
         column = jnp.concatenate(pieces, axis=0)
         column_high = column.astype(jnp.bfloat16)
         column_low = (column - column_high.astype(jnp.float32)).astype(jnp.bfloat16)
@@ -363,88 +371,88 @@
     def shape(*dims):
         return jax.ShapeDtypeStruct(dims, f32)
 
-    def call(kernel, outs, *args, scratch=(), flops, vmem=14 << 20):
+    def call(kernel, outs, *args, scratch=(), flops, first_spec=VMEM):
         return pl.pallas_call(
             kernel,
             out_shape=outs,
-            in_specs=[VMEM] * len(args),
+            in_specs=[first_spec] + [VMEM] * (len(args) - 1),
             out_specs=jax.tree.map(lambda _: VMEM, outs),
             scratch_shapes=list(scratch),
-            compiler_params=pltpu.CompilerParams(vmem_limit_bytes=vmem),
+            compiler_params=pltpu.CompilerParams(vmem_limit_bytes=14 << 20),
             cost_estimate=pl.CostEstimate(flops=flops, bytes_accessed=1 << 20, transcendentals=0),
         )(*args)
 
     def swap(start):
         return [(i + k, i + 1 - k) for i in range(start, tiles_around - 1, 2) for k in range(2)]
 
-    parts = [[chunk] for chunk in plan.chunks]
+    steps = [chunks for chunks in (plan.chunks[:1], plan.chunks[1:]) if chunks]
     fields = []
-    for p, chunks in enumerate(parts):
+    for g, chunks in enumerate(steps):
         field = shape(len(chunks), plan.rows, plan.tiles, SUBS, LANES)
         edge = shape(len(chunks), halo, plan.tiles, SUBS, LANES)
         field, inner, outer = call(
-            functools.partial(arrange_kernel, plan, chunks, p == 0),
+            functools.partial(arrange_kernel, plan, chunks, g == 0),
             (field, edge, edge),
-            increment[: chunks[0][1]] if p == 0 else increment,
+            increment[: chunks[0][1]] if g == 0 else increment,
             flops=10**7,
         )
         outer = lax.ppermute(outer, "tile", swap(1))
         inner = lax.ppermute(inner, "tile", swap(0))
-        fields += [(c, field, inner, outer) for c in range(len(chunks))]
+        fields.append((field, inner, outer))
 
     def exchange(blocks):
-        if not isinstance(blocks, tuple):
-            return [lax.all_to_all(blocks, "lev", 0, 0, tiled=True)]
         got = {0: blocks[0]}
-        for d in reversed(range(1, group)):
+        for d in range(1, group):
             got[d] = lax.ppermute(blocks[d], "lev", [(i, i ^ d) for i in range(group)])
         return [got[d] for d in range(group)]
 
-    together = [c in TOGETHER_CHUNKS for c in range(len(plan.chunks))]
-    held, counts = [], []
-    for c, (first, count) in enumerate(plan.chunks):
-        factor = jnp.pad(
-            kappa[first : first + count], (0, SUBS - count), constant_values=0.125
-        )
-        factor = jnp.broadcast_to(factor[:, None], (SUBS, LANES))
-        if count == SUBS:
-            block = (plan.units, SUBS, LANES)
-        else:
-            block = (up_to(plan.units * count, SUBS), LANES)
-        height = plan.rows_held + 2 * halo
+    whole = [(0, plan.units)]
+    half = plan.units // 2
+    splits = [(0, half), (half, plan.units)]
+    height = plan.rows_held + 2 * halo
+    sources = [[] for _ in splits]
+    held = [[] for _ in splits]
+    for g, chunks in enumerate(steps):
+        parts = [count for _, count in chunks]
+        cuts = splits if g else whole
+        outs = []
+        for begin, stop in cuts:
+            outs += [shape(block_rows(parts, stop - begin)[-1], LANES)] * group
         blocks = call(
-            functools.partial(diffuse_kernel, plan, count, fields[c][0], together[c]),
-            shape(group, *block) if together[c] else (shape(*block),) * group,
-            *fields[c][1:],
-            factor,
+            functools.partial(diffuse_kernel, plan, chunks, cuts),
+            tuple(outs),
+            kappa,
+            *fields[g],
             scratch=[pltpu.VMEM((height, plan.tiles, SUBS, LANES), f32)] * 2,
             flops=10**9,
+            first_spec=pl.BlockSpec(memory_space=pltpu.SMEM),
         )
-        got = exchange(blocks)
-        counts.append(len(got))
-        held += got
+        for s, (begin, stop) in enumerate(cuts):
+            got = exchange(blocks[s * group : (s + 1) * group])
+            for t in range(len(splits)):
+                if len(cuts) == 1 or s == t:
+                    sources[t].append((parts, begin, stop))
+                    held[t] += got
 
     stride = up_to(levels, SUBS)
     operator = jax.ShapeDtypeStruct((group * stride, group * levels), jnp.bfloat16)
     high, low = call(
-        functools.partial(operator_kernel, plan, together),
+        functools.partial(operator_kernel, plan),
         (operator, operator),
         correlation,
         balance,
         flops=10**8,
     )
 
-    half = plan.units // 2
-    splits = [(0, half), (half, plan.units)]
     back = []
-    for begin, stop in splits:
+    for s, (begin, stop) in enumerate(splits):
         block = shape(up_to((stop - begin) * levels, SUBS), LANES)
         blocks = call(
-            functools.partial(mix_kernel, plan, counts, begin, stop),
+            functools.partial(mix_kernel, plan, sources[s], begin, stop),
             (block,) * group,
             high,
             low,
-            *held,
+            *held[s],
             flops=10**9,
         )
         back.append(exchange(blocks))

time: 172 us -> 150 us (0.87)
  the two profiles are of different devices: /device:TPU:0 before, /device:TPU:12 now
where the time goes in v2:
time: 150 us
  starting transfers between devices  66.2 us (44%)
  waiting for transfers between devices  49.7 us (33%)
  Pallas kernels  31.5 us (21%)
  local copies, waits for them, and re-layouts  1.85 us (1%)
    ppermute x35, starting transfers between devices, exchange(): got[d] = lax.ppermute(blocks[d], 'lev', [(i, i ^ d) for i in range(group)])  60 us
    ppermute x35, waiting for transfers between devices, exchange(): got[d] = lax.ppermute(blocks[d], 'lev', [(i, i ^ d) for i in range(group)])  37.4 us
    pallas_call x9, Pallas kernels, call(): pl.pallas_call(kernel, out_shape=outs, in_specs=[first_spec] + [VMEM] * (...  31.5 us
    ppermute x2, waiting for transfers between devices, program(): outer = lax.ppermute(outer, 'tile', swap(1))  12.3 us
    ppermute x2, starting transfers between devices, program(): outer = lax.ppermute(outer, 'tile', swap(1))  5.55 us
  transfers between devices with their start and end apart: 39, of which 11 were waited for; matrix products, arithmetic and copies ran while one was open for 0% of the time, Pallas kernels for 17%

profile of v2, /device:TPU:12, one launch (start us, length us, event | category | flops | bytes accessed | tf_op | source)
XLA Modules:
  0.0 149.5 jit_solution(9108466052799571957)
XLA Ops:
  0.0 1.7 %copy-done = f32[18,24,1440]{2,1,0:T(8,128)S(1)} copy-done((f32[18,24,1440]{2,1,0:T(8,128)S(1)}, f32[18,24,1440]{2,1,0:T(8,128)}, u32[]{:S(2)}) %copy-start) | copy-done | bytes 2488344
  1.8 4.2 %shard_map.58 = (f32[2,24,12,8,128]{4,3,2,1,0:T(8,128)S(1)}, f32[2,10,12,8,128]{4,3,2,1,0:T(8,128)S(1)}, f32[2,10,12,8,128]{4,3,2,1,0:T(8,128)S(1)}) custom-call(f32[18,24,1440]{2,1,0:T(8,128)S(1)} %copy-done), custom_call_target="tpu_custom_call" | custom-call | flops 10000000 | bytes 1048576 | tf_op jit(solution)/shard_map/pallas_call | solution.py:375
  5.9 1.9 %collective-permute-start.10 = (f32[2,10,12,8,128]{4,3,2,1,0:T(8,128)S(1)}, f32[2,10,12,8,128]{4,3,2,1,0:T(8,128)S(1)}, u32[]{:S(2)}, u32[]{:S(2)}) collective-permute-start(f32[2,10,12,8,128]{4,3,2,1,0:T(8,128)S(1)} %get-tuple-element.68), channel_id=1, source_target_pairs={{1,2},{2,1},{5,6},{6,5},{9,10},{10,9},{13,14},{14,13},{17,18},{18,... | collective-permute-start | bytes 2949128 | tf_op jit(solution)/shard_map/ppermute | solution.py:399
  8.0 2.1 %shard_map.56 = (f32[1,24,12,8,128]{4,3,2,1,0:T(8,128)S(1)}, f32[1,10,12,8,128]{4,3,2,1,0:T(8,128)S(1)}, f32[1,10,12,8,128]{4,3,2,1,0:T(8,128)S(1)}) custom-call(f32[8,24,1440]{2,1,0:T(8,128)S(1)} %slice.3.x_ref), custom_call_target="tpu_custom_call" | custom-call | flops 10000000 | bytes 1048576 | tf_op jit(solution)/shard_map/pallas_call | solution.py:375
  10.7 3.6 %collective-permute-start.1 = (f32[1,10,12,8,128]{4,3,2,1,0:T(8,128)S(1)}, f32[1,10,12,8,128]{4,3,2,1,0:T(8,128)S(1)}, u32[]{:S(2)}, u32[]{:S(2)}) collective-permute-start(f32[1,10,12,8,128]{4,3,2,1,0:T(8,128)S(1)} %get-tuple-element.57), channel_id=1, source_target_pairs={{1,2},{2,1},{5,6},{6,5},{9,10},{10,9},{13,14},{14,13},{17,18},{18,... | collective-permute-start | bytes 1474568 | tf_op jit(solution)/shard_map/ppermute | solution.py:399
  14.3 12.3 %collective-permute-done.1.refs_3_ = f32[1,10,12,8,128]{4,3,2,1,0:T(8,128)S(1)} collective-permute-done((f32[1,10,12,8,128]{4,3,2,1,0:T(8,128)S(1)}, f32[1,10,12,8,128]{4,3,2,1,0:T(8,128)S(1)}, u32[]{:S(2)}, u32[]{:S(2)}) %collective-permute-start.1) | collective-permute-done | bytes 491552 | tf_op jit(solution)/shard_map/ppermute | solution.py:399
  26.6 6.5 %shard_map.57 = (f32[272,128]{1,0:T(8,128)S(1)}, f32[272,128]{1,0:T(8,128)S(1)}, f32[272,128]{1,0:T(8,128)S(1)}, f32[272,128]{1,0:T(8,128)S(1)}, f32[272,128]{1,...) custom-call(f32[18]{0:T(128)S(1)} %copy-done.2, ...), custom_call_target="tpu_custom_call" | custom-call | flops 1000000000 | bytes 1048576 | tf_op jit(solution)/shard_map/pallas_call | solution.py:375
  36.7 3.1 %collective-permute-done.2.refs_1_ = f32[272,128]{1,0:T(8,128)S(1)} collective-permute-done((f32[272,128]{1,0:T(8,128)S(1)}, f32[272,128]{1,0:T(8,128)S(1)}, u32[]{:S(2)}, u32[]{:S(2)}) %collective-permute-start.2) | collective-permute-done | bytes 139296 | tf_op jit(solution)/shard_map/ppermute | solution.py:406
  40.8 2.5 %collective-permute-start.6 = (f32[272,128]{1,0:T(8,128)S(1)}, f32[272,128]{1,0:T(8,128)S(1)}, u32[]{:S(2)}, u32[]{:S(2)}) collective-permute-start(f32[272,128]{1,0:T(8,128)S(1)} %get-tuple-element.63), channel_id=1, source_target_pairs={{0,20},{4,16},{8,28},{12,24},{16,4},{20,0},{24,12},{28,8},{1,21},{... | collective-permute-start | bytes 417800 | tf_op jit(solution)/shard_map/ppermute | solution.py:406
  43.3 1.8 %collective-permute-start.7 = (f32[272,128]{1,0:T(8,128)S(1)}, f32[272,128]{1,0:T(8,128)S(1)}, u32[]{:S(2)}, u32[]{:S(2)}) collective-permute-start(f32[272,128]{1,0:T(8,128)S(1)} %get-tuple-element.64), channel_id=1, source_target_pairs={{0,24},{4,28},{8,16},{12,20},{16,8},{20,12},{24,0},{28,4},{1,25},{... | collective-permute-start | bytes 417800 | tf_op jit(solution)/shard_map/ppermute | solution.py:406
  45.6 12.4 %shard_map.59 = (f32[176,128]{1,0:T(8,128)S(1)}, f32[176,128]{1,0:T(8,128)S(1)}, f32[176,128]{1,0:T(8,128)S(1)}, f32[176,128]{1,0:T(8,128)S(1)}, f32[176,128]{1,...) custom-call(f32[18]{0:T(128)S(1)} %copy-done.2, ...), custom_call_target="tpu_custom_call" | custom-call | flops 1000000000 | bytes 1048576 | tf_op jit(solution)/shard_map/pallas_call | solution.py:375
  59.3 2.2 %collective-permute-start.26 = (f32[176,128]{1,0:T(8,128)S(1)}, f32[176,128]{1,0:T(8,128)S(1)}, u32[]{:S(2)}, u32[]{:S(2)}) collective-permute-start(f32[176,128]{1,0:T(8,128)S(1)} %get-tuple-element.87), channel_id=1, source_target_pairs={{0,8},{4,12},{8,0},{12,4},{16,24},{20,28},{24,16},{28,20},{1,9},{5... | collective-permute-start | bytes 270344 | tf_op jit(solution)/shard_map/ppermute | solution.py:406
  61.6 2.8 %collective-permute-start.28 = (f32[176,128]{1,0:T(8,128)S(1)}, f32[176,128]{1,0:T(8,128)S(1)}, u32[]{:S(2)}, u32[]{:S(2)}) collective-permute-start(f32[176,128]{1,0:T(8,128)S(1)} %get-tuple-element.89), channel_id=1, source_target_pairs={{0,16},{4,20},{8,24},{12,28},{16,0},{20,4},{24,8},{28,12},{1,17},{... | collective-permute-start | bytes 270344 | tf_op jit(solution)/shard_map/ppermute | solution.py:406
  69.0 5.2 %collective-permute-done.28.refs_12_ = f32[176,128]{1,0:T(8,128)S(1)} collective-permute-done((f32[176,128]{1,0:T(8,128)S(1)}, f32[176,128]{1,0:T(8,128)S(1)}, u32[]{:S(2)}, u32[]{:S(2)}) %collective-permute-start.28) | collective-permute-done | bytes 90144 | tf_op jit(solution)/shard_map/ppermute | solution.py:406
  74.1 3.0 %collective-permute-start.12 = (f32[176,128]{1,0:T(8,128)S(1)}, f32[176,128]{1,0:T(8,128)S(1)}, u32[]{:S(2)}, u32[]{:S(2)}) collective-permute-start(f32[176,128]{1,0:T(8,128)S(1)} %get-tuple-element.71), channel_id=1, source_target_pairs={{0,8},{4,12},{8,0},{12,4},{16,24},{20,28},{24,16},{28,20},{1,9},{5... | collective-permute-start | bytes 270344 | tf_op jit(solution)/shard_map/ppermute | solution.py:406
  78.0 2.0 %collective-permute-start.13 = (f32[176,128]{1,0:T(8,128)S(1)}, f32[176,128]{1,0:T(8,128)S(1)}, u32[]{:S(2)}, u32[]{:S(2)}) collective-permute-start(f32[176,128]{1,0:T(8,128)S(1)} %get-tuple-element.72), channel_id=1, source_target_pairs={{0,12},{4,8},{8,4},{12,0},{16,28},{20,24},{24,20},{28,16},{1,13},{... | collective-permute-start | bytes 270344 | tf_op jit(solution)/shard_map/ppermute | solution.py:406
  80.0 1.8 %collective-permute-start.14 = (f32[176,128]{1,0:T(8,128)S(1)}, f32[176,128]{1,0:T(8,128)S(1)}, u32[]{:S(2)}, u32[]{:S(2)}) collective-permute-start(f32[176,128]{1,0:T(8,128)S(1)} %get-tuple-element.73), channel_id=1, source_target_pairs={{0,16},{4,20},{8,24},{12,28},{16,0},{20,4},{24,8},{28,12},{1,17},{... | collective-permute-start | bytes 270344 | tf_op jit(solution)/shard_map/ppermute | solution.py:406
  83.3 1.8 %collective-permute-start.16 = (f32[176,128]{1,0:T(8,128)S(1)}, f32[176,128]{1,0:T(8,128)S(1)}, u32[]{:S(2)}, u32[]{:S(2)}) collective-permute-start(f32[176,128]{1,0:T(8,128)S(1)} %get-tuple-element.75), channel_id=1, source_target_pairs={{0,24},{4,28},{8,16},{12,20},{16,8},{20,12},{24,0},{28,4},{1,25},{... | collective-permute-start | bytes 270344 | tf_op jit(solution)/shard_map/ppermute | solution.py:406
  88.4 2.4 %collective-permute-start.33 = (f32[312,128]{1,0:T(8,128)S(1)}, f32[312,128]{1,0:T(8,128)S(1)}, u32[]{:S(2)}, u32[]{:S(2)}) collective-permute-start(f32[312,128]{1,0:T(8,128)S(1)} %get-tuple-element.95), channel_id=1, source_target_pairs={{0,8},{4,12},{8,0},{12,4},{16,24},{20,28},{24,16},{28,20},{1,9},{5... | collective-permute-start | bytes 479240 | tf_op jit(solution)/shard_map/ppermute | solution.py:406
  90.8 5.2 %collective-permute-done.16.refs_14_ = f32[176,128]{1,0:T(8,128)S(1)} collective-permute-done((f32[176,128]{1,0:T(8,128)S(1)}, f32[176,128]{1,0:T(8,128)S(1)}, u32[]{:S(2)}, u32[]{:S(2)}) %collective-permute-start.16) | collective-permute-done | bytes 90144 | tf_op jit(solution)/shard_map/ppermute | solution.py:406
  96.0 5.2 %collective-permute-done.17.refs_15_ = f32[176,128]{1,0:T(8,128)S(1)} collective-permute-done((f32[176,128]{1,0:T(8,128)S(1)}, f32[176,128]{1,0:T(8,128)S(1)}, u32[]{:S(2)}, u32[]{:S(2)}) %collective-permute-start.17) | collective-permute-done | bytes 90144 | tf_op jit(solution)/shard_map/ppermute | solution.py:406
  102.7 2.9 %collective-permute-start.18 = (f32[312,128]{1,0:T(8,128)S(1)}, f32[312,128]{1,0:T(8,128)S(1)}, u32[]{:S(2)}, u32[]{:S(2)}) collective-permute-start(f32[312,128]{1,0:T(8,128)S(1)} %get-tuple-element.78), channel_id=1, source_target_pairs={{0,4},{4,0},{8,12},{12,8},{16,20},{20,16},{24,28},{28,24},{1,5},{5... | collective-permute-start | bytes 479240 | tf_op jit(solution)/shard_map/ppermute | solution.py:406
  107.8 3.7 %collective-permute-start.22 = (f32[312,128]{1,0:T(8,128)S(1)}, f32[312,128]{1,0:T(8,128)S(1)}, u32[]{:S(2)}, u32[]{:S(2)}) collective-permute-start(f32[312,128]{1,0:T(8,128)S(1)} %get-tuple-element.82), channel_id=1, source_target_pairs={{0,20},{4,16},{8,28},{12,24},{16,4},{20,0},{24,12},{28,8},{1,21},{... | collective-permute-start | bytes 479240 | tf_op jit(solution)/shard_map/ppermute | solution.py:406
  113.9 2.2 %collective-permute-done.20.refs_3_ = f32[312,128]{1,0:T(8,128)S(1)} collective-permute-done((f32[312,128]{1,0:T(8,128)S(1)}, f32[312,128]{1,0:T(8,128)S(1)}, u32[]{:S(2)}, u32[]{:S(2)}) %collective-permute-start.20) | collective-permute-done | bytes 159776 | tf_op jit(solution)/shard_map/ppermute | solution.py:406
  116.2 3.4 %collective-permute-start.34 = (f32[312,128]{1,0:T(8,128)S(1)}, f32[312,128]{1,0:T(8,128)S(1)}, u32[]{:S(2)}, u32[]{:S(2)}) collective-permute-start(f32[312,128]{1,0:T(8,128)S(1)} %get-tuple-element.96), channel_id=1, source_target_pairs={{0,12},{4,8},{8,4},{12,0},{16,28},{20,24},{24,20},{28,16},{1,13},{... | collective-permute-start | bytes 479240 | tf_op jit(solution)/shard_map/ppermute | solution.py:406
  119.6 5.2 %collective-permute-start.35 = (f32[312,128]{1,0:T(8,128)S(1)}, f32[312,128]{1,0:T(8,128)S(1)}, u32[]{:S(2)}, u32[]{:S(2)}) collective-permute-start(f32[312,128]{1,0:T(8,128)S(1)} %get-tuple-element.97), channel_id=1, source_target_pairs={{0,16},{4,20},{8,24},{12,28},{16,0},{20,4},{24,8},{28,12},{1,17},{... | collective-permute-start | bytes 479240 | tf_op jit(solution)/shard_map/ppermute | solution.py:406
  124.7 4.3 %collective-permute-start.36 = (f32[312,128]{1,0:T(8,128)S(1)}, f32[312,128]{1,0:T(8,128)S(1)}, u32[]{:S(2)}, u32[]{:S(2)}) collective-permute-start(f32[312,128]{1,0:T(8,128)S(1)} %get-tuple-element.98), channel_id=1, source_target_pairs={{0,20},{4,16},{8,28},{12,24},{16,4},{20,0},{24,12},{28,8},{1,21},{... | collective-permute-start | bytes 479240 | tf_op jit(solution)/shard_map/ppermute | solution.py:406
  129.1 7.6 %collective-permute-done.23.refs_6_ = f32[312,128]{1,0:T(8,128)S(1)} collective-permute-done((f32[312,128]{1,0:T(8,128)S(1)}, f32[312,128]{1,0:T(8,128)S(1)}, u32[]{:S(2)}, u32[]{:S(2)}) %collective-permute-start.23) | collective-permute-done | bytes 159776 | tf_op jit(solution)/shard_map/ppermute | solution.py:406
  136.7 3.7 %collective-permute-done.24.refs_7_ = f32[312,128]{1,0:T(8,128)S(1)} collective-permute-done((f32[312,128]{1,0:T(8,128)S(1)}, f32[312,128]{1,0:T(8,128)S(1)}, u32[]{:S(2)}, u32[]{:S(2)}) %collective-permute-start.24) | collective-permute-done | bytes 159776 | tf_op jit(solution)/shard_map/ppermute | solution.py:406
  142.2 3.2 %collective-permute-done.37.refs_6_ = f32[312,128]{1,0:T(8,128)S(1)} collective-permute-done((f32[312,128]{1,0:T(8,128)S(1)}, f32[312,128]{1,0:T(8,128)S(1)}, u32[]{:S(2)}, u32[]{:S(2)}) %collective-permute-start.37) | collective-permute-done | bytes 159776 | tf_op jit(solution)/shard_map/ppermute | solution.py:406
  145.4 1.8 %collective-permute-done.38.refs_7_ = f32[312,128]{1,0:T(8,128)S(1)} collective-permute-done((f32[312,128]{1,0:T(8,128)S(1)}, f32[312,128]{1,0:T(8,128)S(1)}, u32[]{:S(2)}, u32[]{:S(2)}) %collective-permute-start.38) | collective-permute-done | bytes 159776 | tf_op jit(solution)/shard_map/ppermute | solution.py:406
  147.2 2.3 %shard_map.63 = f32[18,24,1440]{2,1,0:T(8,128)} custom-call(s32[24,1440]{1,0:T(8,128)S(1)} %copy-done.1, f32[12,432,128]{2,1,0:T(8,128)S(1)} %shard_map.61.held_ref, f32[312,128]{1,0:T(8,128)S(1)} %get-tuple-element.93.refs_0_, f32[312,128]{1,0:T(8,128)S(1)} %collective-permute-done.32.refs_1_, f32[312,128]{1,0:T(8,128)S(1)} %collective-permute-done.33.refs_2_, ...), custom_call_target="tpu_custom_call" | custom-call | flops 10000000 | bytes 1048576 | tf_op jit(solution)/shard_map/pallas_call | solution.py:375
  (66 shorter events, 25.2 us)
Async XLA Ops:
  5.9 37.4 %collective-permute-start.10 = (f32[2,10,12,8,128]{4,3,2,1,0:T(8,128)S(1)}, f32[2,10,12,8,128]{4,3,2,1,0:T(8,128)S(1)}, u32[]{:S(2)}, u32[]{:S(2)}) collective-permute-start(f32[2,10,12,8,128]{4,3,2,1,0:T(8,128)S(1)} %get-tuple-element.68), channel_id=1, source_target_pairs={{1,2},{2,1},{5,6},{6,5},{9,10},{10,9},{13,14},{14,13},{17,18},{18,... | collective-permute-start | bytes 2949128 | tf_op jit(solution)/shard_map/ppermute | solution.py:399
  7.9 37.3 %collective-permute-start.9 = (f32[2,10,12,8,128]{4,3,2,1,0:T(8,128)S(1)}, f32[2,10,12,8,128]{4,3,2,1,0:T(8,128)S(1)}, u32[]{:S(2)}, u32[]{:S(2)}) collective-permute-start(f32[2,10,12,8,128]{4,3,2,1,0:T(8,128)S(1)} %get-tuple-element.67), channel_id=1, source_target_pairs={{0,1},{1,0},{2,3},{3,2},{4,5},{5,4},{6,7},{7,6},{8,9},{9,8},{10,11... | collective-permute-start | bytes 2949128 | tf_op jit(solution)/shard_map/ppermute | solution.py:400
  10.7 15.9 %collective-permute-start.1 = (f32[1,10,12,8,128]{4,3,2,1,0:T(8,128)S(1)}, f32[1,10,12,8,128]{4,3,2,1,0:T(8,128)S(1)}, u32[]{:S(2)}, u32[]{:S(2)}) collective-permute-start(f32[1,10,12,8,128]{4,3,2,1,0:T(8,128)S(1)} %get-tuple-element.57), channel_id=1, source_target_pairs={{1,2},{2,1},{5,6},{6,5},{9,10},{10,9},{13,14},{14,13},{17,18},{18,... | collective-permute-start | bytes 1474568 | tf_op jit(solution)/shard_map/ppermute | solution.py:399
  35.1 22.9 %collective-permute-start.4 = (f32[272,128]{1,0:T(8,128)S(1)}, f32[272,128]{1,0:T(8,128)S(1)}, u32[]{:S(2)}, u32[]{:S(2)}) collective-permute-start(f32[272,128]{1,0:T(8,128)S(1)} %get-tuple-element.61), channel_id=1, source_target_pairs={{0,12},{4,8},{8,4},{12,0},{16,28},{20,24},{24,20},{28,16},{1,13},{... | collective-permute-start | bytes 417800 | tf_op jit(solution)/shard_map/ppermute | solution.py:406
  39.7 19.6 %collective-permute-start.5 = (f32[272,128]{1,0:T(8,128)S(1)}, f32[272,128]{1,0:T(8,128)S(1)}, u32[]{:S(2)}, u32[]{:S(2)}) collective-permute-start(f32[272,128]{1,0:T(8,128)S(1)} %get-tuple-element.62), channel_id=1, source_target_pairs={{0,16},{4,20},{8,24},{12,28},{16,0},{20,4},{24,8},{28,12},{1,17},{... | collective-permute-start | bytes 417800 | tf_op jit(solution)/shard_map/ppermute | solution.py:406
  40.8 20.7 %collective-permute-start.6 = (f32[272,128]{1,0:T(8,128)S(1)}, f32[272,128]{1,0:T(8,128)S(1)}, u32[]{:S(2)}, u32[]{:S(2)}) collective-permute-start(f32[272,128]{1,0:T(8,128)S(1)} %get-tuple-element.63), channel_id=1, source_target_pairs={{0,20},{4,16},{8,28},{12,24},{16,4},{20,0},{24,12},{28,8},{1,21},{... | collective-permute-start | bytes 417800 | tf_op jit(solution)/shard_map/ppermute | solution.py:406
  43.3 18.3 %collective-permute-start.7 = (f32[272,128]{1,0:T(8,128)S(1)}, f32[272,128]{1,0:T(8,128)S(1)}, u32[]{:S(2)}, u32[]{:S(2)}) collective-permute-start(f32[272,128]{1,0:T(8,128)S(1)} %get-tuple-element.64), channel_id=1, source_target_pairs={{0,24},{4,28},{8,16},{12,20},{16,8},{20,12},{24,0},{28,4},{1,25},{... | collective-permute-start | bytes 417800 | tf_op jit(solution)/shard_map/ppermute | solution.py:406
  45.2 19.3 %collective-permute-start.8 = (f32[272,128]{1,0:T(8,128)S(1)}, f32[272,128]{1,0:T(8,128)S(1)}, u32[]{:S(2)}, u32[]{:S(2)}) collective-permute-start(f32[272,128]{1,0:T(8,128)S(1)} %get-tuple-element.65), channel_id=1, source_target_pairs={{0,28},{4,24},{8,20},{12,16},{16,12},{20,8},{24,4},{28,0},{1,29},{... | collective-permute-start | bytes 417800 | tf_op jit(solution)/shard_map/ppermute | solution.py:406
  59.3 7.7 %collective-permute-start.26 = (f32[176,128]{1,0:T(8,128)S(1)}, f32[176,128]{1,0:T(8,128)S(1)}, u32[]{:S(2)}, u32[]{:S(2)}) collective-permute-start(f32[176,128]{1,0:T(8,128)S(1)} %get-tuple-element.87), channel_id=1, source_target_pairs={{0,8},{4,12},{8,0},{12,4},{16,24},{20,28},{24,16},{28,20},{1,9},{5... | collective-permute-start | bytes 270344 | tf_op jit(solution)/shard_map/ppermute | solution.py:406
  61.6 12.5 %collective-permute-start.28 = (f32[176,128]{1,0:T(8,128)S(1)}, f32[176,128]{1,0:T(8,128)S(1)}, u32[]{:S(2)}, u32[]{:S(2)}) collective-permute-start(f32[176,128]{1,0:T(8,128)S(1)} %get-tuple-element.89), channel_id=1, source_target_pairs={{0,16},{4,20},{8,24},{12,28},{16,0},{20,4},{24,8},{28,12},{1,17},{... | collective-permute-start | bytes 270344 | tf_op jit(solution)/shard_map/ppermute | solution.py:406
  64.5 13.5 %collective-permute-start.29 = (f32[176,128]{1,0:T(8,128)S(1)}, f32[176,128]{1,0:T(8,128)S(1)}, u32[]{:S(2)}, u32[]{:S(2)}) collective-permute-start(f32[176,128]{1,0:T(8,128)S(1)} %get-tuple-element.90), channel_id=1, source_target_pairs={{0,20},{4,16},{8,28},{12,24},{16,4},{20,0},{24,12},{28,8},{1,21},{... | collective-permute-start | bytes 270344 | tf_op jit(solution)/shard_map/ppermute | solution.py:406
  65.5 14.5 %collective-permute-start.30 = (f32[176,128]{1,0:T(8,128)S(1)}, f32[176,128]{1,0:T(8,128)S(1)}, u32[]{:S(2)}, u32[]{:S(2)}) collective-permute-start(f32[176,128]{1,0:T(8,128)S(1)} %get-tuple-element.91), channel_id=1, source_target_pairs={{0,24},{4,28},{8,16},{12,20},{16,8},{20,12},{24,0},{28,4},{1,25},{... | collective-permute-start | bytes 270344 | tf_op jit(solution)/shard_map/ppermute | solution.py:406
  67.0 14.8 %collective-permute-start.31 = (f32[176,128]{1,0:T(8,128)S(1)}, f32[176,128]{1,0:T(8,128)S(1)}, u32[]{:S(2)}, u32[]{:S(2)}) collective-permute-start(f32[176,128]{1,0:T(8,128)S(1)} %get-tuple-element.92), channel_id=1, source_target_pairs={{0,28},{4,24},{8,20},{12,16},{16,12},{20,8},{24,4},{28,0},{1,29},{... | collective-permute-start | bytes 270344 | tf_op jit(solution)/shard_map/ppermute | solution.py:406
  67.8 15.6 %collective-permute-start.11 = (f32[176,128]{1,0:T(8,128)S(1)}, f32[176,128]{1,0:T(8,128)S(1)}, u32[]{:S(2)}, u32[]{:S(2)}) collective-permute-start(f32[176,128]{1,0:T(8,128)S(1)} %get-tuple-element.70), channel_id=1, source_target_pairs={{0,4},{4,0},{8,12},{12,8},{16,20},{20,16},{24,28},{28,24},{1,5},{5... | collective-permute-start | bytes 270344 | tf_op jit(solution)/shard_map/ppermute | solution.py:406
  74.1 11.1 %collective-permute-start.12 = (f32[176,128]{1,0:T(8,128)S(1)}, f32[176,128]{1,0:T(8,128)S(1)}, u32[]{:S(2)}, u32[]{:S(2)}) collective-permute-start(f32[176,128]{1,0:T(8,128)S(1)} %get-tuple-element.71), channel_id=1, source_target_pairs={{0,8},{4,12},{8,0},{12,4},{16,24},{20,28},{24,16},{28,20},{1,9},{5... | collective-permute-start | bytes 270344 | tf_op jit(solution)/shard_map/ppermute | solution.py:406
  78.0 9.3 %collective-permute-start.13 = (f32[176,128]{1,0:T(8,128)S(1)}, f32[176,128]{1,0:T(8,128)S(1)}, u32[]{:S(2)}, u32[]{:S(2)}) collective-permute-start(f32[176,128]{1,0:T(8,128)S(1)} %get-tuple-element.72), channel_id=1, source_target_pairs={{0,12},{4,8},{8,4},{12,0},{16,28},{20,24},{24,20},{28,16},{1,13},{... | collective-permute-start | bytes 270344 | tf_op jit(solution)/shard_map/ppermute | solution.py:406
  80.0 8.4 %collective-permute-start.14 = (f32[176,128]{1,0:T(8,128)S(1)}, f32[176,128]{1,0:T(8,128)S(1)}, u32[]{:S(2)}, u32[]{:S(2)}) collective-permute-start(f32[176,128]{1,0:T(8,128)S(1)} %get-tuple-element.73), channel_id=1, source_target_pairs={{0,16},{4,20},{8,24},{12,28},{16,0},{20,4},{24,8},{28,12},{1,17},{... | collective-permute-start | bytes 270344 | tf_op jit(solution)/shard_map/ppermute | solution.py:406
  81.8 9.0 %collective-permute-start.15 = (f32[176,128]{1,0:T(8,128)S(1)}, f32[176,128]{1,0:T(8,128)S(1)}, u32[]{:S(2)}, u32[]{:S(2)}) collective-permute-start(f32[176,128]{1,0:T(8,128)S(1)} %get-tuple-element.74), channel_id=1, source_target_pairs={{0,20},{4,16},{8,28},{12,24},{16,4},{20,0},{24,12},{28,8},{1,21},{... | collective-permute-start | bytes 270344 | tf_op jit(solution)/shard_map/ppermute | solution.py:406
  83.3 12.7 %collective-permute-start.16 = (f32[176,128]{1,0:T(8,128)S(1)}, f32[176,128]{1,0:T(8,128)S(1)}, u32[]{:S(2)}, u32[]{:S(2)}) collective-permute-start(f32[176,128]{1,0:T(8,128)S(1)} %get-tuple-element.75), channel_id=1, source_target_pairs={{0,24},{4,28},{8,16},{12,20},{16,8},{20,12},{24,0},{28,4},{1,25},{... | collective-permute-start | bytes 270344 | tf_op jit(solution)/shard_map/ppermute | solution.py:406
  85.2 16.0 %collective-permute-start.17 = (f32[176,128]{1,0:T(8,128)S(1)}, f32[176,128]{1,0:T(8,128)S(1)}, u32[]{:S(2)}, u32[]{:S(2)}) collective-permute-start(f32[176,128]{1,0:T(8,128)S(1)} %get-tuple-element.76), channel_id=1, source_target_pairs={{0,28},{4,24},{8,20},{12,16},{16,12},{20,8},{24,4},{28,0},{1,29},{... | collective-permute-start | bytes 270344 | tf_op jit(solution)/shard_map/ppermute | solution.py:406
  87.3 19.8 %collective-permute-start.32 = (f32[312,128]{1,0:T(8,128)S(1)}, f32[312,128]{1,0:T(8,128)S(1)}, u32[]{:S(2)}, u32[]{:S(2)}) collective-permute-start(f32[312,128]{1,0:T(8,128)S(1)} %get-tuple-element.94), channel_id=1, source_target_pairs={{0,4},{4,0},{8,12},{12,8},{16,20},{20,16},{24,28},{28,24},{1,5},{5... | collective-permute-start | bytes 479240 | tf_op jit(solution)/shard_map/ppermute | solution.py:406
  88.4 19.4 %collective-permute-start.33 = (f32[312,128]{1,0:T(8,128)S(1)}, f32[312,128]{1,0:T(8,128)S(1)}, u32[]{:S(2)}, u32[]{:S(2)}) collective-permute-start(f32[312,128]{1,0:T(8,128)S(1)} %get-tuple-element.95), channel_id=1, source_target_pairs={{0,8},{4,12},{8,0},{12,4},{16,24},{20,28},{24,16},{28,20},{1,9},{5... | collective-permute-start | bytes 479240 | tf_op jit(solution)/shard_map/ppermute | solution.py:406
  102.7 8.7 %collective-permute-start.18 = (f32[312,128]{1,0:T(8,128)S(1)}, f32[312,128]{1,0:T(8,128)S(1)}, u32[]{:S(2)}, u32[]{:S(2)}) collective-permute-start(f32[312,128]{1,0:T(8,128)S(1)} %get-tuple-element.78), channel_id=1, source_target_pairs={{0,4},{4,0},{8,12},{12,8},{16,20},{20,16},{24,28},{28,24},{1,5},{5... | collective-permute-start | bytes 479240 | tf_op jit(solution)/shard_map/ppermute | solution.py:406
  105.6 10.6 %collective-permute-start.20 = (f32[312,128]{1,0:T(8,128)S(1)}, f32[312,128]{1,0:T(8,128)S(1)}, u32[]{:S(2)}, u32[]{:S(2)}) collective-permute-start(f32[312,128]{1,0:T(8,128)S(1)} %get-tuple-element.80), channel_id=1, source_target_pairs={{0,12},{4,8},{8,4},{12,0},{16,28},{20,24},{24,20},{28,16},{1,13},{... | collective-permute-start | bytes 479240 | tf_op jit(solution)/shard_map/ppermute | solution.py:406
  107.1 12.4 %collective-permute-start.21 = (f32[312,128]{1,0:T(8,128)S(1)}, f32[312,128]{1,0:T(8,128)S(1)}, u32[]{:S(2)}, u32[]{:S(2)}) collective-permute-start(f32[312,128]{1,0:T(8,128)S(1)} %get-tuple-element.81), channel_id=1, source_target_pairs={{0,16},{4,20},{8,24},{12,28},{16,0},{20,4},{24,8},{28,12},{1,17},{... | collective-permute-start | bytes 479240 | tf_op jit(solution)/shard_map/ppermute | solution.py:406
  107.8 17.0 %collective-permute-start.22 = (f32[312,128]{1,0:T(8,128)S(1)}, f32[312,128]{1,0:T(8,128)S(1)}, u32[]{:S(2)}, u32[]{:S(2)}) collective-permute-start(f32[312,128]{1,0:T(8,128)S(1)} %get-tuple-element.82), channel_id=1, source_target_pairs={{0,20},{4,16},{8,28},{12,24},{16,4},{20,0},{24,12},{28,8},{1,21},{... | collective-permute-start | bytes 479240 | tf_op jit(solution)/shard_map/ppermute | solution.py:406
  111.5 25.2 %collective-permute-start.23 = (f32[312,128]{1,0:T(8,128)S(1)}, f32[312,128]{1,0:T(8,128)S(1)}, u32[]{:S(2)}, u32[]{:S(2)}) collective-permute-start(f32[312,128]{1,0:T(8,128)S(1)} %get-tuple-element.83), channel_id=1, source_target_pairs={{0,24},{4,28},{8,16},{12,20},{16,8},{20,12},{24,0},{28,4},{1,25},{... | collective-permute-start | bytes 479240 | tf_op jit(solution)/shard_map/ppermute | solution.py:406
  112.6 27.8 %collective-permute-start.24 = (f32[312,128]{1,0:T(8,128)S(1)}, f32[312,128]{1,0:T(8,128)S(1)}, u32[]{:S(2)}, u32[]{:S(2)}) collective-permute-start(f32[312,128]{1,0:T(8,128)S(1)} %get-tuple-element.84), channel_id=1, source_target_pairs={{0,28},{4,24},{8,20},{12,16},{16,12},{20,8},{24,4},{28,0},{1,29},{... | collective-permute-start | bytes 479240 | tf_op jit(solution)/shard_map/ppermute | solution.py:406
  116.2 26.0 %collective-permute-start.34 = (f32[312,128]{1,0:T(8,128)S(1)}, f32[312,128]{1,0:T(8,128)S(1)}, u32[]{:S(2)}, u32[]{:S(2)}) collective-permute-start(f32[312,128]{1,0:T(8,128)S(1)} %get-tuple-element.96), channel_id=1, source_target_pairs={{0,12},{4,8},{8,4},{12,0},{16,28},{20,24},{24,20},{28,16},{1,13},{... | collective-permute-start | bytes 479240 | tf_op jit(solution)/shard_map/ppermute | solution.py:406
  119.6 22.6 %collective-permute-start.35 = (f32[312,128]{1,0:T(8,128)S(1)}, f32[312,128]{1,0:T(8,128)S(1)}, u32[]{:S(2)}, u32[]{:S(2)}) collective-permute-start(f32[312,128]{1,0:T(8,128)S(1)} %get-tuple-element.97), channel_id=1, source_target_pairs={{0,16},{4,20},{8,24},{12,28},{16,0},{20,4},{24,8},{28,12},{1,17},{... | collective-permute-start | bytes 479240 | tf_op jit(solution)/shard_map/ppermute | solution.py:406
  124.7 17.5 %collective-permute-start.36 = (f32[312,128]{1,0:T(8,128)S(1)}, f32[312,128]{1,0:T(8,128)S(1)}, u32[]{:S(2)}, u32[]{:S(2)}) collective-permute-start(f32[312,128]{1,0:T(8,128)S(1)} %get-tuple-element.98), channel_id=1, source_target_pairs={{0,20},{4,16},{8,28},{12,24},{16,4},{20,0},{24,12},{28,8},{1,21},{... | collective-permute-start | bytes 479240 | tf_op jit(solution)/shard_map/ppermute | solution.py:406
  136.7 8.8 %collective-permute-start.37 = (f32[312,128]{1,0:T(8,128)S(1)}, f32[312,128]{1,0:T(8,128)S(1)}, u32[]{:S(2)}, u32[]{:S(2)}) collective-permute-start(f32[312,128]{1,0:T(8,128)S(1)} %get-tuple-element.99), channel_id=1, source_target_pairs={{0,24},{4,28},{8,16},{12,20},{16,8},{20,12},{24,0},{28,4},{1,25},{... | collective-permute-start | bytes 479240 | tf_op jit(solution)/shard_map/ppermute | solution.py:406
  (12 other events, 203.8 us)

commit v3 on v2

--- a/solution.py
+++ b/solution.py
@@ -237,7 +237,7 @@
 
             for i in range(plan.rows_each):
                 for tile in range(plan.full):
-                    put(i * plan.full + tile, b_ref[base + i, tile])
+                    put(tile * plan.rows_each + i, b_ref[base + i, tile])
             for m in range(plan.merged):
                 value = None
                 for k in range(plan.per_merged):
@@ -317,23 +317,24 @@
             ]
 
 
-def unpack(plan, begin, stop, received, held_ref):
+def finish_kernel(plan, begin, stop, tiles, ground_ref, *refs):
+    received, (out_ref, held_ref) = refs[: plan.group], refs[-2:]
     levels, rows_held = plan.levels, plan.rows_held
     me = lax.axis_index("lev")
 
     def store(tile, row, value):
         for first in range(0, levels, SUBS):
             count = min(SUBS, levels - first)
-            held_ref[tile, pl.ds(row + first * rows_held, count, stride=rows_held), :] = value[
-                first : first + count
-            ]
+            held_ref[tile - tiles[0], pl.ds(row + first * rows_held, count, stride=rows_held), :] = (
+                value[first : first + count]
+            )
 
     for d in range(plan.group):
         base = (me ^ d) * plan.rows_each
         for unit in range(begin, stop):
             value = received[d][(unit - begin) * levels : (unit - begin + 1) * levels]
             if unit < plan.rows_each * plan.full:
-                store(unit % plan.full, base + unit // plan.full, value)
+                store(unit // plan.rows_each, base + unit % plan.rows_each, value)
             else:
                 m = unit - plan.rows_each * plan.full
                 for k in range(plan.per_merged):
@@ -341,24 +342,16 @@
                     if i < plan.rows_each:
                         piece = pltpu.roll(value, LANES - k * plan.rest, 1) if k else value
                         store(plan.full, base + i, piece)
-
-
-def unpack_kernel(plan, begin, stop, *refs):
-    unpack(plan, begin, stop, refs[:-1], refs[-1])
-
-
-def finish_kernel(plan, begin, stop, ground_ref, held_ref, *refs):
-    out_ref = refs[plan.group]
-    levels, rows_held = plan.levels, plan.rows_held
-    unpack(plan, begin, stop, refs[: plan.group], held_ref)
-    me = lax.axis_index("lev")
-    for tile in range(plan.tiles):
+    for tile in tiles:
         width = LANES if tile < plan.full else plan.rest
         lanes = slice(tile * LANES, tile * LANES + width)
+        here = slice((tile - tiles[0]) * LANES, (tile - tiles[0]) * LANES + width)
         ground = ground_ref[:, lanes]
         for level in range(levels):
-            value = held_ref[tile, level * rows_held : level * rows_held + plan.rows, :width]
-            out_ref[level, :, lanes] = jnp.where(me * levels + level < ground, value, 0.0)
+            value = held_ref[
+                tile - tiles[0], level * rows_held : level * rows_held + plan.rows, :width
+            ]
+            out_ref[level, :, here] = jnp.where(me * levels + level < ground, value, 0.0)
 
 
 def program(increment, kappa, balance, correlation, ground_level):
@@ -396,8 +389,8 @@
             increment[: chunks[0][1]] if g == 0 else increment,
             flops=10**7,
         )
+        inner = lax.ppermute(inner, "tile", swap(0))
         outer = lax.ppermute(outer, "tile", swap(1))
-        inner = lax.ppermute(inner, "tile", swap(0))
         fields.append((field, inner, outer))
 
     def exchange(blocks):
@@ -407,7 +400,8 @@
         return [got[d] for d in range(group)]
 
     whole = [(0, plan.units)]
-    half = plan.units // 2
+    cut = (plan.full + 1) // 2
+    half = cut * plan.rows_each
     splits = [(0, half), (half, plan.units)]
     height = plan.rows_held + 2 * halo
     sources = [[] for _ in splits]
@@ -457,20 +451,25 @@
         )
         back.append(exchange(blocks))
 
-    partly = call(
-        functools.partial(unpack_kernel, plan, *splits[0]),
-        shape(plan.tiles, levels * plan.rows_held, LANES),
-        *back[0],
-        flops=10**7,
-    )
-    return call(
-        functools.partial(finish_kernel, plan, *splits[1]),
-        shape(*increment.shape),
-        ground_level,
-        partly,
-        *back[1],
-        flops=10**7,
-    )
+    result = ()
+    for s, tiles in enumerate((range(cut), range(cut, plan.tiles))):
+        assert len(tiles) <= cut or s == 1 and len(tiles) == cut
+        result = (
+            pl.pallas_call(
+                functools.partial(finish_kernel, plan, *splits[s], tiles),
+                grid=(1,),
+                out_shape=shape(*increment.shape),
+                in_specs=[VMEM] * (group + 1) + [pl.BlockSpec(memory_space=pl.ANY)] * s,
+                out_specs=pl.BlockSpec((levels, plan.rows, cut * LANES), lambda _, s=s: (0, 0, s)),
+                scratch_shapes=[pltpu.VMEM((cut, levels * plan.rows_held, LANES), f32)],
+                input_output_aliases={group + 1: 0} if s else {},
+                compiler_params=pltpu.CompilerParams(vmem_limit_bytes=14 << 20),
+                cost_estimate=pl.CostEstimate(
+                    flops=10**7, bytes_accessed=1 << 20, transcendentals=0
+                ),
+            )(ground_level, *back[s], *result),
+        )
+    return result[0]
 
 
 def solution(mesh):

time: 150 us -> 151 us (level)
  the two profiles are of different devices: /device:TPU:12 before, /device:TPU:17 now
where the time goes in v3:
time: 151 us
  starting transfers between devices  61.7 us (41%)
  waiting for transfers between devices  55.4 us (37%)
  Pallas kernels  31.8 us (21%)
  local copies, waits for them, and re-layouts  1.85 us (1%)
    ppermute x35, starting transfers between devices, exchange(): got[d] = lax.ppermute(blocks[d], 'lev', [(i, i ^ d) for i in range(group)])  55.5 us
    ppermute x35, waiting for transfers between devices, exchange(): got[d] = lax.ppermute(blocks[d], 'lev', [(i, i ^ d) for i in range(group)])  42.9 us
    pallas_call x7, Pallas kernels, call(): pl.pallas_call(kernel, out_shape=outs, in_specs=[first_spec] + [VMEM] * (...  28.9 us
    ppermute x2, waiting for transfers between devices, program(): outer = lax.ppermute(outer, 'tile', swap(1))  12.6 us
    ppermute x2, starting transfers between devices, program(): outer = lax.ppermute(outer, 'tile', swap(1))  5.62 us
  transfers between devices with their start and end apart: 39, of which 15 were waited for; matrix products, arithmetic and copies ran while one was open for 0% of the time, Pallas kernels for 17%

profile of v3, /device:TPU:17, one launch (start us, length us, event | category | flops | bytes accessed | tf_op | source)
XLA Modules:
  0.0 151.0 jit_solution(5143307731040757980)
XLA Ops:
  0.0 1.7 %copy-done = f32[18,24,1440]{2,1,0:T(8,128)S(1)} copy-done((f32[18,24,1440]{2,1,0:T(8,128)S(1)}, f32[18,24,1440]{2,1,0:T(8,128)}, u32[]{:S(2)}) %copy-start) | copy-done | bytes 2488344
  1.8 4.2 %shard_map.58 = (f32[2,24,12,8,128]{4,3,2,1,0:T(8,128)S(1)}, f32[2,10,12,8,128]{4,3,2,1,0:T(8,128)S(1)}, f32[2,10,12,8,128]{4,3,2,1,0:T(8,128)S(1)}) custom-call(f32[18,24,1440]{2,1,0:T(8,128)S(1)} %copy-done), custom_call_target="tpu_custom_call" | custom-call | flops 10000000 | bytes 1048576 | tf_op jit(solution)/shard_map/pallas_call | solution.py:368
  5.9 3.7 %collective-permute-start.10 = (f32[2,10,12,8,128]{4,3,2,1,0:T(8,128)S(1)}, f32[2,10,12,8,128]{4,3,2,1,0:T(8,128)S(1)}, u32[]{:S(2)}, u32[]{:S(2)}) collective-permute-start(f32[2,10,12,8,128]{4,3,2,1,0:T(8,128)S(1)} %get-tuple-element.68), channel_id=1, source_target_pairs={{1,2},{2,1},{5,6},{6,5},{9,10},{10,9},{13,14},{14,13},{17,18},{18,... | collective-permute-start | bytes 2949128 | tf_op jit(solution)/shard_map/ppermute | solution.py:393
  9.8 2.1 %shard_map.56 = (f32[1,24,12,8,128]{4,3,2,1,0:T(8,128)S(1)}, f32[1,10,12,8,128]{4,3,2,1,0:T(8,128)S(1)}, f32[1,10,12,8,128]{4,3,2,1,0:T(8,128)S(1)}) custom-call(f32[8,24,1440]{2,1,0:T(8,128)S(1)} %slice.3.x_ref), custom_call_target="tpu_custom_call" | custom-call | flops 10000000 | bytes 1048576 | tf_op jit(solution)/shard_map/pallas_call | solution.py:368
  12.5 1.9 %collective-permute-start.1 = (f32[1,10,12,8,128]{4,3,2,1,0:T(8,128)S(1)}, f32[1,10,12,8,128]{4,3,2,1,0:T(8,128)S(1)}, u32[]{:S(2)}, u32[]{:S(2)}) collective-permute-start(f32[1,10,12,8,128]{4,3,2,1,0:T(8,128)S(1)} %get-tuple-element.57), channel_id=1, source_target_pairs={{1,2},{2,1},{5,6},{6,5},{9,10},{10,9},{13,14},{14,13},{17,18},{18,... | collective-permute-start | bytes 1474568 | tf_op jit(solution)/shard_map/ppermute | solution.py:393
  14.4 12.6 %collective-permute-done.1.refs_3_ = f32[1,10,12,8,128]{4,3,2,1,0:T(8,128)S(1)} collective-permute-done((f32[1,10,12,8,128]{4,3,2,1,0:T(8,128)S(1)}, f32[1,10,12,8,128]{4,3,2,1,0:T(8,128)S(1)}, u32[]{:S(2)}, u32[]{:S(2)}) %collective-permute-start.1) | collective-permute-done | bytes 491552 | tf_op jit(solution)/shard_map/ppermute | solution.py:393
  27.0 6.6 %shard_map.57 = (f32[272,128]{1,0:T(8,128)S(1)}, f32[272,128]{1,0:T(8,128)S(1)}, f32[272,128]{1,0:T(8,128)S(1)}, f32[272,128]{1,0:T(8,128)S(1)}, f32[272,128]{1,...) custom-call(f32[18]{0:T(128)S(1)} %copy-done.2, ...), custom_call_target="tpu_custom_call" | custom-call | flops 1000000000 | bytes 1048576 | tf_op jit(solution)/shard_map/pallas_call | solution.py:368
  38.0 1.7 %collective-permute-done.3.refs_2_ = f32[272,128]{1,0:T(8,128)S(1)} collective-permute-done((f32[272,128]{1,0:T(8,128)S(1)}, f32[272,128]{1,0:T(8,128)S(1)}, u32[]{:S(2)}, u32[]{:S(2)}) %collective-permute-start.3) | collective-permute-done | bytes 139296 | tf_op jit(solution)/shard_map/ppermute | solution.py:399
  40.9 2.8 %collective-permute-start.7 = (f32[272,128]{1,0:T(8,128)S(1)}, f32[272,128]{1,0:T(8,128)S(1)}, u32[]{:S(2)}, u32[]{:S(2)}) collective-permute-start(f32[272,128]{1,0:T(8,128)S(1)} %get-tuple-element.64), channel_id=1, source_target_pairs={{0,24},{4,28},{8,16},{12,20},{16,8},{20,12},{24,0},{28,4},{1,25},{... | collective-permute-start | bytes 417800 | tf_op jit(solution)/shard_map/ppermute | solution.py:399
  44.1 12.2 %shard_map.59 = (f32[184,128]{1,0:T(8,128)S(1)}, f32[184,128]{1,0:T(8,128)S(1)}, f32[184,128]{1,0:T(8,128)S(1)}, f32[184,128]{1,0:T(8,128)S(1)}, f32[184,128]{1,...) custom-call(f32[18]{0:T(128)S(1)} %copy-done.2, ...), custom_call_target="tpu_custom_call" | custom-call | flops 1000000000 | bytes 1048576 | tf_op jit(solution)/shard_map/pallas_call | solution.py:368
  57.3 3.9 %collective-permute-start.26 = (f32[184,128]{1,0:T(8,128)S(1)}, f32[184,128]{1,0:T(8,128)S(1)}, u32[]{:S(2)}, u32[]{:S(2)}) collective-permute-start(f32[184,128]{1,0:T(8,128)S(1)} %get-tuple-element.87), channel_id=1, source_target_pairs={{0,8},{4,12},{8,0},{12,4},{16,24},{20,28},{24,16},{28,20},{1,9},{5... | collective-permute-start | bytes 282632 | tf_op jit(solution)/shard_map/ppermute | solution.py:399
  66.4 3.0 %collective-permute-start.29 = (f32[184,128]{1,0:T(8,128)S(1)}, f32[184,128]{1,0:T(8,128)S(1)}, u32[]{:S(2)}, u32[]{:S(2)}) collective-permute-start(f32[184,128]{1,0:T(8,128)S(1)} %get-tuple-element.90), channel_id=1, source_target_pairs={{0,20},{4,16},{8,28},{12,24},{16,4},{20,0},{24,12},{28,8},{1,21},{... | collective-permute-start | bytes 282632 | tf_op jit(solution)/shard_map/ppermute | solution.py:399
  69.6 2.9 %collective-permute-start.31 = (f32[184,128]{1,0:T(8,128)S(1)}, f32[184,128]{1,0:T(8,128)S(1)}, u32[]{:S(2)}, u32[]{:S(2)}) collective-permute-start(f32[184,128]{1,0:T(8,128)S(1)} %get-tuple-element.92), channel_id=1, source_target_pairs={{0,28},{4,24},{8,20},{12,16},{16,12},{20,8},{24,4},{28,0},{1,29},{... | collective-permute-start | bytes 282632 | tf_op jit(solution)/shard_map/ppermute | solution.py:399
  73.3 2.1 %collective-permute-start.13 = (f32[160,128]{1,0:T(8,128)S(1)}, f32[160,128]{1,0:T(8,128)S(1)}, u32[]{:S(2)}, u32[]{:S(2)}) collective-permute-start(f32[160,128]{1,0:T(8,128)S(1)} %get-tuple-element.72), channel_id=1, source_target_pairs={{0,12},{4,8},{8,4},{12,0},{16,28},{20,24},{24,20},{28,16},{1,13},{... | collective-permute-start | bytes 245768 | tf_op jit(solution)/shard_map/ppermute | solution.py:399
  75.4 3.1 %collective-permute-start.14 = (f32[160,128]{1,0:T(8,128)S(1)}, f32[160,128]{1,0:T(8,128)S(1)}, u32[]{:S(2)}, u32[]{:S(2)}) collective-permute-start(f32[160,128]{1,0:T(8,128)S(1)} %get-tuple-element.73), channel_id=1, source_target_pairs={{0,16},{4,20},{8,24},{12,28},{16,0},{20,4},{24,8},{28,12},{1,17},{... | collective-permute-start | bytes 245768 | tf_op jit(solution)/shard_map/ppermute | solution.py:399
  78.6 3.4 %collective-permute-start.15 = (f32[160,128]{1,0:T(8,128)S(1)}, f32[160,128]{1,0:T(8,128)S(1)}, u32[]{:S(2)}, u32[]{:S(2)}) collective-permute-start(f32[160,128]{1,0:T(8,128)S(1)} %get-tuple-element.74), channel_id=1, source_target_pairs={{0,20},{4,16},{8,28},{12,24},{16,4},{20,0},{24,12},{28,8},{1,21},{... | collective-permute-start | bytes 245768 | tf_op jit(solution)/shard_map/ppermute | solution.py:399
  82.6 2.5 %collective-permute-done.31.refs_15_ = f32[184,128]{1,0:T(8,128)S(1)} collective-permute-done((f32[184,128]{1,0:T(8,128)S(1)}, f32[184,128]{1,0:T(8,128)S(1)}, u32[]{:S(2)}, u32[]{:S(2)}) %collective-permute-start.31) | collective-permute-done | bytes 94240 | tf_op jit(solution)/shard_map/ppermute | solution.py:399
  86.9 2.3 %collective-permute-start.32 = (f32[328,128]{1,0:T(8,128)S(1)}, f32[328,128]{1,0:T(8,128)S(1)}, u32[]{:S(2)}, u32[]{:S(2)}) collective-permute-start(f32[328,128]{1,0:T(8,128)S(1)} %get-tuple-element.94), channel_id=1, source_target_pairs={{0,4},{4,0},{8,12},{12,8},{16,20},{20,16},{24,28},{28,24},{1,5},{5... | collective-permute-start | bytes 503816 | tf_op jit(solution)/shard_map/ppermute | solution.py:399
  93.7 1.9 %collective-permute-done.18.refs_1_ = f32[288,128]{1,0:T(8,128)S(1)} collective-permute-done((f32[288,128]{1,0:T(8,128)S(1)}, f32[288,128]{1,0:T(8,128)S(1)}, u32[]{:S(2)}, u32[]{:S(2)}) %collective-permute-start.18) | collective-permute-done | bytes 147488 | tf_op jit(solution)/shard_map/ppermute | solution.py:399
  96.5 3.7 %collective-permute-start.36 = (f32[328,128]{1,0:T(8,128)S(1)}, f32[328,128]{1,0:T(8,128)S(1)}, u32[]{:S(2)}, u32[]{:S(2)}) collective-permute-start(f32[328,128]{1,0:T(8,128)S(1)} %get-tuple-element.98), channel_id=1, source_target_pairs={{0,20},{4,16},{8,28},{12,24},{16,4},{20,0},{24,12},{28,8},{1,21},{... | collective-permute-start | bytes 503816 | tf_op jit(solution)/shard_map/ppermute | solution.py:399
  100.2 2.9 %collective-permute-start.38 = (f32[328,128]{1,0:T(8,128)S(1)}, f32[328,128]{1,0:T(8,128)S(1)}, u32[]{:S(2)}, u32[]{:S(2)}) collective-permute-start(f32[328,128]{1,0:T(8,128)S(1)} %get-tuple-element.100), channel_id=1, source_target_pairs={{0,28},{4,24},{8,20},{12,16},{16,12},{20,8},{24,4},{28,0},{1,29},{... | collective-permute-start | bytes 503816 | tf_op jit(solution)/shard_map/ppermute | solution.py:399
  103.1 1.6 %collective-permute-start.20 = (f32[288,128]{1,0:T(8,128)S(1)}, f32[288,128]{1,0:T(8,128)S(1)}, u32[]{:S(2)}, u32[]{:S(2)}) collective-permute-start(f32[288,128]{1,0:T(8,128)S(1)} %get-tuple-element.80), channel_id=1, source_target_pairs={{0,12},{4,8},{8,4},{12,0},{16,28},{20,24},{24,20},{28,16},{1,13},{... | collective-permute-start | bytes 442376 | tf_op jit(solution)/shard_map/ppermute | solution.py:399
  104.7 11.1 %collective-permute-done.35.refs_4_ = f32[328,128]{1,0:T(8,128)S(1)} collective-permute-done((f32[328,128]{1,0:T(8,128)S(1)}, f32[328,128]{1,0:T(8,128)S(1)}, u32[]{:S(2)}, u32[]{:S(2)}) %collective-permute-start.35) | collective-permute-done | bytes 167968 | tf_op jit(solution)/shard_map/ppermute | solution.py:399
  115.8 2.9 %collective-permute-start.21 = (f32[288,128]{1,0:T(8,128)S(1)}, f32[288,128]{1,0:T(8,128)S(1)}, u32[]{:S(2)}, u32[]{:S(2)}) collective-permute-start(f32[288,128]{1,0:T(8,128)S(1)} %get-tuple-element.81), channel_id=1, source_target_pairs={{0,16},{4,20},{8,24},{12,28},{16,0},{20,4},{24,8},{28,12},{1,17},{... | collective-permute-start | bytes 442376 | tf_op jit(solution)/shard_map/ppermute | solution.py:399
  118.7 7.0 %collective-permute-done.36.refs_5_ = f32[328,128]{1,0:T(8,128)S(1)} collective-permute-done((f32[328,128]{1,0:T(8,128)S(1)}, f32[328,128]{1,0:T(8,128)S(1)}, u32[]{:S(2)}, u32[]{:S(2)}) %collective-permute-start.36) | collective-permute-done | bytes 167968 | tf_op jit(solution)/shard_map/ppermute | solution.py:399
  125.7 3.8 %collective-permute-start.22 = (f32[288,128]{1,0:T(8,128)S(1)}, f32[288,128]{1,0:T(8,128)S(1)}, u32[]{:S(2)}, u32[]{:S(2)}) collective-permute-start(f32[288,128]{1,0:T(8,128)S(1)} %get-tuple-element.82), channel_id=1, source_target_pairs={{0,20},{4,16},{8,28},{12,24},{16,4},{20,0},{24,12},{28,8},{1,21},{... | collective-permute-start | bytes 442376 | tf_op jit(solution)/shard_map/ppermute | solution.py:399
  129.6 4.6 %collective-permute-done.37.refs_6_ = f32[328,128]{1,0:T(8,128)S(1)} collective-permute-done((f32[328,128]{1,0:T(8,128)S(1)}, f32[328,128]{1,0:T(8,128)S(1)}, u32[]{:S(2)}, u32[]{:S(2)}) %collective-permute-start.37) | collective-permute-done | bytes 167968 | tf_op jit(solution)/shard_map/ppermute | solution.py:399
  134.2 1.9 %collective-permute-start.23 = (f32[288,128]{1,0:T(8,128)S(1)}, f32[288,128]{1,0:T(8,128)S(1)}, u32[]{:S(2)}, u32[]{:S(2)}) collective-permute-start(f32[288,128]{1,0:T(8,128)S(1)} %get-tuple-element.83), channel_id=1, source_target_pairs={{0,24},{4,28},{8,16},{12,20},{16,8},{20,12},{24,0},{28,4},{1,25},{... | collective-permute-start | bytes 442376 | tf_op jit(solution)/shard_map/ppermute | solution.py:399
  136.1 2.4 %collective-permute-done.38.refs_7_ = f32[328,128]{1,0:T(8,128)S(1)} collective-permute-done((f32[328,128]{1,0:T(8,128)S(1)}, f32[328,128]{1,0:T(8,128)S(1)}, u32[]{:S(2)}, u32[]{:S(2)}) %collective-permute-start.38) | collective-permute-done | bytes 167968 | tf_op jit(solution)/shard_map/ppermute | solution.py:399
  138.5 2.1 %collective-permute-start.24 = (f32[288,128]{1,0:T(8,128)S(1)}, f32[288,128]{1,0:T(8,128)S(1)}, u32[]{:S(2)}, u32[]{:S(2)}) collective-permute-start(f32[288,128]{1,0:T(8,128)S(1)} %get-tuple-element.84), channel_id=1, source_target_pairs={{0,28},{4,24},{8,20},{12,16},{16,12},{20,8},{24,4},{28,0},{1,29},{... | collective-permute-start | bytes 442376 | tf_op jit(solution)/shard_map/ppermute | solution.py:399
  143.5 4.0 %collective-permute-done.23.refs_6_ = f32[288,128]{1,0:T(8,128)S(1)} collective-permute-done((f32[288,128]{1,0:T(8,128)S(1)}, f32[288,128]{1,0:T(8,128)S(1)}, u32[]{:S(2)}, u32[]{:S(2)}) %collective-permute-start.23) | collective-permute-done | bytes 147488 | tf_op jit(solution)/shard_map/ppermute | solution.py:399
  147.5 2.0 %collective-permute-done.24.refs_7_ = f32[288,128]{1,0:T(8,128)S(1)} collective-permute-done((f32[288,128]{1,0:T(8,128)S(1)}, f32[288,128]{1,0:T(8,128)S(1)}, u32[]{:S(2)}, u32[]{:S(2)}) %collective-permute-start.24) | collective-permute-done | bytes 147488 | tf_op jit(solution)/shard_map/ppermute | solution.py:399
  (66 shorter events, 26.0 us)
Async XLA Ops:
  5.9 35.0 %collective-permute-start.10 = (f32[2,10,12,8,128]{4,3,2,1,0:T(8,128)S(1)}, f32[2,10,12,8,128]{4,3,2,1,0:T(8,128)S(1)}, u32[]{:S(2)}, u32[]{:S(2)}) collective-permute-start(f32[2,10,12,8,128]{4,3,2,1,0:T(8,128)S(1)} %get-tuple-element.68), channel_id=1, source_target_pairs={{1,2},{2,1},{5,6},{6,5},{9,10},{10,9},{13,14},{14,13},{17,18},{18,... | collective-permute-start | bytes 2949128 | tf_op jit(solution)/shard_map/ppermute | solution.py:393
  9.7 34.0 %collective-permute-start.9 = (f32[2,10,12,8,128]{4,3,2,1,0:T(8,128)S(1)}, f32[2,10,12,8,128]{4,3,2,1,0:T(8,128)S(1)}, u32[]{:S(2)}, u32[]{:S(2)}) collective-permute-start(f32[2,10,12,8,128]{4,3,2,1,0:T(8,128)S(1)} %get-tuple-element.67), channel_id=1, source_target_pairs={{0,1},{1,0},{2,3},{3,2},{4,5},{5,4},{6,7},{7,6},{8,9},{9,8},{10,11... | collective-permute-start | bytes 2949128 | tf_op jit(solution)/shard_map/ppermute | solution.py:392
  12.5 14.5 %collective-permute-start.1 = (f32[1,10,12,8,128]{4,3,2,1,0:T(8,128)S(1)}, f32[1,10,12,8,128]{4,3,2,1,0:T(8,128)S(1)}, u32[]{:S(2)}, u32[]{:S(2)}) collective-permute-start(f32[1,10,12,8,128]{4,3,2,1,0:T(8,128)S(1)} %get-tuple-element.57), channel_id=1, source_target_pairs={{1,2},{2,1},{5,6},{6,5},{9,10},{10,9},{13,14},{14,13},{17,18},{18,... | collective-permute-start | bytes 1474568 | tf_op jit(solution)/shard_map/ppermute | solution.py:393
  35.9 20.4 %collective-permute-start.4 = (f32[272,128]{1,0:T(8,128)S(1)}, f32[272,128]{1,0:T(8,128)S(1)}, u32[]{:S(2)}, u32[]{:S(2)}) collective-permute-start(f32[272,128]{1,0:T(8,128)S(1)} %get-tuple-element.61), channel_id=1, source_target_pairs={{0,12},{4,8},{8,4},{12,0},{16,28},{20,24},{24,20},{28,16},{1,13},{... | collective-permute-start | bytes 417800 | tf_op jit(solution)/shard_map/ppermute | solution.py:399
  37.6 19.6 %collective-permute-start.5 = (f32[272,128]{1,0:T(8,128)S(1)}, f32[272,128]{1,0:T(8,128)S(1)}, u32[]{:S(2)}, u32[]{:S(2)}) collective-permute-start(f32[272,128]{1,0:T(8,128)S(1)} %get-tuple-element.62), channel_id=1, source_target_pairs={{0,16},{4,20},{8,24},{12,28},{16,0},{20,4},{24,8},{28,12},{1,17},{... | collective-permute-start | bytes 417800 | tf_op jit(solution)/shard_map/ppermute | solution.py:399
  39.7 21.6 %collective-permute-start.6 = (f32[272,128]{1,0:T(8,128)S(1)}, f32[272,128]{1,0:T(8,128)S(1)}, u32[]{:S(2)}, u32[]{:S(2)}) collective-permute-start(f32[272,128]{1,0:T(8,128)S(1)} %get-tuple-element.63), channel_id=1, source_target_pairs={{0,20},{4,16},{8,28},{12,24},{16,4},{20,0},{24,12},{28,8},{1,21},{... | collective-permute-start | bytes 417800 | tf_op jit(solution)/shard_map/ppermute | solution.py:399
  40.9 21.3 %collective-permute-start.7 = (f32[272,128]{1,0:T(8,128)S(1)}, f32[272,128]{1,0:T(8,128)S(1)}, u32[]{:S(2)}, u32[]{:S(2)}) collective-permute-start(f32[272,128]{1,0:T(8,128)S(1)} %get-tuple-element.64), channel_id=1, source_target_pairs={{0,24},{4,28},{8,16},{12,20},{16,8},{20,12},{24,0},{28,4},{1,25},{... | collective-permute-start | bytes 417800 | tf_op jit(solution)/shard_map/ppermute | solution.py:399
  43.7 18.6 %collective-permute-start.8 = (f32[272,128]{1,0:T(8,128)S(1)}, f32[272,128]{1,0:T(8,128)S(1)}, u32[]{:S(2)}, u32[]{:S(2)}) collective-permute-start(f32[272,128]{1,0:T(8,128)S(1)} %get-tuple-element.65), channel_id=1, source_target_pairs={{0,28},{4,24},{8,20},{12,16},{16,12},{20,8},{24,4},{28,0},{1,29},{... | collective-permute-start | bytes 417800 | tf_op jit(solution)/shard_map/ppermute | solution.py:399
  56.3 13.1 %collective-permute-start.25 = (f32[184,128]{1,0:T(8,128)S(1)}, f32[184,128]{1,0:T(8,128)S(1)}, u32[]{:S(2)}, u32[]{:S(2)}) collective-permute-start(f32[184,128]{1,0:T(8,128)S(1)} %get-tuple-element.86), channel_id=1, source_target_pairs={{0,4},{4,0},{8,12},{12,8},{16,20},{20,16},{24,28},{28,24},{1,5},{5... | collective-permute-start | bytes 282632 | tf_op jit(solution)/shard_map/ppermute | solution.py:399
  57.3 12.3 %collective-permute-start.26 = (f32[184,128]{1,0:T(8,128)S(1)}, f32[184,128]{1,0:T(8,128)S(1)}, u32[]{:S(2)}, u32[]{:S(2)}) collective-permute-start(f32[184,128]{1,0:T(8,128)S(1)} %get-tuple-element.87), channel_id=1, source_target_pairs={{0,8},{4,12},{8,0},{12,4},{16,24},{20,28},{24,16},{28,20},{1,9},{5... | collective-permute-start | bytes 282632 | tf_op jit(solution)/shard_map/ppermute | solution.py:399
  62.3 11.0 %collective-permute-start.27 = (f32[184,128]{1,0:T(8,128)S(1)}, f32[184,128]{1,0:T(8,128)S(1)}, u32[]{:S(2)}, u32[]{:S(2)}) collective-permute-start(f32[184,128]{1,0:T(8,128)S(1)} %get-tuple-element.88), channel_id=1, source_target_pairs={{0,12},{4,8},{8,4},{12,0},{16,28},{20,24},{24,20},{28,16},{1,13},{... | collective-permute-start | bytes 282632 | tf_op jit(solution)/shard_map/ppermute | solution.py:399
  65.4 10.0 %collective-permute-start.28 = (f32[184,128]{1,0:T(8,128)S(1)}, f32[184,128]{1,0:T(8,128)S(1)}, u32[]{:S(2)}, u32[]{:S(2)}) collective-permute-start(f32[184,128]{1,0:T(8,128)S(1)} %get-tuple-element.89), channel_id=1, source_target_pairs={{0,16},{4,20},{8,24},{12,28},{16,0},{20,4},{24,8},{28,12},{1,17},{... | collective-permute-start | bytes 282632 | tf_op jit(solution)/shard_map/ppermute | solution.py:399
  66.4 12.1 %collective-permute-start.29 = (f32[184,128]{1,0:T(8,128)S(1)}, f32[184,128]{1,0:T(8,128)S(1)}, u32[]{:S(2)}, u32[]{:S(2)}) collective-permute-start(f32[184,128]{1,0:T(8,128)S(1)} %get-tuple-element.90), channel_id=1, source_target_pairs={{0,20},{4,16},{8,28},{12,24},{16,4},{20,0},{24,12},{28,8},{1,21},{... | collective-permute-start | bytes 282632 | tf_op jit(solution)/shard_map/ppermute | solution.py:399
  69.4 12.6 %collective-permute-start.30 = (f32[184,128]{1,0:T(8,128)S(1)}, f32[184,128]{1,0:T(8,128)S(1)}, u32[]{:S(2)}, u32[]{:S(2)}) collective-permute-start(f32[184,128]{1,0:T(8,128)S(1)} %get-tuple-element.91), channel_id=1, source_target_pairs={{0,24},{4,28},{8,16},{12,20},{16,8},{20,12},{24,0},{28,4},{1,25},{... | collective-permute-start | bytes 282632 | tf_op jit(solution)/shard_map/ppermute | solution.py:399
  69.6 15.5 %collective-permute-start.31 = (f32[184,128]{1,0:T(8,128)S(1)}, f32[184,128]{1,0:T(8,128)S(1)}, u32[]{:S(2)}, u32[]{:S(2)}) collective-permute-start(f32[184,128]{1,0:T(8,128)S(1)} %get-tuple-element.92), channel_id=1, source_target_pairs={{0,28},{4,24},{8,20},{12,16},{16,12},{20,8},{24,4},{28,0},{1,29},{... | collective-permute-start | bytes 282632 | tf_op jit(solution)/shard_map/ppermute | solution.py:399
  73.3 13.5 %collective-permute-start.13 = (f32[160,128]{1,0:T(8,128)S(1)}, f32[160,128]{1,0:T(8,128)S(1)}, u32[]{:S(2)}, u32[]{:S(2)}) collective-permute-start(f32[160,128]{1,0:T(8,128)S(1)} %get-tuple-element.72), channel_id=1, source_target_pairs={{0,12},{4,8},{8,4},{12,0},{16,28},{20,24},{24,20},{28,16},{1,13},{... | collective-permute-start | bytes 245768 | tf_op jit(solution)/shard_map/ppermute | solution.py:399
  75.4 13.8 %collective-permute-start.14 = (f32[160,128]{1,0:T(8,128)S(1)}, f32[160,128]{1,0:T(8,128)S(1)}, u32[]{:S(2)}, u32[]{:S(2)}) collective-permute-start(f32[160,128]{1,0:T(8,128)S(1)} %get-tuple-element.73), channel_id=1, source_target_pairs={{0,16},{4,20},{8,24},{12,28},{16,0},{20,4},{24,8},{28,12},{1,17},{... | collective-permute-start | bytes 245768 | tf_op jit(solution)/shard_map/ppermute | solution.py:399
  78.6 10.6 %collective-permute-start.15 = (f32[160,128]{1,0:T(8,128)S(1)}, f32[160,128]{1,0:T(8,128)S(1)}, u32[]{:S(2)}, u32[]{:S(2)}) collective-permute-start(f32[160,128]{1,0:T(8,128)S(1)} %get-tuple-element.74), channel_id=1, source_target_pairs={{0,20},{4,16},{8,28},{12,24},{16,4},{20,0},{24,12},{28,8},{1,21},{... | collective-permute-start | bytes 245768 | tf_op jit(solution)/shard_map/ppermute | solution.py:399
  82.0 7.2 %collective-permute-start.16 = (f32[160,128]{1,0:T(8,128)S(1)}, f32[160,128]{1,0:T(8,128)S(1)}, u32[]{:S(2)}, u32[]{:S(2)}) collective-permute-start(f32[160,128]{1,0:T(8,128)S(1)} %get-tuple-element.75), channel_id=1, source_target_pairs={{0,24},{4,28},{8,16},{12,20},{16,8},{20,12},{24,0},{28,4},{1,25},{... | collective-permute-start | bytes 245768 | tf_op jit(solution)/shard_map/ppermute | solution.py:399
  86.9 13.3 %collective-permute-start.32 = (f32[328,128]{1,0:T(8,128)S(1)}, f32[328,128]{1,0:T(8,128)S(1)}, u32[]{:S(2)}, u32[]{:S(2)}) collective-permute-start(f32[328,128]{1,0:T(8,128)S(1)} %get-tuple-element.94), channel_id=1, source_target_pairs={{0,4},{4,0},{8,12},{12,8},{16,20},{20,16},{24,28},{28,24},{1,5},{5... | collective-permute-start | bytes 503816 | tf_op jit(solution)/shard_map/ppermute | solution.py:399
  89.2 11.0 %collective-permute-start.33 = (f32[328,128]{1,0:T(8,128)S(1)}, f32[328,128]{1,0:T(8,128)S(1)}, u32[]{:S(2)}, u32[]{:S(2)}) collective-permute-start(f32[328,128]{1,0:T(8,128)S(1)} %get-tuple-element.95), channel_id=1, source_target_pairs={{0,8},{4,12},{8,0},{12,4},{16,24},{20,28},{24,16},{28,20},{1,9},{5... | collective-permute-start | bytes 503816 | tf_op jit(solution)/shard_map/ppermute | solution.py:399
  91.2 5.3 %collective-permute-start.19 = (f32[288,128]{1,0:T(8,128)S(1)}, f32[288,128]{1,0:T(8,128)S(1)}, u32[]{:S(2)}, u32[]{:S(2)}) collective-permute-start(f32[288,128]{1,0:T(8,128)S(1)} %get-tuple-element.79), channel_id=1, source_target_pairs={{0,8},{4,12},{8,0},{12,4},{16,24},{20,28},{24,16},{28,20},{1,9},{5... | collective-permute-start | bytes 442376 | tf_op jit(solution)/shard_map/ppermute | solution.py:399
  92.2 10.9 %collective-permute-start.34 = (f32[328,128]{1,0:T(8,128)S(1)}, f32[328,128]{1,0:T(8,128)S(1)}, u32[]{:S(2)}, u32[]{:S(2)}) collective-permute-start(f32[328,128]{1,0:T(8,128)S(1)} %get-tuple-element.96), channel_id=1, source_target_pairs={{0,12},{4,8},{8,4},{12,0},{16,28},{20,24},{24,20},{28,16},{1,13},{... | collective-permute-start | bytes 503816 | tf_op jit(solution)/shard_map/ppermute | solution.py:399
  95.6 20.2 %collective-permute-start.35 = (f32[328,128]{1,0:T(8,128)S(1)}, f32[328,128]{1,0:T(8,128)S(1)}, u32[]{:S(2)}, u32[]{:S(2)}) collective-permute-start(f32[328,128]{1,0:T(8,128)S(1)} %get-tuple-element.97), channel_id=1, source_target_pairs={{0,16},{4,20},{8,24},{12,28},{16,0},{20,4},{24,8},{28,12},{1,17},{... | collective-permute-start | bytes 503816 | tf_op jit(solution)/shard_map/ppermute | solution.py:399
  96.5 29.2 %collective-permute-start.36 = (f32[328,128]{1,0:T(8,128)S(1)}, f32[328,128]{1,0:T(8,128)S(1)}, u32[]{:S(2)}, u32[]{:S(2)}) collective-permute-start(f32[328,128]{1,0:T(8,128)S(1)} %get-tuple-element.98), channel_id=1, source_target_pairs={{0,20},{4,16},{8,28},{12,24},{16,4},{20,0},{24,12},{28,8},{1,21},{... | collective-permute-start | bytes 503816 | tf_op jit(solution)/shard_map/ppermute | solution.py:399
  100.2 34.0 %collective-permute-start.37 = (f32[328,128]{1,0:T(8,128)S(1)}, f32[328,128]{1,0:T(8,128)S(1)}, u32[]{:S(2)}, u32[]{:S(2)}) collective-permute-start(f32[328,128]{1,0:T(8,128)S(1)} %get-tuple-element.99), channel_id=1, source_target_pairs={{0,24},{4,28},{8,16},{12,20},{16,8},{20,12},{24,0},{28,4},{1,25},{... | collective-permute-start | bytes 503816 | tf_op jit(solution)/shard_map/ppermute | solution.py:399
  100.2 38.3 %collective-permute-start.38 = (f32[328,128]{1,0:T(8,128)S(1)}, f32[328,128]{1,0:T(8,128)S(1)}, u32[]{:S(2)}, u32[]{:S(2)}) collective-permute-start(f32[328,128]{1,0:T(8,128)S(1)} %get-tuple-element.100), channel_id=1, source_target_pairs={{0,28},{4,24},{8,20},{12,16},{16,12},{20,8},{24,4},{28,0},{1,29},{... | collective-permute-start | bytes 503816 | tf_op jit(solution)/shard_map/ppermute | solution.py:399
  103.1 38.9 %collective-permute-start.20 = (f32[288,128]{1,0:T(8,128)S(1)}, f32[288,128]{1,0:T(8,128)S(1)}, u32[]{:S(2)}, u32[]{:S(2)}) collective-permute-start(f32[288,128]{1,0:T(8,128)S(1)} %get-tuple-element.80), channel_id=1, source_target_pairs={{0,12},{4,8},{8,4},{12,0},{16,28},{20,24},{24,20},{28,16},{1,13},{... | collective-permute-start | bytes 442376 | tf_op jit(solution)/shard_map/ppermute | solution.py:399
  115.8 26.2 %collective-permute-start.21 = (f32[288,128]{1,0:T(8,128)S(1)}, f32[288,128]{1,0:T(8,128)S(1)}, u32[]{:S(2)}, u32[]{:S(2)}) collective-permute-start(f32[288,128]{1,0:T(8,128)S(1)} %get-tuple-element.81), channel_id=1, source_target_pairs={{0,16},{4,20},{8,24},{12,28},{16,0},{20,4},{24,8},{28,12},{1,17},{... | collective-permute-start | bytes 442376 | tf_op jit(solution)/shard_map/ppermute | solution.py:399
  125.7 17.8 %collective-permute-start.22 = (f32[288,128]{1,0:T(8,128)S(1)}, f32[288,128]{1,0:T(8,128)S(1)}, u32[]{:S(2)}, u32[]{:S(2)}) collective-permute-start(f32[288,128]{1,0:T(8,128)S(1)} %get-tuple-element.82), channel_id=1, source_target_pairs={{0,20},{4,16},{8,28},{12,24},{16,4},{20,0},{24,12},{28,8},{1,21},{... | collective-permute-start | bytes 442376 | tf_op jit(solution)/shard_map/ppermute | solution.py:399
  134.2 13.3 %collective-permute-start.23 = (f32[288,128]{1,0:T(8,128)S(1)}, f32[288,128]{1,0:T(8,128)S(1)}, u32[]{:S(2)}, u32[]{:S(2)}) collective-permute-start(f32[288,128]{1,0:T(8,128)S(1)} %get-tuple-element.83), channel_id=1, source_target_pairs={{0,24},{4,28},{8,16},{12,20},{16,8},{20,12},{24,0},{28,4},{1,25},{... | collective-permute-start | bytes 442376 | tf_op jit(solution)/shard_map/ppermute | solution.py:399
  138.5 11.0 %collective-permute-start.24 = (f32[288,128]{1,0:T(8,128)S(1)}, f32[288,128]{1,0:T(8,128)S(1)}, u32[]{:S(2)}, u32[]{:S(2)}) collective-permute-start(f32[288,128]{1,0:T(8,128)S(1)} %get-tuple-element.84), channel_id=1, source_target_pairs={{0,28},{4,24},{8,20},{12,16},{16,12},{20,8},{24,4},{28,0},{1,29},{... | collective-permute-start | bytes 442376 | tf_op jit(solution)/shard_map/ppermute | solution.py:399
  (12 other events, 187.4 us)

commit v4 on v3

--- a/solution.py
+++ b/solution.py
@@ -11,7 +11,7 @@
 PASSES = 10
 LANES = 128
 SUBS = 8
-UNROLLS = (4, 2)
+UNROLLS = (6, 4, 2)
 DEAL = 4
 
 VMEM = pl.BlockSpec(memory_space=pltpu.VMEM)
@@ -47,6 +47,15 @@
         self.units = self.rows_each * self.full + self.merged
         self.chunks = level_chunks(self.levels)
 
+    def edge_places(self, chunks):
+        places, used = [], 0
+        for c, (_, count) in enumerate(chunks):
+            share = SUBS // count
+            for row in range(self.halo):
+                places.append((c, row, used + row // share, row % share * count))
+            used += -(-self.halo // share)
+        return places, used
+
 
 def lane_ids():
     return lax.broadcasted_iota(jnp.int32, (SUBS, LANES), 1)
@@ -128,17 +137,20 @@
             return 0
 
         lax.fori_loop(0, plan.rows // unroll, deal, 0)
-        for row in range(plan.halo):
-            for tile in range(plan.tiles):
-                inner_ref[c, row, tile] = all_ref[c, inner_row + row, tile]
-                outer_ref[c, row, tile] = all_ref[c, outer_row + row, tile]
-
-
-def diffuse(plan, at, chunk, kappa_ref, x_ref, inner_ref, outer_ref, a_ref, b_ref):
+    for c, row, place, sublane in plan.edge_places(chunks)[0]:
+        count = chunks[c][1]
+        here = slice(sublane, sublane + count)
+        for tile in range(plan.tiles):
+            inner_ref[place, tile, here] = all_ref[c, inner_row + row, tile, :count]
+            outer_ref[place, tile, here] = all_ref[c, outer_row + row, tile, :count]
+
+
+def diffuse(plan, at, chunks, kappa_ref, x_ref, inner_ref, outer_ref, a_ref, b_ref):
     tile_index = lax.axis_index("tile")
     height = plan.rows + 2 * plan.halo
     lane = lane_ids()
     at_start, at_end = lane == 0, lane == LANES - 1
+    chunk = chunks[at]
     level = lax.broadcasted_iota(jnp.int32, (SUBS, LANES), 0)
     kappa = jnp.full((SUBS, LANES), 0.125, jnp.float32)
     for i in range(chunk[1]):
@@ -150,9 +162,13 @@
     }
     below = plan.halo + plan.rows
     inner_row = jnp.where(tile_index % 2 == 0, below, 0)
-    for row in range(plan.halo):
-        a_ref[inner_row + row] = inner_ref[at, row]
-        a_ref[below - inner_row + row] = outer_ref[at, row]
+    for c, row, place, sublane in plan.edge_places(chunks)[0]:
+        if c == at:
+            count = chunk[1]
+            here = slice(sublane, sublane + count)
+            for tile in range(plan.tiles):
+                a_ref[inner_row + row, tile, :count] = inner_ref[place, tile, here]
+                a_ref[below - inner_row + row, tile, :count] = outer_ref[place, tile, here]
     a_ref[plan.halo : below] = x_ref[at]
 
     groups = range(0, plan.tiles, DEAL)
@@ -225,7 +241,7 @@
     me = lax.axis_index("lev")
     lane = lane_ids()
     for p, count in enumerate(parts):
-        diffuse(plan, p, chunks[p], *given, a_ref, b_ref)
+        diffuse(plan, p, chunks, *given, a_ref, b_ref)
         for d in range(plan.group):
             base = (me ^ d) * plan.rows_each
 
@@ -382,7 +398,7 @@
     fields = []
     for g, chunks in enumerate(steps):
         field = shape(len(chunks), plan.rows, plan.tiles, SUBS, LANES)
-        edge = shape(len(chunks), halo, plan.tiles, SUBS, LANES)
+        edge = shape(plan.edge_places(chunks)[1], plan.tiles, SUBS, LANES)
         field, inner, outer = call(
             functools.partial(arrange_kernel, plan, chunks, g == 0),
             (field, edge, edge),
@@ -400,7 +416,7 @@
         return [got[d] for d in range(group)]
 
     whole = [(0, plan.units)]
-    cut = (plan.full + 1) // 2
+    cut = 3 * plan.full // 4
     half = cut * plan.rows_each
     splits = [(0, half), (half, plan.units)]
     height = plan.rows_held + 2 * halo
@@ -453,7 +469,7 @@
 
     result = ()
     for s, tiles in enumerate((range(cut), range(cut, plan.tiles))):
-        assert len(tiles) <= cut or s == 1 and len(tiles) == cut
+        assert len(tiles) <= cut
         result = (
             pl.pallas_call(
                 functools.partial(finish_kernel, plan, *splits[s], tiles),

time: 151 us -> 158 us (1.046)
  the two profiles are of different devices: /device:TPU:17 before, /device:TPU:0 now
where the time goes in v4:
time: 158 us; the launch traced here: 155 us
  starting transfers between devices  61 us (39%)
  waiting for transfers between devices  54.1 us (34%)
  Pallas kernels  38.4 us (24%)
    ppermute x35, waiting for transfers between devices, exchange(): got[d] = lax.ppermute(blocks[d], 'lev', [(i, i ^ d) for i in range(group)])  54.1 us
    ppermute x35, starting transfers between devices, exchange(): got[d] = lax.ppermute(blocks[d], 'lev', [(i, i ^ d) for i in range(group)])  53.9 us
    pallas_call x7, Pallas kernels, call(): pl.pallas_call(kernel, out_shape=outs, in_specs=[first_spec] + [VMEM] * (...  35.4 us
    ppermute x2, starting transfers between devices, program(): inner = lax.ppermute(inner, 'tile', swap(0))  5.7 us
  transfers between devices with their start and end apart: 39, of which 11 were waited for; matrix products, arithmetic and copies ran while one was open for 0% of the time, Pallas kernels for 22%

profile of v4, /device:TPU:0, one launch (start us, length us, event | category | flops | bytes accessed | tf_op | source)
XLA Modules:
  0.0 155.2 jit_solution(4318269171909310150)
XLA Ops:
  1.5 3.0 %shard_map.56 = (f32[1,24,12,8,128]{4,3,2,1,0:T(8,128)S(1)}, f32[10,12,8,128]{3,2,1,0:T(8,128)S(1)}, f32[10,12,8,128]{3,2,1,0:T(8,128)S(1)}) custom-call(f32[8,24,1440]{2,1,0:T(8,128)S(1)} %slice.3.x_ref), custom_call_target="tpu_custom_call" | custom-call | flops 10000000 | bytes 1048576 | tf_op jit(solution)/shard_map/pallas_call | solution.py:384
  5.8 6.1 %shard_map.58 = (f32[2,24,12,8,128]{4,3,2,1,0:T(8,128)S(1)}, f32[13,12,8,128]{3,2,1,0:T(8,128)S(1)}, f32[13,12,8,128]{3,2,1,0:T(8,128)S(1)}) custom-call(f32[18,24,1440]{2,1,0:T(8,128)S(1)} %copy-done), custom_call_target="tpu_custom_call" | custom-call | flops 10000000 | bytes 1048576 | tf_op jit(solution)/shard_map/pallas_call | solution.py:384
  12.6 5.1 %collective-permute-start.9 = (f32[13,12,8,128]{3,2,1,0:T(8,128)S(1)}, f32[13,12,8,128]{3,2,1,0:T(8,128)S(1)}, u32[]{:S(2)}, u32[]{:S(2)}) collective-permute-start(f32[13,12,8,128]{3,2,1,0:T(8,128)S(1)} %get-tuple-element.67), channel_id=1, source_target_pairs={{0,1},{1,0},{2,3},{3,2},{4,5},{5,4},{6,7},{7,6},{8,9},{9,8},{10,11... | collective-permute-start | bytes 1916936 | tf_op jit(solution)/shard_map/ppermute | solution.py:408
  17.8 7.7 %shard_map.57 = (f32[272,128]{1,0:T(8,128)S(1)}, f32[272,128]{1,0:T(8,128)S(1)}, f32[272,128]{1,0:T(8,128)S(1)}, f32[272,128]{1,0:T(8,128)S(1)}, f32[272,128]{1,...) custom-call(f32[18]{0:T(128)S(1)} %copy-done.4, ...), custom_call_target="tpu_custom_call" | custom-call | flops 1000000000 | bytes 1048576 | tf_op jit(solution)/shard_map/pallas_call | solution.py:384
  25.5 2.1 %collective-permute-start.2 = (f32[272,128]{1,0:T(8,128)S(1)}, f32[272,128]{1,0:T(8,128)S(1)}, u32[]{:S(2)}, u32[]{:S(2)}) collective-permute-start(f32[272,128]{1,0:T(8,128)S(1)} %get-tuple-element.59), channel_id=1, source_target_pairs={{0,4},{4,0},{8,12},{12,8},{16,20},{20,16},{24,28},{28,24},{1,5},{5... | collective-permute-start | bytes 417800 | tf_op jit(solution)/shard_map/ppermute | solution.py:415
  29.2 2.3 %collective-permute-done.2.refs_1_ = f32[272,128]{1,0:T(8,128)S(1)} collective-permute-done((f32[272,128]{1,0:T(8,128)S(1)}, f32[272,128]{1,0:T(8,128)S(1)}, u32[]{:S(2)}, u32[]{:S(2)}) %collective-permute-start.2) | collective-permute-done | bytes 139296 | tf_op jit(solution)/shard_map/ppermute | solution.py:415
  31.5 2.8 %collective-permute-start.5 = (f32[272,128]{1,0:T(8,128)S(1)}, f32[272,128]{1,0:T(8,128)S(1)}, u32[]{:S(2)}, u32[]{:S(2)}) collective-permute-start(f32[272,128]{1,0:T(8,128)S(1)} %get-tuple-element.62), channel_id=1, source_target_pairs={{0,16},{4,20},{8,24},{12,28},{16,0},{20,4},{24,8},{28,12},{1,17},{... | collective-permute-start | bytes 417800 | tf_op jit(solution)/shard_map/ppermute | solution.py:415
  34.3 1.9 %collective-permute-start.6 = (f32[272,128]{1,0:T(8,128)S(1)}, f32[272,128]{1,0:T(8,128)S(1)}, u32[]{:S(2)}, u32[]{:S(2)}) collective-permute-start(f32[272,128]{1,0:T(8,128)S(1)} %get-tuple-element.63), channel_id=1, source_target_pairs={{0,20},{4,16},{8,28},{12,24},{16,4},{20,0},{24,12},{28,8},{1,21},{... | collective-permute-start | bytes 417800 | tf_op jit(solution)/shard_map/ppermute | solution.py:415
  36.3 3.0 %collective-permute-start.7 = (f32[272,128]{1,0:T(8,128)S(1)}, f32[272,128]{1,0:T(8,128)S(1)}, u32[]{:S(2)}, u32[]{:S(2)}) collective-permute-start(f32[272,128]{1,0:T(8,128)S(1)} %get-tuple-element.64), channel_id=1, source_target_pairs={{0,24},{4,28},{8,16},{12,20},{16,8},{20,12},{24,0},{28,4},{1,25},{... | collective-permute-start | bytes 417800 | tf_op jit(solution)/shard_map/ppermute | solution.py:415
  39.2 2.3 %collective-permute-start.8 = (f32[272,128]{1,0:T(8,128)S(1)}, f32[272,128]{1,0:T(8,128)S(1)}, u32[]{:S(2)}, u32[]{:S(2)}) collective-permute-start(f32[272,128]{1,0:T(8,128)S(1)} %get-tuple-element.65), channel_id=1, source_target_pairs={{0,28},{4,24},{8,20},{12,16},{16,12},{20,8},{24,4},{28,0},{1,29},{... | collective-permute-start | bytes 417800 | tf_op jit(solution)/shard_map/ppermute | solution.py:415
  41.5 14.9 %shard_map.59 = (f32[240,128]{1,0:T(8,128)S(1)}, f32[240,128]{1,0:T(8,128)S(1)}, f32[240,128]{1,0:T(8,128)S(1)}, f32[240,128]{1,0:T(8,128)S(1)}, f32[240,128]{1,...) custom-call(f32[18]{0:T(128)S(1)} %copy-done.4, ...), custom_call_target="tpu_custom_call" | custom-call | flops 1000000000 | bytes 1048576 | tf_op jit(solution)/shard_map/pallas_call | solution.py:384
  56.7 1.8 %collective-permute-start.11 = (f32[104,128]{1,0:T(8,128)S(1)}, f32[104,128]{1,0:T(8,128)S(1)}, u32[]{:S(2)}, u32[]{:S(2)}) collective-permute-start(f32[104,128]{1,0:T(8,128)S(1)} %get-tuple-element.70), channel_id=1, source_target_pairs={{0,4},{4,0},{8,12},{12,8},{16,20},{20,16},{24,28},{28,24},{1,5},{5... | collective-permute-start | bytes 159752 | tf_op jit(solution)/shard_map/ppermute | solution.py:415
  58.5 2.0 %collective-permute-start.12 = (f32[104,128]{1,0:T(8,128)S(1)}, f32[104,128]{1,0:T(8,128)S(1)}, u32[]{:S(2)}, u32[]{:S(2)}) collective-permute-start(f32[104,128]{1,0:T(8,128)S(1)} %get-tuple-element.71), channel_id=1, source_target_pairs={{0,8},{4,12},{8,0},{12,4},{16,24},{20,28},{24,16},{28,20},{1,9},{5... | collective-permute-start | bytes 159752 | tf_op jit(solution)/shard_map/ppermute | solution.py:415
  60.5 2.7 %collective-permute-done.11.refs_9_ = f32[104,128]{1,0:T(8,128)S(1)} collective-permute-done((f32[104,128]{1,0:T(8,128)S(1)}, f32[104,128]{1,0:T(8,128)S(1)}, u32[]{:S(2)}, u32[]{:S(2)}) %collective-permute-start.11) | collective-permute-done | bytes 53280 | tf_op jit(solution)/shard_map/ppermute | solution.py:415
  64.3 1.9 %collective-permute-start.29 = (f32[240,128]{1,0:T(8,128)S(1)}, f32[240,128]{1,0:T(8,128)S(1)}, u32[]{:S(2)}, u32[]{:S(2)}) collective-permute-start(f32[240,128]{1,0:T(8,128)S(1)} %get-tuple-element.90), channel_id=1, source_target_pairs={{0,20},{4,16},{8,28},{12,24},{16,4},{20,0},{24,12},{28,8},{1,21},{... | collective-permute-start | bytes 368648 | tf_op jit(solution)/shard_map/ppermute | solution.py:415
  67.9 3.0 %collective-permute-start.31 = (f32[240,128]{1,0:T(8,128)S(1)}, f32[240,128]{1,0:T(8,128)S(1)}, u32[]{:S(2)}, u32[]{:S(2)}) collective-permute-start(f32[240,128]{1,0:T(8,128)S(1)} %get-tuple-element.92), channel_id=1, source_target_pairs={{0,28},{4,24},{8,20},{12,16},{16,12},{20,8},{24,4},{28,0},{1,29},{... | collective-permute-start | bytes 368648 | tf_op jit(solution)/shard_map/ppermute | solution.py:415
  71.7 8.3 %collective-permute-done.28.refs_12_ = f32[240,128]{1,0:T(8,128)S(1)} collective-permute-done((f32[240,128]{1,0:T(8,128)S(1)}, f32[240,128]{1,0:T(8,128)S(1)}, u32[]{:S(2)}, u32[]{:S(2)}) %collective-permute-start.28) | collective-permute-done | bytes 122912 | tf_op jit(solution)/shard_map/ppermute | solution.py:415
  80.0 4.9 %collective-permute-done.29.refs_13_ = f32[240,128]{1,0:T(8,128)S(1)} collective-permute-done((f32[240,128]{1,0:T(8,128)S(1)}, f32[240,128]{1,0:T(8,128)S(1)}, u32[]{:S(2)}, u32[]{:S(2)}) %collective-permute-start.29) | collective-permute-done | bytes 122912 | tf_op jit(solution)/shard_map/ppermute | solution.py:415
  85.2 2.5 %collective-permute-start.17 = (f32[104,128]{1,0:T(8,128)S(1)}, f32[104,128]{1,0:T(8,128)S(1)}, u32[]{:S(2)}, u32[]{:S(2)}) collective-permute-start(f32[104,128]{1,0:T(8,128)S(1)} %get-tuple-element.76), channel_id=1, source_target_pairs={{0,28},{4,24},{8,20},{12,16},{16,12},{20,8},{24,4},{28,0},{1,29},{... | collective-permute-start | bytes 159752 | tf_op jit(solution)/shard_map/ppermute | solution.py:415
  87.7 2.0 %shard_map.61 = (f32[432,128]{1,0:T(8,128)S(1)}, f32[432,128]{1,0:T(8,128)S(1)}, f32[432,128]{1,0:T(8,128)S(1)}, f32[432,128]{1,0:T(8,128)S(1)}, f32[432,128]{1,...) custom-call(bf16[192,144]{1,0:T(8,128)(2,1)S(1)} %get-tuple-element.53.high_ref, ...), custom_call_target="tpu_custom_call" | custom-call | flops 1000000000 | bytes 1048576 | tf_op jit(solution)/shard_map/pallas_call | solution.py:384
  89.7 2.6 %collective-permute-start.32 = (f32[432,128]{1,0:T(8,128)S(1)}, f32[432,128]{1,0:T(8,128)S(1)}, u32[]{:S(2)}, u32[]{:S(2)}) collective-permute-start(f32[432,128]{1,0:T(8,128)S(1)} %get-tuple-element.94), channel_id=1, source_target_pairs={{0,4},{4,0},{8,12},{12,8},{16,20},{20,16},{24,28},{28,24},{1,5},{5... | collective-permute-start | bytes 663560 | tf_op jit(solution)/shard_map/ppermute | solution.py:415
  92.9 3.6 %collective-permute-start.33 = (f32[432,128]{1,0:T(8,128)S(1)}, f32[432,128]{1,0:T(8,128)S(1)}, u32[]{:S(2)}, u32[]{:S(2)}) collective-permute-start(f32[432,128]{1,0:T(8,128)S(1)} %get-tuple-element.95), channel_id=1, source_target_pairs={{0,8},{4,12},{8,0},{12,4},{16,24},{20,28},{24,16},{28,20},{1,9},{5... | collective-permute-start | bytes 663560 | tf_op jit(solution)/shard_map/ppermute | solution.py:415
  98.3 1.7 %collective-permute-start.19 = (f32[184,128]{1,0:T(8,128)S(1)}, f32[184,128]{1,0:T(8,128)S(1)}, u32[]{:S(2)}, u32[]{:S(2)}) collective-permute-start(f32[184,128]{1,0:T(8,128)S(1)} %get-tuple-element.79), channel_id=1, source_target_pairs={{0,8},{4,12},{8,0},{12,4},{16,24},{20,28},{24,16},{28,20},{1,9},{5... | collective-permute-start | bytes 282632 | tf_op jit(solution)/shard_map/ppermute | solution.py:415
  102.5 3.7 %collective-permute-start.35 = (f32[432,128]{1,0:T(8,128)S(1)}, f32[432,128]{1,0:T(8,128)S(1)}, u32[]{:S(2)}, u32[]{:S(2)}) collective-permute-start(f32[432,128]{1,0:T(8,128)S(1)} %get-tuple-element.97), channel_id=1, source_target_pairs={{0,16},{4,20},{8,24},{12,28},{16,0},{20,4},{24,8},{28,12},{1,17},{... | collective-permute-start | bytes 663560 | tf_op jit(solution)/shard_map/ppermute | solution.py:415
  107.6 2.5 %collective-permute-start.36 = (f32[432,128]{1,0:T(8,128)S(1)}, f32[432,128]{1,0:T(8,128)S(1)}, u32[]{:S(2)}, u32[]{:S(2)}) collective-permute-start(f32[432,128]{1,0:T(8,128)S(1)} %get-tuple-element.98), channel_id=1, source_target_pairs={{0,20},{4,16},{8,28},{12,24},{16,4},{20,0},{24,12},{28,8},{1,21},{... | collective-permute-start | bytes 663560 | tf_op jit(solution)/shard_map/ppermute | solution.py:415
  110.1 1.9 %collective-permute-start.37 = (f32[432,128]{1,0:T(8,128)S(1)}, f32[432,128]{1,0:T(8,128)S(1)}, u32[]{:S(2)}, u32[]{:S(2)}) collective-permute-start(f32[432,128]{1,0:T(8,128)S(1)} %get-tuple-element.99), channel_id=1, source_target_pairs={{0,24},{4,28},{8,16},{12,20},{16,8},{20,12},{24,0},{28,4},{1,25},{... | collective-permute-start | bytes 663560 | tf_op jit(solution)/shard_map/ppermute | solution.py:415
  112.0 2.7 %collective-permute-start.38 = (f32[432,128]{1,0:T(8,128)S(1)}, f32[432,128]{1,0:T(8,128)S(1)}, u32[]{:S(2)}, u32[]{:S(2)}) collective-permute-start(f32[432,128]{1,0:T(8,128)S(1)} %get-tuple-element.100), channel_id=1, source_target_pairs={{0,28},{4,24},{8,20},{12,16},{16,12},{20,8},{24,4},{28,0},{1,29},{... | collective-permute-start | bytes 663560 | tf_op jit(solution)/shard_map/ppermute | solution.py:415
  115.6 17.8 %collective-permute-done.35.refs_4_ = f32[432,128]{1,0:T(8,128)S(1)} collective-permute-done((f32[432,128]{1,0:T(8,128)S(1)}, f32[432,128]{1,0:T(8,128)S(1)}, u32[]{:S(2)}, u32[]{:S(2)}) %collective-permute-start.35) | collective-permute-done | bytes 221216 | tf_op jit(solution)/shard_map/ppermute | solution.py:415
  133.4 6.3 %collective-permute-done.36.refs_5_ = f32[432,128]{1,0:T(8,128)S(1)} collective-permute-done((f32[432,128]{1,0:T(8,128)S(1)}, f32[432,128]{1,0:T(8,128)S(1)}, u32[]{:S(2)}, u32[]{:S(2)}) %collective-permute-start.36) | collective-permute-done | bytes 221216 | tf_op jit(solution)/shard_map/ppermute | solution.py:415
  139.7 2.8 %collective-permute-start.23 = (f32[184,128]{1,0:T(8,128)S(1)}, f32[184,128]{1,0:T(8,128)S(1)}, u32[]{:S(2)}, u32[]{:S(2)}) collective-permute-start(f32[184,128]{1,0:T(8,128)S(1)} %get-tuple-element.83), channel_id=1, source_target_pairs={{0,24},{4,28},{8,16},{12,20},{16,8},{20,12},{24,0},{28,4},{1,25},{... | collective-permute-start | bytes 282632 | tf_op jit(solution)/shard_map/ppermute | solution.py:415
  143.9 1.8 %shard_map.62.refs_8_ = f32[18,24,1440]{2,1,0:T(8,128)} custom-call(s32[24,1440]{1,0:T(8,128)S(1)} %copy-done.1, f32[432,128]{1,0:T(8,128)S(1)} %get-tuple-element.93.refs_0_, f32[432,128]{1,0:T(8,128)S(1)} %collective-permute-done.32.refs_1_, f32[432,128]{1,0:T(8,128)S(1)} %collective-permute-done.33.refs_2_, ...), custom_call_target="tpu_custom_call" | custom-call | flops 10000000 | bytes 1048576 | tf_op jit(solution)/shard_map/pallas_call | solution.py:474
  145.7 6.7 %collective-permute-done.21.refs_4_ = f32[184,128]{1,0:T(8,128)S(1)} collective-permute-done((f32[184,128]{1,0:T(8,128)S(1)}, f32[184,128]{1,0:T(8,128)S(1)}, u32[]{:S(2)}, u32[]{:S(2)}) %collective-permute-start.21) | collective-permute-done | bytes 94240 | tf_op jit(solution)/shard_map/ppermute | solution.py:415
  (66 shorter events, 20.6 us)
Async XLA Ops:
  4.6 13.2 %collective-permute-start = (f32[10,12,8,128]{3,2,1,0:T(8,128)S(1)}, f32[10,12,8,128]{3,2,1,0:T(8,128)S(1)}, u32[]{:S(2)}, u32[]{:S(2)}) collective-permute-start(f32[10,12,8,128]{3,2,1,0:T(8,128)S(1)} %get-tuple-element.56), channel_id=1, source_target_pairs={{0,1},{1,0},{2,3},{3,2},{4,5},{5,4},{6,7},{7,6},{8,9},{9,8},{10,11... | collective-permute-start | bytes 1474568 | tf_op jit(solution)/shard_map/ppermute | solution.py:408
  5.1 12.6 %collective-permute-start.1 = (f32[10,12,8,128]{3,2,1,0:T(8,128)S(1)}, f32[10,12,8,128]{3,2,1,0:T(8,128)S(1)}, u32[]{:S(2)}, u32[]{:S(2)}) collective-permute-start(f32[10,12,8,128]{3,2,1,0:T(8,128)S(1)} %get-tuple-element.57), channel_id=1, source_target_pairs={{1,2},{2,1},{5,6},{6,5},{9,10},{10,9},{13,14},{14,13},{17,18},{18,... | collective-permute-start | bytes 1474568 | tf_op jit(solution)/shard_map/ppermute | solution.py:409
  11.9 24.4 %collective-permute-start.10 = (f32[13,12,8,128]{3,2,1,0:T(8,128)S(1)}, f32[13,12,8,128]{3,2,1,0:T(8,128)S(1)}, u32[]{:S(2)}, u32[]{:S(2)}) collective-permute-start(f32[13,12,8,128]{3,2,1,0:T(8,128)S(1)} %get-tuple-element.68), channel_id=1, source_target_pairs={{1,2},{2,1},{5,6},{6,5},{9,10},{10,9},{13,14},{14,13},{17,18},{18,... | collective-permute-start | bytes 1916936 | tf_op jit(solution)/shard_map/ppermute | solution.py:409
  12.6 26.6 %collective-permute-start.9 = (f32[13,12,8,128]{3,2,1,0:T(8,128)S(1)}, f32[13,12,8,128]{3,2,1,0:T(8,128)S(1)}, u32[]{:S(2)}, u32[]{:S(2)}) collective-permute-start(f32[13,12,8,128]{3,2,1,0:T(8,128)S(1)} %get-tuple-element.67), channel_id=1, source_target_pairs={{0,1},{1,0},{2,3},{3,2},{4,5},{5,4},{6,7},{7,6},{8,9},{9,8},{10,11... | collective-permute-start | bytes 1916936 | tf_op jit(solution)/shard_map/ppermute | solution.py:408
  29.2 27.1 %collective-permute-start.4 = (f32[272,128]{1,0:T(8,128)S(1)}, f32[272,128]{1,0:T(8,128)S(1)}, u32[]{:S(2)}, u32[]{:S(2)}) collective-permute-start(f32[272,128]{1,0:T(8,128)S(1)} %get-tuple-element.61), channel_id=1, source_target_pairs={{0,12},{4,8},{8,4},{12,0},{16,28},{20,24},{24,20},{28,16},{1,13},{... | collective-permute-start | bytes 417800 | tf_op jit(solution)/shard_map/ppermute | solution.py:415
  31.5 25.0 %collective-permute-start.5 = (f32[272,128]{1,0:T(8,128)S(1)}, f32[272,128]{1,0:T(8,128)S(1)}, u32[]{:S(2)}, u32[]{:S(2)}) collective-permute-start(f32[272,128]{1,0:T(8,128)S(1)} %get-tuple-element.62), channel_id=1, source_target_pairs={{0,16},{4,20},{8,24},{12,28},{16,0},{20,4},{24,8},{28,12},{1,17},{... | collective-permute-start | bytes 417800 | tf_op jit(solution)/shard_map/ppermute | solution.py:415
  34.3 22.4 %collective-permute-start.6 = (f32[272,128]{1,0:T(8,128)S(1)}, f32[272,128]{1,0:T(8,128)S(1)}, u32[]{:S(2)}, u32[]{:S(2)}) collective-permute-start(f32[272,128]{1,0:T(8,128)S(1)} %get-tuple-element.63), channel_id=1, source_target_pairs={{0,20},{4,16},{8,28},{12,24},{16,4},{20,0},{24,12},{28,8},{1,21},{... | collective-permute-start | bytes 417800 | tf_op jit(solution)/shard_map/ppermute | solution.py:415
  36.3 22.3 %collective-permute-start.7 = (f32[272,128]{1,0:T(8,128)S(1)}, f32[272,128]{1,0:T(8,128)S(1)}, u32[]{:S(2)}, u32[]{:S(2)}) collective-permute-start(f32[272,128]{1,0:T(8,128)S(1)} %get-tuple-element.64), channel_id=1, source_target_pairs={{0,24},{4,28},{8,16},{12,20},{16,8},{20,12},{24,0},{28,4},{1,25},{... | collective-permute-start | bytes 417800 | tf_op jit(solution)/shard_map/ppermute | solution.py:415
  39.2 21.3 %collective-permute-start.8 = (f32[272,128]{1,0:T(8,128)S(1)}, f32[272,128]{1,0:T(8,128)S(1)}, u32[]{:S(2)}, u32[]{:S(2)}) collective-permute-start(f32[272,128]{1,0:T(8,128)S(1)} %get-tuple-element.65), channel_id=1, source_target_pairs={{0,28},{4,24},{8,20},{12,16},{16,12},{20,8},{24,4},{28,0},{1,29},{... | collective-permute-start | bytes 417800 | tf_op jit(solution)/shard_map/ppermute | solution.py:415
  56.5 11.4 %collective-permute-start.26 = (f32[240,128]{1,0:T(8,128)S(1)}, f32[240,128]{1,0:T(8,128)S(1)}, u32[]{:S(2)}, u32[]{:S(2)}) collective-permute-start(f32[240,128]{1,0:T(8,128)S(1)} %get-tuple-element.87), channel_id=1, source_target_pairs={{0,8},{4,12},{8,0},{12,4},{16,24},{20,28},{24,16},{28,20},{1,9},{5... | collective-permute-start | bytes 368648 | tf_op jit(solution)/shard_map/ppermute | solution.py:415
  60.5 11.2 %collective-permute-start.27 = (f32[240,128]{1,0:T(8,128)S(1)}, f32[240,128]{1,0:T(8,128)S(1)}, u32[]{:S(2)}, u32[]{:S(2)}) collective-permute-start(f32[240,128]{1,0:T(8,128)S(1)} %get-tuple-element.88), channel_id=1, source_target_pairs={{0,12},{4,8},{8,4},{12,0},{16,28},{20,24},{24,20},{28,16},{1,13},{... | collective-permute-start | bytes 368648 | tf_op jit(solution)/shard_map/ppermute | solution.py:415
  63.2 16.9 %collective-permute-start.28 = (f32[240,128]{1,0:T(8,128)S(1)}, f32[240,128]{1,0:T(8,128)S(1)}, u32[]{:S(2)}, u32[]{:S(2)}) collective-permute-start(f32[240,128]{1,0:T(8,128)S(1)} %get-tuple-element.89), channel_id=1, source_target_pairs={{0,16},{4,20},{8,24},{12,28},{16,0},{20,4},{24,8},{28,12},{1,17},{... | collective-permute-start | bytes 368648 | tf_op jit(solution)/shard_map/ppermute | solution.py:415
  64.3 20.7 %collective-permute-start.29 = (f32[240,128]{1,0:T(8,128)S(1)}, f32[240,128]{1,0:T(8,128)S(1)}, u32[]{:S(2)}, u32[]{:S(2)}) collective-permute-start(f32[240,128]{1,0:T(8,128)S(1)} %get-tuple-element.90), channel_id=1, source_target_pairs={{0,20},{4,16},{8,28},{12,24},{16,4},{20,0},{24,12},{28,8},{1,21},{... | collective-permute-start | bytes 368648 | tf_op jit(solution)/shard_map/ppermute | solution.py:415
  66.2 18.8 %collective-permute-start.30 = (f32[240,128]{1,0:T(8,128)S(1)}, f32[240,128]{1,0:T(8,128)S(1)}, u32[]{:S(2)}, u32[]{:S(2)}) collective-permute-start(f32[240,128]{1,0:T(8,128)S(1)} %get-tuple-element.91), channel_id=1, source_target_pairs={{0,24},{4,28},{8,16},{12,20},{16,8},{20,12},{24,0},{28,4},{1,25},{... | collective-permute-start | bytes 368648 | tf_op jit(solution)/shard_map/ppermute | solution.py:415
  67.9 17.3 %collective-permute-start.31 = (f32[240,128]{1,0:T(8,128)S(1)}, f32[240,128]{1,0:T(8,128)S(1)}, u32[]{:S(2)}, u32[]{:S(2)}) collective-permute-start(f32[240,128]{1,0:T(8,128)S(1)} %get-tuple-element.92), channel_id=1, source_target_pairs={{0,28},{4,24},{8,20},{12,16},{16,12},{20,8},{24,4},{28,0},{1,29},{... | collective-permute-start | bytes 368648 | tf_op jit(solution)/shard_map/ppermute | solution.py:415
  71.7 18.1 %collective-permute-start.13 = (f32[104,128]{1,0:T(8,128)S(1)}, f32[104,128]{1,0:T(8,128)S(1)}, u32[]{:S(2)}, u32[]{:S(2)}) collective-permute-start(f32[104,128]{1,0:T(8,128)S(1)} %get-tuple-element.72), channel_id=1, source_target_pairs={{0,12},{4,8},{8,4},{12,0},{16,28},{20,24},{24,20},{28,16},{1,13},{... | collective-permute-start | bytes 159752 | tf_op jit(solution)/shard_map/ppermute | solution.py:415
  80.0 12.9 %collective-permute-start.14 = (f32[104,128]{1,0:T(8,128)S(1)}, f32[104,128]{1,0:T(8,128)S(1)}, u32[]{:S(2)}, u32[]{:S(2)}) collective-permute-start(f32[104,128]{1,0:T(8,128)S(1)} %get-tuple-element.73), channel_id=1, source_target_pairs={{0,16},{4,20},{8,24},{12,28},{16,0},{20,4},{24,8},{28,12},{1,17},{... | collective-permute-start | bytes 159752 | tf_op jit(solution)/shard_map/ppermute | solution.py:415
  85.0 11.5 %collective-permute-start.15 = (f32[104,128]{1,0:T(8,128)S(1)}, f32[104,128]{1,0:T(8,128)S(1)}, u32[]{:S(2)}, u32[]{:S(2)}) collective-permute-start(f32[104,128]{1,0:T(8,128)S(1)} %get-tuple-element.74), channel_id=1, source_target_pairs={{0,20},{4,16},{8,28},{12,24},{16,4},{20,0},{24,12},{28,8},{1,21},{... | collective-permute-start | bytes 159752 | tf_op jit(solution)/shard_map/ppermute | solution.py:415
  85.0 11.5 %collective-permute-start.16 = (f32[104,128]{1,0:T(8,128)S(1)}, f32[104,128]{1,0:T(8,128)S(1)}, u32[]{:S(2)}, u32[]{:S(2)}) collective-permute-start(f32[104,128]{1,0:T(8,128)S(1)} %get-tuple-element.75), channel_id=1, source_target_pairs={{0,24},{4,28},{8,16},{12,20},{16,8},{20,12},{24,0},{28,4},{1,25},{... | collective-permute-start | bytes 159752 | tf_op jit(solution)/shard_map/ppermute | solution.py:415
  85.2 11.3 %collective-permute-start.17 = (f32[104,128]{1,0:T(8,128)S(1)}, f32[104,128]{1,0:T(8,128)S(1)}, u32[]{:S(2)}, u32[]{:S(2)}) collective-permute-start(f32[104,128]{1,0:T(8,128)S(1)} %get-tuple-element.76), channel_id=1, source_target_pairs={{0,28},{4,24},{8,20},{12,16},{16,12},{20,8},{24,4},{28,0},{1,29},{... | collective-permute-start | bytes 159752 | tf_op jit(solution)/shard_map/ppermute | solution.py:415
  89.7 20.4 %collective-permute-start.32 = (f32[432,128]{1,0:T(8,128)S(1)}, f32[432,128]{1,0:T(8,128)S(1)}, u32[]{:S(2)}, u32[]{:S(2)}) collective-permute-start(f32[432,128]{1,0:T(8,128)S(1)} %get-tuple-element.94), channel_id=1, source_target_pairs={{0,4},{4,0},{8,12},{12,8},{16,20},{20,16},{24,28},{28,24},{1,5},{5... | collective-permute-start | bytes 663560 | tf_op jit(solution)/shard_map/ppermute | solution.py:415
  92.9 19.1 %collective-permute-start.33 = (f32[432,128]{1,0:T(8,128)S(1)}, f32[432,128]{1,0:T(8,128)S(1)}, u32[]{:S(2)}, u32[]{:S(2)}) collective-permute-start(f32[432,128]{1,0:T(8,128)S(1)} %get-tuple-element.95), channel_id=1, source_target_pairs={{0,8},{4,12},{8,0},{12,4},{16,24},{20,28},{24,16},{28,20},{1,9},{5... | collective-permute-start | bytes 663560 | tf_op jit(solution)/shard_map/ppermute | solution.py:415
  100.0 14.7 %collective-permute-start.34 = (f32[432,128]{1,0:T(8,128)S(1)}, f32[432,128]{1,0:T(8,128)S(1)}, u32[]{:S(2)}, u32[]{:S(2)}) collective-permute-start(f32[432,128]{1,0:T(8,128)S(1)} %get-tuple-element.96), channel_id=1, source_target_pairs={{0,12},{4,8},{8,4},{12,0},{16,28},{20,24},{24,20},{28,16},{1,13},{... | collective-permute-start | bytes 663560 | tf_op jit(solution)/shard_map/ppermute | solution.py:415
  102.5 30.9 %collective-permute-start.35 = (f32[432,128]{1,0:T(8,128)S(1)}, f32[432,128]{1,0:T(8,128)S(1)}, u32[]{:S(2)}, u32[]{:S(2)}) collective-permute-start(f32[432,128]{1,0:T(8,128)S(1)} %get-tuple-element.97), channel_id=1, source_target_pairs={{0,16},{4,20},{8,24},{12,28},{16,0},{20,4},{24,8},{28,12},{1,17},{... | collective-permute-start | bytes 663560 | tf_op jit(solution)/shard_map/ppermute | solution.py:415
  107.6 32.0 %collective-permute-start.36 = (f32[432,128]{1,0:T(8,128)S(1)}, f32[432,128]{1,0:T(8,128)S(1)}, u32[]{:S(2)}, u32[]{:S(2)}) collective-permute-start(f32[432,128]{1,0:T(8,128)S(1)} %get-tuple-element.98), channel_id=1, source_target_pairs={{0,20},{4,16},{8,28},{12,24},{16,4},{20,0},{24,12},{28,8},{1,21},{... | collective-permute-start | bytes 663560 | tf_op jit(solution)/shard_map/ppermute | solution.py:415
  110.1 29.6 %collective-permute-start.37 = (f32[432,128]{1,0:T(8,128)S(1)}, f32[432,128]{1,0:T(8,128)S(1)}, u32[]{:S(2)}, u32[]{:S(2)}) collective-permute-start(f32[432,128]{1,0:T(8,128)S(1)} %get-tuple-element.99), channel_id=1, source_target_pairs={{0,24},{4,28},{8,16},{12,20},{16,8},{20,12},{24,0},{28,4},{1,25},{... | collective-permute-start | bytes 663560 | tf_op jit(solution)/shard_map/ppermute | solution.py:415
  112.0 30.5 %collective-permute-start.38 = (f32[432,128]{1,0:T(8,128)S(1)}, f32[432,128]{1,0:T(8,128)S(1)}, u32[]{:S(2)}, u32[]{:S(2)}) collective-permute-start(f32[432,128]{1,0:T(8,128)S(1)} %get-tuple-element.100), channel_id=1, source_target_pairs={{0,28},{4,24},{8,20},{12,16},{16,12},{20,8},{24,4},{28,0},{1,29},{... | collective-permute-start | bytes 663560 | tf_op jit(solution)/shard_map/ppermute | solution.py:415
  114.7 31.0 %collective-permute-start.20 = (f32[184,128]{1,0:T(8,128)S(1)}, f32[184,128]{1,0:T(8,128)S(1)}, u32[]{:S(2)}, u32[]{:S(2)}) collective-permute-start(f32[184,128]{1,0:T(8,128)S(1)} %get-tuple-element.80), channel_id=1, source_target_pairs={{0,12},{4,8},{8,4},{12,0},{16,28},{20,24},{24,20},{28,16},{1,13},{... | collective-permute-start | bytes 282632 | tf_op jit(solution)/shard_map/ppermute | solution.py:415
  133.4 19.0 %collective-permute-start.21 = (f32[184,128]{1,0:T(8,128)S(1)}, f32[184,128]{1,0:T(8,128)S(1)}, u32[]{:S(2)}, u32[]{:S(2)}) collective-permute-start(f32[184,128]{1,0:T(8,128)S(1)} %get-tuple-element.81), channel_id=1, source_target_pairs={{0,16},{4,20},{8,24},{12,28},{16,0},{20,4},{24,8},{28,12},{1,17},{... | collective-permute-start | bytes 282632 | tf_op jit(solution)/shard_map/ppermute | solution.py:415
  139.7 14.3 %collective-permute-start.22 = (f32[184,128]{1,0:T(8,128)S(1)}, f32[184,128]{1,0:T(8,128)S(1)}, u32[]{:S(2)}, u32[]{:S(2)}) collective-permute-start(f32[184,128]{1,0:T(8,128)S(1)} %get-tuple-element.82), channel_id=1, source_target_pairs={{0,20},{4,16},{8,28},{12,24},{16,4},{20,0},{24,12},{28,8},{1,21},{... | collective-permute-start | bytes 282632 | tf_op jit(solution)/shard_map/ppermute | solution.py:415
  139.7 14.3 %collective-permute-start.23 = (f32[184,128]{1,0:T(8,128)S(1)}, f32[184,128]{1,0:T(8,128)S(1)}, u32[]{:S(2)}, u32[]{:S(2)}) collective-permute-start(f32[184,128]{1,0:T(8,128)S(1)} %get-tuple-element.83), channel_id=1, source_target_pairs={{0,24},{4,28},{8,16},{12,20},{16,8},{20,12},{24,0},{28,4},{1,25},{... | collective-permute-start | bytes 282632 | tf_op jit(solution)/shard_map/ppermute | solution.py:415
  142.5 11.5 %collective-permute-start.24 = (f32[184,128]{1,0:T(8,128)S(1)}, f32[184,128]{1,0:T(8,128)S(1)}, u32[]{:S(2)}, u32[]{:S(2)}) collective-permute-start(f32[184,128]{1,0:T(8,128)S(1)} %get-tuple-element.84), channel_id=1, source_target_pairs={{0,28},{4,24},{8,20},{12,16},{16,12},{20,8},{24,4},{28,0},{1,29},{... | collective-permute-start | bytes 282632 | tf_op jit(solution)/shard_map/ppermute | solution.py:415
  (12 other events, 217.6 us)
